TPU v7x, 512 devices: a whole 4x8x8 slice. The times are simulated.
512 devices in a mesh: section: 8 (over y_lo, core), dp: 64 (over z, x, y_hi).
Axes of the slice: x: 4, y: 8 (y_hi: 2, y_lo: 4; y = y_hi * 4 + y_lo), z: 8, core: 2. Of those that a mesh axis runs over, the one named last changes fastest.
Arguments:
- acts: float32 [8, 8192, 1024], P('section', 'dp'), may hold values from -6 to 6
- grads: float32 [8, 8192, 1024], P('section', 'dp'), may hold values from -0.6 to 0.6
- in_proj: bfloat16 [8, 2048, 512], P('section', 'dp'), may hold values from -0.25 to 0.25
- out_proj: bfloat16 [8, 2048, 512], P('section', 'dp'), may hold values from -0.125 to 0.125
- gain: float32 [8, 512], P('section'), may hold values from 0.1 to 1.9
Outputs:
- acts_out: float32 [8, 8192, 1024], P('section', 'dp')
- grads_out: float32 [8, 8192, 1024], P('section', 'dp')
- out_proj_grad: float32 [8, 2048, 512], P('section', 'dp')
All inputs are finite; a program needn't handle non-finite values.
Results may differ from a plain program's by a relative error of at most 0.012.
Values may be sent and summed in bfloat16 or wider, within the bound.
No kernel may reach another device: no remote copies, remote signals or barrier semaphores. Data moves between devices by JAX's collectives and lax.ppermute only.
A program may use at most 64 MiB of HBM per device.

v0:
```python
import jax
import jax.numpy as jnp
from jax import lax
from jax.sharding import PartitionSpec as P

coupling_scale = 32.0**0.25
rms_epsilon = 1e-06
root_half = 0.7071067811865476
inv_root_two_pi = 0.3989422804014327


def passed_along(block, axis, distance):
    devices = range(lax.axis_size(axis))
    route = [(i - distance, i) for i in devices if i - distance in devices]
    return lax.ppermute(block, axis, route)


def normalize(first_half, gain_row):
    inv_rms = lax.rsqrt(jnp.mean(first_half * first_half, axis=-1, keepdims=True) + rms_epsilon)
    normed = (first_half * inv_rms * gain_row).astype(jnp.bfloat16)
    return (inv_rms, normed)


def gelu_slope(preact):
    normal_cdf = 0.5 * (1.0 + lax.erf(preact * root_half))
    density = jnp.exp(-0.5 * preact * preact) * inv_root_two_pi
    return (preact * normal_cdf, normal_cdf + preact * density)


def forward_half(normed, weight_in):
    preact = lax.dot_general(
        normed, weight_in, (((1,), (1,)), ((), ())), preferred_element_type=jnp.float32
    )
    hidden, slopes = gelu_slope(preact)
    return (hidden.astype(jnp.bfloat16), slopes)


def backward_half(hidden_b, slopes, cotangent, weight_in, weight_out):
    branch = jnp.dot(hidden_b, weight_out, preferred_element_type=jnp.float32)
    hidden_grad = lax.dot_general(
        cotangent, weight_out, (((1,), (1,)), ((), ())), preferred_element_type=jnp.float32
    )
    pre_grad = (hidden_grad * slopes).astype(jnp.bfloat16)
    norm_grad = jnp.dot(pre_grad, weight_in, preferred_element_type=jnp.float32)
    return (branch, norm_grad)


def invert_step(
    first_half, second_half, first_grad, second_grad, inv_rms, gain_row, branch, norm_grad
):
    scaled = norm_grad * gain_row
    inner = jnp.mean(first_half * scaled, axis=-1, keepdims=True)
    input_grad = inv_rms * scaled - first_half * (inv_rms * inv_rms * inv_rms) * inner
    new_acts = jnp.concatenate([(second_half - branch) / coupling_scale, first_half], axis=-1)
    new_grads = jnp.concatenate([coupling_scale * second_grad, first_grad + input_grad], axis=-1)
    return (new_acts, new_grads)


def outer_rows(hidden_b, cotangent):
    return lax.dot_general(
        hidden_b, cotangent, (((0,), (0,)), ((), ())), preferred_element_type=jnp.float32
    )


def reduce_rows(grad_total):
    return lax.psum_scatter(grad_total, "dp", scatter_dimension=0, tiled=True)


def local(acts, grads, in_proj, out_proj, gain):
    section_count = lax.axis_size("section")
    tick_count = min(4, section_count // 2)
    feature_half = acts.shape[2] // 2
    hidden_units = in_proj.shape[1] * lax.axis_size("dp")
    gain_row = gain[0]
    held_pair = jnp.stack([acts[0], grads[0]])
    full_in, full_out = (
        lax.all_gather(in_proj, "dp", axis=1, tiled=True),
        lax.all_gather(out_proj, "dp", axis=1, tiled=True),
    )
    weight_in = full_in[0]
    weight_out = full_out[0]
    grad_total = jnp.zeros((hidden_units, feature_half), jnp.float32)
    grad_share = None
    for tick_index in range(tick_count):
        first_half = held_pair[0, :, :feature_half]
        second_half = held_pair[0, :, feature_half:]
        first_grad = held_pair[1, :, :feature_half]
        second_grad = held_pair[1, :, feature_half:]
        inv_rms, normed = normalize(first_half, gain_row)
        cotangent = second_grad.astype(jnp.bfloat16)
        hidden_b, slopes = forward_half(normed, weight_in)
        grad_total = grad_total + outer_rows(hidden_b, cotangent)
        branch, norm_grad = backward_half(hidden_b, slopes, cotangent, weight_in, weight_out)
        new_acts, new_grads = invert_step(
            first_half, second_half, first_grad, second_grad, inv_rms, gain_row, branch, norm_grad
        )
        held_pair = passed_along(jnp.stack([new_acts, new_grads]), "section", -1)
    grad_share = reduce_rows(grad_total)
    return (held_pair[0][None], held_pair[1][None], grad_share[None])


def solution(mesh):
    placed = (
        P("section", "dp", None),
        P("section", "dp", None),
        P("section", "dp", None),
        P("section", "dp", None),
        P("section", None),
    )
    return jax.shard_map(
        local,
        mesh=mesh,
        in_specs=placed,
        out_specs=(P("section", "dp", None), P("section", "dp", None), P("section", "dp", None)),
        check_vma=False,
    )
```

profile of v0, /device:TPU:16, one launch (start us, length us, event | category | flops | bytes accessed | tf_op | source)
XLA Modules:
  0.0 827.4 jit_solution(17977913412300295236)
XLA Ops:
  10.8 1.7 multiply_bitcast_fusion.3
  12.4 139.1 %all-gather.3.cloned.1.call-done = bf16[1,2048,512]{2,1,0:T(8,128)(2,1)} async-done(((bf16[1,32,512]{2,1,0:T(8,128)(2,1)}), bf16[1,2048,512]{2,1,0:T(8,128)(2,1)}) %all-gather.3.cloned.1.call-update) | async-done | bytes 2097168 | tf_op jit(solution)/shard_map/all_gather | solution.py:77
  151.5 2.5 fusion.30
  154.0 131.6 %all-gather.5.cloned.1.call-done = bf16[1,2048,512]{2,1,0:T(8,128)(2,1)} async-done(((bf16[1,32,512]{2,1,0:T(8,128)(2,1)}), bf16[1,2048,512]{2,1,0:T(8,128)(2,1)}) %all-gather.5.cloned.1.call-update) | async-done | bytes 2097168 | tf_op jit(solution)/shard_map/all_gather | solution.py:78
  285.6 4.3 multiply_reduce_fusion.6
  291.1 1.5 fusion.63
  292.8 2.1 collective-permute-start
  294.8 12.3 %collective-permute-done = f32[2,128,1024]{2,1,0:T(8,128)S(1)} collective-permute-done((f32[2,128,1024]{2,1,0:T(8,128)S(1)}, f32[2,128,1024]{2,1,0:T(8,128)S(1)}, u32[]{:S(2)}, u32[]{:S(2)}) %collective-permute-start) | collective-permute-done | bytes 1048608 | tf_op jit(solution)/shard_map/ppermute | solution.py:15
  308.1 1.8 fusion.26
  309.9 3.2 multiply_reduce_fusion.4
  314.2 1.8 fusion.102
  316.4 4.0 collective-permute-start.1
  320.4 12.3 %collective-permute-done.1 = f32[2,128,1024]{2,1,0:T(8,128)S(1)} collective-permute-done((f32[2,128,1024]{2,1,0:T(8,128)S(1)}, f32[2,128,1024]{2,1,0:T(8,128)S(1)}, u32[]{:S(2)}, u32[]{:S(2)}) %collective-permute-start.1) | collective-permute-done | bytes 1048608 | tf_op jit(solution)/shard_map/ppermute | solution.py:15
  333.7 1.8 fusion.22
  335.5 3.2 multiply_reduce_fusion.2
  339.8 1.8 fusion.99
  342.0 4.1 collective-permute-start.2
  346.9 1.8 fusion.133
  349.4 8.8 %collective-permute-done.2 = f32[2,128,1024]{2,1,0:T(8,128)S(1)} collective-permute-done((f32[2,128,1024]{2,1,0:T(8,128)S(1)}, f32[2,128,1024]{2,1,0:T(8,128)S(1)}, u32[]{:S(2)}, u32[]{:S(2)}) %collective-permute-start.2) | collective-permute-done | bytes 1048608 | tf_op jit(solution)/shard_map/ppermute | solution.py:15
  359.2 2.8 add_add_fusion
  365.4 3.5 multiply_reduce_fusion
  370.4 3.8 collective-permute-start.3
  374.1 19.0 %collective-permute-done.3 = f32[2,128,1024]{2,1,0:T(8,128)S(1)} collective-permute-done((f32[2,128,1024]{2,1,0:T(8,128)S(1)}, f32[2,128,1024]{2,1,0:T(8,128)S(1)}, u32[]{:S(2)}, u32[]{:S(2)}) %collective-permute-start.3) | collective-permute-done | bytes 1048608 | tf_op jit(solution)/shard_map/ppermute | solution.py:15
  394.2 426.7 %reduce-scatter.2.cloned.1.call-done = f32[32,512]{1,0:T(8,128)} async-done(((f32[2048,512]{1,0:T(8,128)}), f32[32,512]{1,0:T(8,128)}) %reduce-scatter.2.cloned.1.call-update) | async-done | bytes 65552 | tf_op jit(solution)/shard_map/reduce_scatter | solution.py:66
  (72 shorter events, 18.0 us)
Async XLA Ops:
  7.2 144.3 %all-gather.3.cloned.1.call-start = ((), (), s32[]{:S(2)}) async-start(), calls=%async_computation.1 | async-start | bytes 2129920 | tf_op jit(solution)/shard_map/all_gather | solution.py:77
  7.9 277.7 %all-gather.5.cloned.1.call-start = ((), (), s32[]{:S(2)}) async-start(), calls=%async_computation.2 | async-start | bytes 2129920 | tf_op jit(solution)/shard_map/all_gather | solution.py:78
  8.6 812.2 %reduce-scatter.2.cloned.1.call-start = ((), (), s32[]{:S(2)}) async-start(), calls=%async_computation.3 | async-start | bytes 4259840 | tf_op jit(solution)/shard_map/reduce_scatter | solution.py:66
  10.7 274.8 %copy-start.14 = (f32[1,512]{1,0:T(1,128)S(1)}, f32[1,512]{1,0:T(1,128)}, u32[]{:S(2)}) copy-start(f32[1,512]{1,0:T(1,128)} %param.9) | copy-start | bytes 6148
  285.6 5.5 copy-start
  291.1 1.5 copy-start.13
  292.6 15.5 %copy-start.1 = (bf16[1,2048,512]{2,1,0:T(8,128)(2,1)S(1)}, bf16[1,2048,512]{2,1,0:T(8,128)(2,1)}, u32[]{:S(2)}) copy-start(bf16[1,2048,512]{2,1,0:T(8,128)(2,1)} %all-gather.3.cloned.1.call-done) | copy-start | bytes 6291460
  292.8 14.4 %collective-permute-start = (f32[2,128,1024]{2,1,0:T(8,128)S(1)}, f32[2,128,1024]{2,1,0:T(8,128)S(1)}, u32[]{:S(2)}, u32[]{:S(2)}) collective-permute-start(f32[2,128,1024]{2,1,0:T(8,128)S(1)} %pad_maximum_fusion), channel_id=1, source_target_pairs={{64,0},{128,64},{192,128},{256,192},{320,256},{384,320},{448,384},... | collective-permute-start | bytes 3145736 | tf_op jit(solution)/shard_map/ppermute | solution.py:15
  307.1 1.0 copy-start.7
  314.2 1.9 copy-start.8
  316.1 17.5 %copy-start.2 = (bf16[1,2048,512]{2,1,0:T(8,128)(2,1)S(1)}, bf16[1,2048,512]{2,1,0:T(8,128)(2,1)}, u32[]{:S(2)}) copy-start(bf16[1,2048,512]{2,1,0:T(8,128)(2,1)} %all-gather.3.cloned.1.call-done) | copy-start | bytes 6291460
  316.4 16.3 %collective-permute-start.1 = (f32[2,128,1024]{2,1,0:T(8,128)S(1)}, f32[2,128,1024]{2,1,0:T(8,128)S(1)}, u32[]{:S(2)}, u32[]{:S(2)}) collective-permute-start(f32[2,128,1024]{2,1,0:T(8,128)S(1)} %pad_maximum_fusion.1), channel_id=1, source_target_pairs={{64,0},{128,64},{192,128},{256,192},{320,256},{384,320},{448,384},... | collective-permute-start | bytes 3145736 | tf_op jit(solution)/shard_map/ppermute | solution.py:15
  332.7 1.0 copy-start.9
  339.8 1.9 copy-start.10
  341.7 4.5 copy-start.12
  342.0 4.9 copy-start.4
  342.0 16.3 %collective-permute-start.2 = (f32[2,128,1024]{2,1,0:T(8,128)S(1)}, f32[2,128,1024]{2,1,0:T(8,128)S(1)}, u32[]{:S(2)}, u32[]{:S(2)}) collective-permute-start(f32[2,128,1024]{2,1,0:T(8,128)S(1)} %pad_maximum_fusion.2), channel_id=1, source_target_pairs={{64,0},{128,64},{192,128},{256,192},{320,256},{384,320},{448,384},... | collective-permute-start | bytes 3145736 | tf_op jit(solution)/shard_map/ppermute | solution.py:15
  346.9 1.8 copy-start.5
  348.7 9.7 %copy-start.3 = (bf16[1,2048,512]{2,1,0:T(8,128)(2,1)S(1)}, bf16[1,2048,512]{2,1,0:T(8,128)(2,1)}, u32[]{:S(2)}) copy-start(bf16[1,2048,512]{2,1,0:T(8,128)(2,1)} %all-gather.3.cloned.1.call-done) | copy-start | bytes 6291460
  358.2 1.0 copy-start.6
  368.9 1.3 copy-start.11
  370.4 22.8 %collective-permute-start.3 = (f32[2,128,1024]{2,1,0:T(8,128)S(1)}, f32[2,128,1024]{2,1,0:T(8,128)S(1)}, u32[]{:S(2)}, u32[]{:S(2)}) collective-permute-start(f32[2,128,1024]{2,1,0:T(8,128)S(1)} %pad_maximum_fusion.3), channel_id=1, source_target_pairs={{64,0},{128,64},{192,128},{256,192},{320,256},{384,320},{448,384},... | collective-permute-start | bytes 3145736 | tf_op jit(solution)/shard_map/ppermute | solution.py:15
Sparse Core Ops, SparseCore 0:
  12.3 139.1 all-gather.2
  155.9 129.6 all-gather.4
  362.2 458.6 reduce-scatter.1
where the time goes:
time: 828 us; the launch traced here: 827 us
  waiting for transfers between devices  751 us (91%)
  matrix products  33.7 us (4%)
  between operations  14.2 us (2%)
  starting transfers between devices  14 us (2%)
  other arithmetic  10.5 us (1%)
    reduce_scatter x1, waiting for transfers between devices, reduce_rows(): return lax.psum_scatter(grad_total, 'dp', scatter_dimension=0, tiled=True)  427 us
    all_gather x1, waiting for transfers between devices, local(): lax.all_gather(in_proj, 'dp', axis=1, tiled=True)  139 us
    all_gather x1, waiting for transfers between devices, local(): lax.all_gather(out_proj, 'dp', axis=1, tiled=True)  132 us
    ppermute x4, waiting for transfers between devices, passed_along(): return lax.ppermute(block, axis, route)  52.4 us
  transfers between devices with their start and end apart: 7, of which 7 were waited for; matrix products, arithmetic and copies ran while one was open for 2% of the time, Pallas kernels for 0%

commit v1 on v0

v1 whole, which is shorter than its diff:
```python
import jax
import jax.numpy as jnp
from jax import lax
from jax.sharding import PartitionSpec as P

coupling_scale = 32.0**0.25
rms_epsilon = 1e-06
root_half = 0.7071067811865476
inv_root_two_pi = 0.3989422804014327

x_size = 4
pair_size = 2


def column_groups(dp_size):
    z_size = dp_size // (x_size * pair_size)
    at = lambda z, x, y: (z * x_size + x) * pair_size + y
    along_x = [[at(z, x, y) for x in range(x_size)] for z in range(z_size) for y in range(pair_size)]
    across_x = [[at(z, x, y) for z in range(z_size) for y in range(pair_size)] for x in range(x_size)]
    return along_x, across_x


def exchanged(blocks, groups):
    return lax.all_to_all(blocks, "dp", 0, 0, axis_index_groups=groups, tiled=True)


def copied_to_group(block, groups):
    size = len(groups[0])
    return exchanged(jnp.tile(block, (size, 1)), groups)


def passed_back(block):
    devices = range(lax.axis_size("section"))
    return lax.ppermute(block, "section", [(i, i - 1) for i in devices if i])


def forward(first, second, gain_row, weight_in, weight_out):
    inv_rms = lax.rsqrt(jnp.mean(first * first, axis=-1, keepdims=True) + rms_epsilon)
    normed = (first * inv_rms * gain_row).astype(jnp.bfloat16)
    preact = lax.dot_general(
        normed, weight_in, (((1,), (1,)), ((), ())), preferred_element_type=jnp.float32
    )
    normal_cdf = 0.5 * (1.0 + lax.erf(preact * root_half))
    density = jnp.exp(-0.5 * preact * preact) * inv_root_two_pi
    hidden = (preact * normal_cdf).astype(jnp.bfloat16)
    slopes = normal_cdf + preact * density
    branch = jnp.dot(hidden, weight_out, preferred_element_type=jnp.float32)
    return inv_rms, hidden, slopes, (second - branch) / coupling_scale


def backward(first, inv_rms, slopes, cotangent, first_grad, gain_row, weight_in, weight_out):
    hidden_grad = lax.dot_general(
        cotangent, weight_out, (((1,), (1,)), ((), ())), preferred_element_type=jnp.float32
    )
    pre_grad = (hidden_grad * slopes).astype(jnp.bfloat16)
    scaled = jnp.dot(pre_grad, weight_in, preferred_element_type=jnp.float32) * gain_row
    inner = jnp.mean(first * scaled, axis=-1, keepdims=True)
    return first_grad + inv_rms * scaled - first * (inv_rms * inv_rms * inv_rms) * inner


def local(acts, grads, in_proj, out_proj, gain):
    half = acts.shape[2] // 2
    dp_size = lax.axis_size("dp")
    tick_count = min(4, lax.axis_size("section") // 2)
    along_x, across_x = column_groups(dp_size)
    gain_row = gain[0]
    shard = jnp.concatenate([in_proj[0], out_proj[0]], axis=1)
    weights = copied_to_group(copied_to_group(shard, across_x), along_x)
    weight_in, weight_out = weights[:, :half], weights[:, half:]
    first, second = acts[0, :, :half], acts[0, :, half:]
    first_grad, second_grad = grads[0, :, :half], grads[0, :, half:]
    hiddens, cotangents = [], []
    for tick_index in range(tick_count):
        inv_rms, hidden, slopes, new_first = forward(first, second, gain_row, weight_in, weight_out)
        acts_pair = passed_back(
            jnp.concatenate([new_first, first], axis=1).astype(jnp.bfloat16)
        )
        cotangent = second_grad.astype(jnp.bfloat16)
        hiddens.append(hidden)
        cotangents.append(cotangent)
        new_second_grad = backward(
            first, inv_rms, slopes, cotangent, first_grad, gain_row, weight_in, weight_out
        )
        grads_pair = passed_back(
            jnp.concatenate([cotangent, new_second_grad.astype(jnp.bfloat16)], axis=1)
        )
        acts_pair = acts_pair.astype(jnp.float32)
        grads_pair = grads_pair.astype(jnp.float32)
        first, second = acts_pair[:, :half], acts_pair[:, half:]
        first_grad, second_grad = coupling_scale * grads_pair[:, :half], grads_pair[:, half:]
    outer = lax.dot_general(
        jnp.concatenate(hiddens, axis=0),
        jnp.concatenate(cotangents, axis=0),
        (((0,), (0,)), ((), ())),
        preferred_element_type=jnp.float32,
    ).astype(jnp.bfloat16)
    parts = exchanged(outer, along_x).reshape(x_size, -1, half)
    parts = jnp.sum(parts.astype(jnp.float32), axis=0).astype(jnp.bfloat16)
    parts = exchanged(parts, across_x).reshape(dp_size // x_size, -1, half)
    share = jnp.sum(parts.astype(jnp.float32), axis=0)
    grads_out = jnp.concatenate([first_grad, second_grad], axis=1)
    return (acts_pair[None], grads_out[None], share[None])


def solution(mesh):
    pair = P("section", "dp", None)
    return jax.shard_map(
        local,
        mesh=mesh,
        in_specs=(pair, pair, pair, pair, P("section", None)),
        out_specs=(pair, pair, pair),
        check_vma=False,
    )
```

time: 828 us -> 219 us (0.26)
  the two profiles are of different devices: /device:TPU:16 before, /device:TPU:72 now
where the time goes in v1:
time: 219 us; the launch traced here: 218 us
  waiting for transfers between devices  88.2 us (40%)
  blocking collectives  48.4 us (22%)
  matrix products  37.8 us (17%)
  starting transfers between devices  33.4 us (15%)
  other arithmetic  5.35 us (2%)
  local copies, waits for them, and re-layouts  3.7 us (2%)
    all_to_all x3, waiting for transfers between devices, exchanged(): lax.all_to_all(blocks, 'dp', 0, 0, axis_index_groups=groups, tiled=True)  73.2 us
    all_to_all x1, blocking collectives, exchanged(): lax.all_to_all(blocks, 'dp', 0, 0, axis_index_groups=groups, tiled=True)  48.4 us
    ppermute x8, starting transfers between devices, passed_back(): return lax.ppermute(block, 'section', [(i, i - 1) for i in devices if i])  19.3 us
    ppermute x8, waiting for transfers between devices, passed_back(): return lax.ppermute(block, 'section', [(i, i - 1) for i in devices if i])  15 us
    dot_general x4, matrix products, backward(): jnp.dot(pre_grad, weight_in, preferred_element_type=jnp.float32) * gain_row  15 us
    all_to_all x3, starting transfers between devices, exchanged(): lax.all_to_all(blocks, 'dp', 0, 0, axis_index_groups=groups, tiled=True)  14.1 us
    dot_general x4, matrix products, forward(): lax.dot_general(normed, weight_in, (((1,), (1,)), ((), ())), preferred_el...  11.7 us
    dot_general x4, matrix products, forward(): branch = jnp.dot(hidden, weight_out, preferred_element_type=jnp.float32)  8.42 us
  transfers between devices with their start and end apart: 11, of which 9 were waited for; matrix products, arithmetic and copies ran while one was open for 10% of the time, Pallas kernels for 0%

profile of v1, /device:TPU:72, one launch (start us, length us, event | category | flops | bytes accessed | tf_op | source)
XLA Modules:
  0.0 218.0 jit_solution(11454991336331172075)
XLA Ops:
  1.5 48.4 %all_to_all.33 = bf16[16,32,1024]{2,1,0:T(8,128)(2,1)S(1)} all-to-all(bf16[16,32,1024]{2,1,0:T(8,128)(2,1)S(1)} %tile.6), channel_id=1, replica_groups={{0,1,8,9,16,17,24,25,32,33,40,41,48,49,56,57},{2,3,10,11,18,19,26,27,34..., dimensions={0} | all-to-all | bytes 2097152 | tf_op jit(solution)/shard_map/all_to_all | solution.py:24
  49.9 2.6 %tile.8 = bf16[4,512,1024]{2,1,0:T(8,128)(2,1)} broadcast(bf16[512,1024]{1,0:T(8,128)(2,1)S(1)} %bitcast.62), dimensions={1,2} | broadcast | bytes 5242880 | tf_op jit(solution)/shard_map/tile | solution.py:29
  52.5 5.0 %all-to-all-start.1 = ((bf16[4,512,1024]{2,1,0:T(8,128)(2,1)}), bf16[4,512,1024]{2,1,0:T(8,128)(2,1)}, u32[]{:S(2)}, u32[]{:S(2)}) async-start(bf16[4,512,1024]{2,1,0:T(8,128)(2,1)} %tile.8), calls=%async_computation.1 | async-start | bytes 8388608 | tf_op jit(solution)/shard_map/all_to_all | solution.py:24
  57.7 48.3 %all-to-all-done.1 = bf16[4,512,1024]{2,1,0:T(8,128)(2,1)} async-done(((bf16[4,512,1024]{2,1,0:T(8,128)(2,1)}), bf16[4,512,1024]{2,1,0:T(8,128)(2,1)}, u32[]{:S(2)}, u32[]{:S(2)}) %all-to-all-start.1) | async-done | bytes 4194336 | tf_op jit(solution)/shard_map/all_to_all | solution.py:24
  106.0 3.4 %multiply_convert_fusion.3 = (bf16[128,2048]{1,0:T(8,128)(2,1)S(1)}, f32[128,2048]{1,0:T(8,128)}) fusion(bf16[2048,1024]{1,0:T(8,128)(2,1)} %bitcast.6, f32[1,128,1024]{2,1,0:T(8,128)S(1)} %copy-done, f32[512]{0:T(512)S(1)} %bitcast.67, f32[128]{0:T(128)S(1)} %get-tuple-element.16), kind=kOutput, calls=%fused_computation.55 | convolution fusion | flops 269942784 | bytes 3934720 | tf_op jit(solution)/shard_map/dot_general | solution.py:40
  110.3 2.0 fusion.21
  114.3 3.8 %fusion.96 = (f32[128]{0:T(128)S(1)}, f32[128,512]{1,0:T(8,128)S(1)}) fusion(f32[1,128,1024]{2,1,0:T(8,128)S(1)} %copy-done, f32[512]{0:T(512)S(1)} %bitcast.68, bf16[2048,1024]{1,0:T(8,128)(2,1)} %bitcast.6, f32[128,2048]{1,0:T(8,128)} %get-tuple-element.18, f32[1,128,1024]{2,1,0:T(8,128)S(1)} %copy-done.3), kind=kOutput, calls=%fused_computation.128 | convolution fusion | flops 539688832 | bytes 5900800 | tf_op jit(solution)/shard_map/dot_general | solution.py:56
  120.3 2.5 %multiply_convert_fusion.2 = (bf16[128,2048]{1,0:T(8,128)(2,1)S(1)}, f32[128,2048]{1,0:T(8,128)S(1)}) fusion(bf16[2048,1024]{1,0:T(8,128)(2,1)} %bitcast.6, f32[128,1024]{1,0:T(8,128)S(1)} %convert_element_type.85, f32[128]{0:T(128)S(1)} %get-tuple-element.14, f32[512]{0:T(512)S(1)} %bitcast.69), kind=kOutput, calls=%fused_computation.53 | convolution fusion | flops 269942784 | bytes 3934720 | tf_op jit(solution)/shard_map/dot_general | solution.py:40
  124.0 3.4 %multiply_reduce_fusion.2 = (f32[128]{0:T(128)S(1)}, f32[128,512]{1,0:T(8,128)S(1)}) fusion(f32[128,1024]{1,0:T(8,128)S(1)} %convert_element_type.85, f32[512]{0:T(512)S(1)} %bitcast.70, bf16[2048,1024]{1,0:T(8,128)(2,1)} %bitcast.6, f32[128,2048]{1,0:T(8,128)S(1)} %get-tuple-element.24, bf16[128,1024]{1,0:T(8,128)(2,1)S(1)} %collective-permute-done.4), kind=kOutput, calls=%fused_computation.134 | convolution fusion | flops 539688832 | bytes 5900800 | tf_op jit(solution)/shard_map/dot_general | solution.py:56
  127.5 2.1 subtract_convert_fusion.2
  129.6 3.8 %collective-permute-start.1 = (bf16[128,1024]{1,0:T(8,128)(2,1)S(1)}, bf16[128,1024]{1,0:T(8,128)(2,1)S(1)}, u32[]{:S(2)}, u32[]{:S(2)}) collective-permute-start(bf16[128,1024]{1,0:T(8,128)(2,1)S(1)} %pad_maximum_fusion.1), channel_id=1, source_target_pairs={{64,0},{128,64},{192,128},{256,192},{320,256},{384,320},{448,384},... | collective-permute-start | bytes 786440 | tf_op jit(solution)/shard_map/ppermute | solution.py:34
  137.5 2.5 %multiply_convert_fusion.1 = (bf16[128,2048]{1,0:T(8,128)(2,1)S(1)}, f32[128,2048]{1,0:T(8,128)S(1)}) fusion(bf16[2048,1024]{1,0:T(8,128)(2,1)} %bitcast.6, f32[128,1024]{1,0:T(8,128)S(1)} %convert_element_type.88, f32[128]{0:T(128)S(1)} %get-tuple-element.12, f32[512]{0:T(512)S(1)} %bitcast.71), kind=kOutput, calls=%fused_computation.51 | convolution fusion | flops 269942784 | bytes 3934720 | tf_op jit(solution)/shard_map/dot_general | solution.py:40
  140.1 3.4 %multiply_reduce_fusion.1 = (f32[128]{0:T(128)S(1)}, f32[128,512]{1,0:T(8,128)S(1)}) fusion(f32[128,1024]{1,0:T(8,128)S(1)} %convert_element_type.88, f32[512]{0:T(512)S(1)} %bitcast.72, bf16[2048,1024]{1,0:T(8,128)(2,1)} %bitcast.6, f32[128,2048]{1,0:T(8,128)S(1)} %get-tuple-element.28, bf16[128,1024]{1,0:T(8,128)(2,1)S(1)} %collective-permute-done.5), kind=kOutput, calls=%fused_computation.132 | convolution fusion | flops 539688832 | bytes 5900800 | tf_op jit(solution)/shard_map/dot_general | solution.py:56
  143.6 2.1 subtract_convert_fusion.1
  145.8 3.9 %collective-permute-start.2 = (bf16[128,1024]{1,0:T(8,128)(2,1)S(1)}, bf16[128,1024]{1,0:T(8,128)(2,1)S(1)}, u32[]{:S(2)}, u32[]{:S(2)}) collective-permute-start(bf16[128,1024]{1,0:T(8,128)(2,1)S(1)} %pad_maximum_fusion.2), channel_id=1, source_target_pairs={{64,0},{128,64},{192,128},{256,192},{320,256},{384,320},{448,384},... | collective-permute-start | bytes 786440 | tf_op jit(solution)/shard_map/ppermute | solution.py:34
  153.8 3.4 %multiply_convert_fusion = (bf16[128,2048]{1,0:T(8,128)(2,1)S(1)}, f32[128,2048]{1,0:T(8,128)}) fusion(bf16[2048,1024]{1,0:T(8,128)(2,1)} %bitcast.6, f32[128,1024]{1,0:T(8,128)S(1)} %convert_element_type.91, f32[128]{0:T(128)S(1)} %get-tuple-element.10, f32[512]{0:T(512)S(1)} %bitcast.73), kind=kOutput, calls=%fused_computation.49 | convolution fusion | flops 269942784 | bytes 3934720 | tf_op jit(solution)/shard_map/dot_general | solution.py:40
  157.3 2.7 %convolution_convert_fusion = bf16[2048,512]{1,0:T(8,128)(2,1)} fusion(bf16[128,2048]{1,0:T(8,128)(2,1)S(1)} %get-tuple-element.31, bf16[128,2048]{1,0:T(8,128)(2,1)S(1)} %copy-done.10, bf16[128,2048]{1,0:T(8,128)(2,1)S(1)} %copy-done.8, bf16[128,2048]{1,0:T(8,128)(2,1)S(1)} %copy-done.6, bf16[128,512]{1,0:T(8,128)(2,1)S(1)} %slice.109, ...), kind=kOutput, calls=%fused_computation | convolution fusion | flops 1085276160 | bytes 4718592 | tf_op jit(solution)/shard_map/dot_general | solution.py:91
  159.9 3.6 %all-to-all-start.2 = ((bf16[4,512,512]{2,1,0:T(8,128)(2,1)}), bf16[4,512,512]{2,1,0:T(8,128)(2,1)S(1)}, u32[]{:S(2)}, u32[]{:S(2)}) async-start(bf16[4,512,512]{2,1,0:T(8,128)(2,1)} %bitcast.63), calls=%async_computation.2 | async-start | bytes 4194304 | tf_op jit(solution)/shard_map/all_to_all | solution.py:24
  163.5 4.4 %multiply_reduce_fusion = (f32[128]{0:T(128)S(1)}, f32[128,512]{1,0:T(8,128)}) fusion(f32[128,1024]{1,0:T(8,128)S(1)} %convert_element_type.91, f32[512]{0:T(512)S(1)} %bitcast.74, bf16[2048,1024]{1,0:T(8,128)(2,1)} %bitcast.6, f32[128,2048]{1,0:T(8,128)} %get-tuple-element.32, bf16[128,1024]{1,0:T(8,128)(2,1)S(1)} %collective-permute-done.6), kind=kOutput, calls=%fused_computation.130 | convolution fusion | flops 539688832 | bytes 5900800 | tf_op jit(solution)/shard_map/dot_general | solution.py:56
  167.9 2.2 %subtract_convert_fusion = (bf16[128,512]{1,0:T(8,128)(2,1)S(1)}, bf16[128,512]{1,0:T(8,128)(2,1)S(1)}) fusion(f32[128,512]{1,0:T(8,128)} %get-tuple-element.30, f32[128,1024]{1,0:T(8,128)S(1)} %convert_element_type.91, bf16[128,1024]{1,0:T(8,128)(2,1)S(1)} %collective-permute-done.6, f32[128]{0:T(128)S(1)} %broadcast_multiply_fusion, ...), kind=kOutput, calls=%fused_computation.129 | convolution fusion | flops 269156352 | bytes 3802624 | tf_op jit(solution)/shard_map/dot_general | solution.py:47
  170.1 19.7 %all-to-all-done.2 = bf16[4,512,512]{2,1,0:T(8,128)(2,1)S(1)} async-done(((bf16[4,512,512]{2,1,0:T(8,128)(2,1)}), bf16[4,512,512]{2,1,0:T(8,128)(2,1)S(1)}, u32[]{:S(2)}, u32[]{:S(2)}) %all-to-all-start.2) | async-done | bytes 2097184 | tf_op jit(solution)/shard_map/all_to_all | solution.py:24
  191.1 5.5 %all-to-all-start.3 = ((bf16[16,32,512]{2,1,0:T(8,128)(2,1)}), bf16[16,32,512]{2,1,0:T(8,128)(2,1)S(1)}, u32[]{:S(2)}, u32[]{:S(2)}) async-start(bf16[16,32,512]{2,1,0:T(8,128)(2,1)} %bitcast.13), calls=%async_computation.3 | async-start | bytes 1048576 | tf_op jit(solution)/shard_map/all_to_all | solution.py:24
  200.5 8.0 %collective-permute-done.7 = bf16[128,1024]{1,0:T(8,128)(2,1)S(1)} collective-permute-done((bf16[128,1024]{1,0:T(8,128)(2,1)S(1)}, bf16[128,1024]{1,0:T(8,128)(2,1)S(1)}, u32[]{:S(2)}, u32[]{:S(2)}) %collective-permute-start.7) | collective-permute-done | bytes 262176 | tf_op jit(solution)/shard_map/ppermute | solution.py:34
  212.2 5.2 %all-to-all-done.3 = bf16[16,32,512]{2,1,0:T(8,128)(2,1)S(1)} async-done(((bf16[16,32,512]{2,1,0:T(8,128)(2,1)}), bf16[16,32,512]{2,1,0:T(8,128)(2,1)S(1)}, u32[]{:S(2)}, u32[]{:S(2)}) %all-to-all-start.3) | async-done | bytes 524320 | tf_op jit(solution)/shard_map/all_to_all | solution.py:24
  (80 shorter events, 25.0 us)
Async XLA Ops:
  52.5 5.0 %copy-start = (f32[1,128,1024]{2,1,0:T(8,128)S(1)}, f32[1,128,1024]{2,1,0:T(8,128)}, u32[]{:S(2)}) copy-start(f32[1,128,1024]{2,1,0:T(8,128)} %param.5) | copy-start | bytes 1572868
  52.5 5.2 %copy-start.3 = (f32[1,128,1024]{2,1,0:T(8,128)S(1)}, f32[1,128,1024]{2,1,0:T(8,128)}, u32[]{:S(2)}) copy-start(f32[1,128,1024]{2,1,0:T(8,128)} %param.6) | copy-start | bytes 1572868
  52.5 53.5 %copy-start.4 = (f32[1,512]{1,0:T(1,128)S(1)}, f32[1,512]{1,0:T(1,128)}, u32[]{:S(2)}) copy-start(f32[1,512]{1,0:T(1,128)} %param.9) | copy-start | bytes 6148
  52.5 53.5 %all-to-all-start.1 = ((bf16[4,512,1024]{2,1,0:T(8,128)(2,1)}), bf16[4,512,1024]{2,1,0:T(8,128)(2,1)}, u32[]{:S(2)}, u32[]{:S(2)}) async-start(bf16[4,512,1024]{2,1,0:T(8,128)(2,1)} %tile.8), calls=%async_computation.1 | async-start | bytes 8388608 | tf_op jit(solution)/shard_map/all_to_all | solution.py:24
  112.3 7.8 %collective-permute-start = (bf16[128,1024]{1,0:T(8,128)(2,1)S(1)}, bf16[128,1024]{1,0:T(8,128)(2,1)S(1)}, u32[]{:S(2)}, u32[]{:S(2)}) collective-permute-start(bf16[128,1024]{1,0:T(8,128)(2,1)S(1)} %pad_maximum_fusion), channel_id=1, source_target_pairs={{64,0},{128,64},{192,128},{256,192},{320,256},{384,320},{448,384},... | collective-permute-start | bytes 786440 | tf_op jit(solution)/shard_map/ppermute | solution.py:34
  118.2 5.8 %collective-permute-start.4 = (bf16[128,1024]{1,0:T(8,128)(2,1)S(1)}, bf16[128,1024]{1,0:T(8,128)(2,1)S(1)}, u32[]{:S(2)}, u32[]{:S(2)}) collective-permute-start(bf16[128,1024]{1,0:T(8,128)(2,1)S(1)} %pad_maximum_fusion.4), channel_id=1, source_target_pairs={{64,0},{128,64},{192,128},{256,192},{320,256},{384,320},{448,384},... | collective-permute-start | bytes 786440 | tf_op jit(solution)/shard_map/ppermute | solution.py:34
  120.1 7.3 %copy-start.1 = (bf16[128,1024]{1,0:T(8,128)(2,1)}, bf16[128,1024]{1,0:T(8,128)(2,1)S(1)}, u32[]{:S(2)}) copy-start(bf16[128,1024]{1,0:T(8,128)(2,1)S(1)} %collective-permute-done) | copy-start | bytes 786436
  122.8 4.7 %copy-start.7 = (bf16[128,2048]{1,0:T(8,128)(2,1)}, bf16[128,2048]{1,0:T(8,128)(2,1)S(1)}, u32[]{:S(2)}) copy-start(bf16[128,2048]{1,0:T(8,128)(2,1)S(1)} %get-tuple-element.23) | copy-start | bytes 1572868
  127.4 2.1 slice-start
  129.6 7.7 %collective-permute-start.1 = (bf16[128,1024]{1,0:T(8,128)(2,1)S(1)}, bf16[128,1024]{1,0:T(8,128)(2,1)S(1)}, u32[]{:S(2)}, u32[]{:S(2)}) collective-permute-start(bf16[128,1024]{1,0:T(8,128)(2,1)S(1)} %pad_maximum_fusion.1), channel_id=1, source_target_pairs={{64,0},{128,64},{192,128},{256,192},{320,256},{384,320},{448,384},... | collective-permute-start | bytes 786440 | tf_op jit(solution)/shard_map/ppermute | solution.py:34
  133.5 6.6 %collective-permute-start.5 = (bf16[128,1024]{1,0:T(8,128)(2,1)S(1)}, bf16[128,1024]{1,0:T(8,128)(2,1)S(1)}, u32[]{:S(2)}, u32[]{:S(2)}) collective-permute-start(bf16[128,1024]{1,0:T(8,128)(2,1)S(1)} %pad_maximum_fusion.5), channel_id=1, source_target_pairs={{64,0},{128,64},{192,128},{256,192},{320,256},{384,320},{448,384},... | collective-permute-start | bytes 786440 | tf_op jit(solution)/shard_map/ppermute | solution.py:34
  137.3 6.3 %copy-start.2 = (bf16[128,1024]{1,0:T(8,128)(2,1)}, bf16[128,1024]{1,0:T(8,128)(2,1)S(1)}, u32[]{:S(2)}) copy-start(bf16[128,1024]{1,0:T(8,128)(2,1)S(1)} %collective-permute-done.1) | copy-start | bytes 786436
  139.9 3.7 %copy-start.9 = (bf16[128,2048]{1,0:T(8,128)(2,1)}, bf16[128,2048]{1,0:T(8,128)(2,1)S(1)}, u32[]{:S(2)}) copy-start(bf16[128,2048]{1,0:T(8,128)(2,1)S(1)} %get-tuple-element.27) | copy-start | bytes 1572868
  143.6 2.1 slice-start.1
  145.7 11.5 %copy-start.6 = (bf16[128,2048]{1,0:T(8,128)(2,1)S(1)}, bf16[128,2048]{1,0:T(8,128)(2,1)}, u32[]{:S(2)}) copy-start(bf16[128,2048]{1,0:T(8,128)(2,1)} %copy-done.5) | copy-start | bytes 1572868
  145.7 11.5 %copy-start.8 = (bf16[128,2048]{1,0:T(8,128)(2,1)S(1)}, bf16[128,2048]{1,0:T(8,128)(2,1)}, u32[]{:S(2)}) copy-start(bf16[128,2048]{1,0:T(8,128)(2,1)} %copy-done.7) | copy-start | bytes 1572868
  145.7 11.5 %copy-start.10 = (bf16[128,2048]{1,0:T(8,128)(2,1)S(1)}, bf16[128,2048]{1,0:T(8,128)(2,1)}, u32[]{:S(2)}) copy-start(bf16[128,2048]{1,0:T(8,128)(2,1)} %copy-done.9) | copy-start | bytes 1572868
  145.8 7.8 %collective-permute-start.2 = (bf16[128,1024]{1,0:T(8,128)(2,1)S(1)}, bf16[128,1024]{1,0:T(8,128)(2,1)S(1)}, u32[]{:S(2)}, u32[]{:S(2)}) collective-permute-start(bf16[128,1024]{1,0:T(8,128)(2,1)S(1)} %pad_maximum_fusion.2), channel_id=1, source_target_pairs={{64,0},{128,64},{192,128},{256,192},{320,256},{384,320},{448,384},... | collective-permute-start | bytes 786440 | tf_op jit(solution)/shard_map/ppermute | solution.py:34
  149.8 7.4 %collective-permute-start.6 = (bf16[128,1024]{1,0:T(8,128)(2,1)S(1)}, bf16[128,1024]{1,0:T(8,128)(2,1)S(1)}, u32[]{:S(2)}, u32[]{:S(2)}) collective-permute-start(bf16[128,1024]{1,0:T(8,128)(2,1)S(1)} %pad_maximum_fusion.6), channel_id=1, source_target_pairs={{64,0},{128,64},{192,128},{256,192},{320,256},{384,320},{448,384},... | collective-permute-start | bytes 786440 | tf_op jit(solution)/shard_map/ppermute | solution.py:34
  157.2 2.7 %copy-start.11 = (bf16[128,2048]{1,0:T(8,128)(2,1)}, bf16[128,2048]{1,0:T(8,128)(2,1)S(1)}, u32[]{:S(2)}) copy-start(bf16[128,2048]{1,0:T(8,128)(2,1)S(1)} %get-tuple-element.31) | copy-start | bytes 1572868
  159.9 29.9 %all-to-all-start.2 = ((bf16[4,512,512]{2,1,0:T(8,128)(2,1)}), bf16[4,512,512]{2,1,0:T(8,128)(2,1)S(1)}, u32[]{:S(2)}, u32[]{:S(2)}) async-start(bf16[4,512,512]{2,1,0:T(8,128)(2,1)} %bitcast.63), calls=%async_computation.2 | async-start | bytes 4194304 | tf_op jit(solution)/shard_map/all_to_all | solution.py:24
  191.1 26.3 %all-to-all-start.3 = ((bf16[16,32,512]{2,1,0:T(8,128)(2,1)}), bf16[16,32,512]{2,1,0:T(8,128)(2,1)S(1)}, u32[]{:S(2)}, u32[]{:S(2)}) async-start(bf16[16,32,512]{2,1,0:T(8,128)(2,1)} %bitcast.13), calls=%async_computation.3 | async-start | bytes 1048576 | tf_op jit(solution)/shard_map/all_to_all | solution.py:24
  196.6 11.9 %collective-permute-start.7 = (bf16[128,1024]{1,0:T(8,128)(2,1)S(1)}, bf16[128,1024]{1,0:T(8,128)(2,1)S(1)}, u32[]{:S(2)}, u32[]{:S(2)}) collective-permute-start(bf16[128,1024]{1,0:T(8,128)(2,1)S(1)} %pad_maximum_fusion.7), channel_id=1, source_target_pairs={{64,0},{128,64},{192,128},{256,192},{320,256},{384,320},{448,384},... | collective-permute-start | bytes 786440 | tf_op jit(solution)/shard_map/ppermute | solution.py:34
  198.6 12.8 %collective-permute-start.3 = (bf16[128,1024]{1,0:T(8,128)(2,1)S(1)}, bf16[128,1024]{1,0:T(8,128)(2,1)S(1)}, u32[]{:S(2)}, u32[]{:S(2)}) collective-permute-start(bf16[128,1024]{1,0:T(8,128)(2,1)S(1)} %pad_maximum_fusion.3), channel_id=1, source_target_pairs={{64,0},{128,64},{192,128},{256,192},{320,256},{384,320},{448,384},... | collective-permute-start | bytes 786440 | tf_op jit(solution)/shard_map/ppermute | solution.py:34
  (1 other events, 0.8 us)

commit v2 on v1

v2 whole, which is shorter than its diff:
```python
import functools

import jax
import jax.numpy as jnp
from jax import lax
from jax.experimental import pallas as pl
from jax.experimental.pallas import tpu as pltpu
from jax.sharding import PartitionSpec as P

coupling_scale = 32.0**0.25
rms_epsilon = 1e-06
root_half = 0.7071067811865476
inv_root_two_pi = 0.3989422804014327

x_size = 4
pair_size = 2


def dp_index(z, x, y):
    return (z * x_size + x) * pair_size + y


def z_size():
    return lax.axis_size("dp") // (x_size * pair_size)


def along_z():
    return [
        [dp_index(z, x, y) for z in range(z_size())]
        for x in range(x_size)
        for y in range(pair_size)
    ]


def across_x():
    return [
        [dp_index(z, x, y) for z in range(z_size()) for y in range(pair_size)]
        for x in range(x_size)
    ]


def shifted(block, x_step, y_step=0):
    route = [
        (dp_index(z, (x + x_step) % x_size, (y + y_step) % pair_size), dp_index(z, x, y))
        for z in range(z_size())
        for x in range(x_size)
        for y in range(pair_size)
    ]
    return lax.ppermute(block, "dp", route)


def exchanged(blocks, groups):
    return lax.all_to_all(blocks, "dp", 0, 0, axis_index_groups=groups, tiled=True)


def passed_back(block):
    devices = range(lax.axis_size("section"))
    return lax.ppermute(block, "section", [(i, i - 1) for i in devices if i])


def gathered_along_z(shard):
    return exchanged(jnp.tile(shard, (z_size(), 1)), along_z())


def gathered_along_x(block):
    rows = block.shape[0] // 2
    left, right = shifted(block, -1), shifted(block, 1)
    far_head = shifted(left[:rows], -1)
    far_tail = shifted(right[rows:], 1)
    return block, left, right, far_head, far_tail


def local_copies(weight_refs, weights, sems):
    copies, offset = [], 0
    for i, ref in enumerate(weight_refs):
        rows = ref.shape[0]
        copies.append(
            pltpu.make_async_copy(ref, weights.at[pl.ds(offset, rows)], sems.at[i])
        )
        offset += rows
    for copy in copies:
        copy.start()
    return copies


def forward_kernel(count, acts_ref, gain_ref, *refs):
    weight_refs, (hidden_ref, slopes_ref, acts_out_ref, weights, sems) = refs[:count], refs[count:]
    half = acts_ref.shape[1] // 2
    copies = local_copies(weight_refs, weights, sems)
    first = acts_ref[:, :half].astype(jnp.float32)
    inv_rms = lax.rsqrt(jnp.mean(first * first, axis=-1, keepdims=True) + rms_epsilon)
    normed = (first * inv_rms * gain_ref[...]).astype(jnp.bfloat16)
    offset = 0
    for copy, ref in zip(copies, weight_refs):
        rows = ref.shape[0]
        span = pl.ds(offset, rows)
        copy.wait()
        preact = lax.dot_general(
            normed,
            weights[span, :half],
            (((1,), (1,)), ((), ())),
            preferred_element_type=jnp.float32,
        )
        normal_cdf = 0.5 * (1.0 + lax.erf(preact * root_half))
        density = jnp.exp(-0.5 * preact * preact) * inv_root_two_pi
        hidden_ref[:, span] = (preact * normal_cdf).astype(jnp.bfloat16)
        slopes_ref[:, span] = (normal_cdf + preact * density).astype(slopes_ref.dtype)
        offset += rows
    branch = jnp.dot(hidden_ref[...], weights[:, half:], preferred_element_type=jnp.float32)
    second = acts_ref[:, half:].astype(jnp.float32)
    acts_out_ref[:, :half] = ((second - branch) / coupling_scale).astype(jnp.bfloat16)
    acts_out_ref[:, half:] = first.astype(jnp.bfloat16)


def backward_kernel(count, scale, acts_ref, grads_ref, gain_ref, slopes_ref, *refs):
    weight_refs, (grads_out_ref, pre_grad, weights, sems) = refs[:count], refs[count:]
    half = acts_ref.shape[1] // 2
    copies = local_copies(weight_refs, weights, sems)
    cotangent = grads_ref[:, half:].astype(jnp.bfloat16)
    offset = 0
    for copy, ref in zip(copies, weight_refs):
        rows = ref.shape[0]
        span = pl.ds(offset, rows)
        copy.wait()
        hidden_grad = lax.dot_general(
            cotangent,
            weights[span, half:],
            (((1,), (1,)), ((), ())),
            preferred_element_type=jnp.float32,
        )
        slopes = slopes_ref[:, span].astype(jnp.float32)
        pre_grad[:, span] = (hidden_grad * slopes).astype(jnp.bfloat16)
        offset += rows
    norm_grad = jnp.dot(pre_grad[...], weights[:, :half], preferred_element_type=jnp.float32)
    first = acts_ref[:, :half].astype(jnp.float32)
    inv_rms = lax.rsqrt(jnp.mean(first * first, axis=-1, keepdims=True) + rms_epsilon)
    scaled = norm_grad * gain_ref[...]
    inner = jnp.mean(first * scaled, axis=-1, keepdims=True)
    input_grad = inv_rms * scaled - first * (inv_rms * inv_rms * inv_rms) * inner
    first_grad = grads_ref[:, :half].astype(jnp.float32)
    if scale != 1.0:
        first_grad = first_grad * scale
    grads_out_ref[:, :half] = cotangent
    grads_out_ref[:, half:] = (first_grad + input_grad).astype(jnp.bfloat16)


def scratch(weights, *more):
    rows = sum(w.shape[0] for w in weights)
    return [
        *more,
        pltpu.VMEM((rows, weights[0].shape[1]), jnp.bfloat16),
        pltpu.SemaphoreType.DMA((len(weights),)),
    ]


def in_vmem(count):
    return [pl.BlockSpec(memory_space=pltpu.VMEM)] * count


def cost(tokens, units, half):
    return pl.CostEstimate(
        flops=4 * tokens * units * half,
        bytes_accessed=4 * units * half + 4 * tokens * units,
        transcendentals=2 * tokens * units,
    )


def forward(acts, gain, weights):
    tokens, width = acts.shape
    units = sum(w.shape[0] for w in weights)
    return pl.pallas_call(
        functools.partial(forward_kernel, len(weights)),
        out_shape=(
            jax.ShapeDtypeStruct((tokens, units), jnp.bfloat16),
            jax.ShapeDtypeStruct((tokens, units), jnp.bfloat16),
            jax.ShapeDtypeStruct((tokens, width), jnp.bfloat16),
        ),
        in_specs=in_vmem(2) + [pl.BlockSpec(memory_space=pl.ANY)] * len(weights),
        out_specs=tuple(in_vmem(3)),
        scratch_shapes=scratch(weights),
        cost_estimate=cost(tokens, units, width // 2),
        compiler_params=pltpu.CompilerParams(vmem_limit_bytes=24 * 2**20),
        name="forward_half",
    )(acts, gain, *weights)


def backward(scale, acts, grads, gain, slopes, weights):
    tokens, width = acts.shape
    units = slopes.shape[1]
    return pl.pallas_call(
        functools.partial(backward_kernel, len(weights), scale),
        out_shape=jax.ShapeDtypeStruct((tokens, width), jnp.bfloat16),
        in_specs=in_vmem(4) + [pl.BlockSpec(memory_space=pl.ANY)] * len(weights),
        out_specs=in_vmem(1)[0],
        scratch_shapes=scratch(weights, pltpu.VMEM((tokens, units), jnp.bfloat16)),
        cost_estimate=cost(tokens, units, width // 2),
        compiler_params=pltpu.CompilerParams(vmem_limit_bytes=24 * 2**20),
        name="backward_half",
    )(acts, grads, gain, slopes, *weights)


def outer_rows(hidden, cotangent, start, count):
    rows = lax.slice_in_dim(hidden, start, start + count, axis=1)
    return lax.dot_general(
        rows, cotangent, (((0,), (0,)), ((), ())), preferred_element_type=jnp.float32
    ).astype(jnp.bfloat16)


def local(acts, grads, in_proj, out_proj, gain):
    half = acts.shape[2] // 2
    tick_count = min(4, lax.axis_size("section") // 2)
    shard = jnp.concatenate([in_proj[0], out_proj[0]], axis=1)
    partner_shard = shifted(shard, 0, 1)
    near = gathered_along_x(gathered_along_z(shard))
    far = gathered_along_x(gathered_along_z(partner_shard))
    own_n, left_n, right_n, head_n, tail_n = near
    own_f, left_f, right_f, head_f, tail_f = far
    weights = (own_n, own_f, left_n, left_f, right_n, right_f, head_n, tail_n, head_f, tail_f)
    quarter = own_n.shape[0] * 2

    acts_pair, grads_pair, scale = acts[0], grads[0], 1.0
    hiddens, cotangents = [], []
    for tick_index in range(tick_count):
        hidden, slopes, new_acts = forward(acts_pair, gain, weights)
        next_acts = passed_back(new_acts)
        new_grads = backward(scale, acts_pair, grads_pair, gain, slopes, weights)
        hiddens.append(hidden)
        cotangents.append(new_grads[:, :half])
        acts_pair, grads_pair, scale = next_acts, passed_back(new_grads), coupling_scale

    hidden, cotangent = jnp.concatenate(hiddens, axis=0), jnp.concatenate(cotangents, axis=0)
    far_x = shifted(outer_rows(hidden, cotangent, 3 * quarter, quarter), 2)
    from_right = shifted(outer_rows(hidden, cotangent, quarter, quarter), 1)
    from_left = shifted(outer_rows(hidden, cotangent, 2 * quarter, quarter), -1)
    own = outer_rows(hidden, cotangent, 0, quarter)
    total = (
        own.astype(jnp.float32)
        + from_right.astype(jnp.float32)
        + from_left.astype(jnp.float32)
        + far_x.astype(jnp.float32)
    ).astype(jnp.bfloat16)
    y_hi = lax.axis_index("dp") % pair_size
    mine, other = total[: quarter // 2], total[quarter // 2 :]
    low, high = jnp.where(y_hi == 0, mine, other), jnp.where(y_hi == 0, other, mine)
    units = in_proj.shape[1]
    blocks = jnp.stack([low.reshape(-1, units, half), high.reshape(-1, units, half)], axis=1)
    parts = exchanged(blocks.reshape(-1, half), across_x()).reshape(-1, units, half)
    share = jnp.sum(parts.astype(jnp.float32), axis=0)

    grads_pair = grads_pair.astype(jnp.float32)
    grads_out = jnp.concatenate(
        [coupling_scale * grads_pair[:, :half], grads_pair[:, half:]], axis=1
    )
    return (acts_pair.astype(jnp.float32)[None], grads_out[None], share[None])


def solution(mesh):
    pair = P("section", "dp", None)
    return jax.shard_map(
        local,
        mesh=mesh,
        in_specs=(pair, pair, pair, pair, P("section", None)),
        out_specs=(pair, pair, pair),
        check_vma=False,
    )
```

time: 219 us -> 193 us (0.88)
  the two profiles are of different devices: /device:TPU:72 before, /device:TPU:8 now
where the time goes in v2:
time: 193 us; the launch traced here: 192 us
  starting transfers between devices  79.9 us (41%)
  waiting for transfers between devices  71.7 us (37%)
  Pallas kernels  28.3 us (15%)
  matrix products  4.63 us (2%)
  other arithmetic  4.12 us (2%)
  local copies, waits for them, and re-layouts  2.03 us (1%)
    ppermute x12, starting transfers between devices, shifted(): return lax.ppermute(block, 'dp', route)  42.5 us
    ppermute x12, waiting for transfers between devices, shifted(): return lax.ppermute(block, 'dp', route)  36.9 us
    all_to_all x3, waiting for transfers between devices, exchanged(): lax.all_to_all(blocks, 'dp', 0, 0, axis_index_groups=groups, tiled=True)  22.7 us
    all_to_all x3, starting transfers between devices, exchanged(): lax.all_to_all(blocks, 'dp', 0, 0, axis_index_groups=groups, tiled=True)  21 us
    ppermute x8, starting transfers between devices, passed_back(): return lax.ppermute(block, 'section', [(i, i - 1) for i in devices if i])  16.4 us
    pallas_call x4, Pallas kernels, forward(): pl.pallas_call(functools.partial(forward_kernel, len(weights)), out_shape...  14.7 us
    pallas_call x4, Pallas kernels, backward(): pl.pallas_call(functools.partial(backward_kernel, len(weights), scale), o...  13.6 us
    ppermute x8, waiting for transfers between devices, passed_back(): return lax.ppermute(block, 'section', [(i, i - 1) for i in devices if i])  12.1 us
  transfers between devices with their start and end apart: 23, of which 12 were waited for; matrix products, arithmetic and copies ran while one was open for 1% of the time, Pallas kernels for 11%

profile of v2, /device:TPU:8, one launch (start us, length us, event | category | flops | bytes accessed | tf_op | source)
XLA Modules:
  0.0 191.7 jit_solution(16064168803633011175)
XLA Ops:
  2.3 10.3 %all-to-all-start = ((bf16[8,32,1024]{2,1,0:T(8,128)(2,1)}), bf16[8,32,1024]{2,1,0:T(8,128)(2,1)S(1)}, u32[]{:S(2)}, u32[]{:S(2)}) async-start(bf16[8,32,1024]{2,1,0:T(8,128)(2,1)} %tile.4), calls=%async_computation | async-start | bytes 1048576 | tf_op jit(solution)/shard_map/all_to_all | solution.py:53
  12.6 7.0 %collective-permute-start = (bf16[32,1024]{1,0:T(8,128)(2,1)S(1)}, bf16[32,1024]{1,0:T(8,128)(2,1)S(1)}, u32[]{:S(2)}, u32[]{:S(2)}) collective-permute-start(bf16[32,1024]{1,0:T(8,128)(2,1)S(1)} %pad_maximum_fusion.2), channel_id=1, source_target_pairs={{1,0},{0,1},{3,2},{2,3},{5,4},{4,5},{7,6},{6,7},{9,8},{8,9},{11,10... | collective-permute-start | bytes 196616 | tf_op jit(solution)/shard_map/ppermute | solution.py:49
  22.9 7.2 %all-to-all-done = bf16[8,32,1024]{2,1,0:T(8,128)(2,1)S(1)} async-done(((bf16[8,32,1024]{2,1,0:T(8,128)(2,1)}), bf16[8,32,1024]{2,1,0:T(8,128)(2,1)S(1)}, u32[]{:S(2)}, u32[]{:S(2)}) %all-to-all-start) | async-done | bytes 524320 | tf_op jit(solution)/shard_map/all_to_all | solution.py:53
  30.9 3.5 %all-to-all-start.1 = ((bf16[8,32,1024]{2,1,0:T(8,128)(2,1)}), bf16[8,32,1024]{2,1,0:T(8,128)(2,1)S(1)}, u32[]{:S(2)}, u32[]{:S(2)}) async-start(bf16[8,32,1024]{2,1,0:T(8,128)(2,1)} %tile.5), calls=%async_computation.1 | async-start | bytes 1048576 | tf_op jit(solution)/shard_map/all_to_all | solution.py:53
  34.4 4.7 %collective-permute-start.3 = (bf16[256,1024]{1,0:T(8,128)(2,1)S(1)}, bf16[256,1024]{1,0:T(8,128)(2,1)S(1)}, u32[]{:S(2)}, u32[]{:S(2)}) collective-permute-start(bf16[256,1024]{1,0:T(8,128)(2,1)S(1)} %bitcast.19), channel_id=1, source_target_pairs={{2,0},{3,1},{4,2},{5,3},{6,4},{7,5},{0,6},{1,7},{10,8},{11,9},{12,... | collective-permute-start | bytes 1572872 | tf_op jit(solution)/shard_map/ppermute | solution.py:49
  41.0 11.3 %all-to-all-done.1 = bf16[8,32,1024]{2,1,0:T(8,128)(2,1)S(1)} async-done(((bf16[8,32,1024]{2,1,0:T(8,128)(2,1)}), bf16[8,32,1024]{2,1,0:T(8,128)(2,1)S(1)}, u32[]{:S(2)}, u32[]{:S(2)}) %all-to-all-start.1) | async-done | bytes 524320 | tf_op jit(solution)/shard_map/all_to_all | solution.py:53
  52.3 4.7 %collective-permute-start.4 = (bf16[256,1024]{1,0:T(8,128)(2,1)S(1)}, bf16[256,1024]{1,0:T(8,128)(2,1)S(1)}, u32[]{:S(2)}, u32[]{:S(2)}) collective-permute-start(bf16[256,1024]{1,0:T(8,128)(2,1)S(1)} %bitcast.29), channel_id=1, source_target_pairs={{2,0},{3,1},{4,2},{5,3},{6,4},{7,5},{0,6},{1,7},{10,8},{11,9},{12,... | collective-permute-start | bytes 1572872 | tf_op jit(solution)/shard_map/ppermute | solution.py:49
  58.9 5.1 %collective-permute-start.6 = (bf16[128,1024]{1,0:T(8,128)(2,1)S(1)}, bf16[128,1024]{1,0:T(8,128)(2,1)S(1)}, u32[]{:S(2)}, u32[]{:S(2)}) collective-permute-start(bf16[128,1024]{1,0:T(8,128)(2,1)S(1)} %slice.65), channel_id=1, source_target_pairs={{2,0},{3,1},{4,2},{5,3},{6,4},{7,5},{0,6},{1,7},{10,8},{11,9},{12,... | collective-permute-start | bytes 786440 | tf_op jit(solution)/shard_map/ppermute | solution.py:49
  69.3 5.6 %collective-permute-start.8 = (bf16[128,1024]{1,0:T(8,128)(2,1)S(1)}, bf16[128,1024]{1,0:T(8,128)(2,1)S(1)}, u32[]{:S(2)}, u32[]{:S(2)}) collective-permute-start(bf16[128,1024]{1,0:T(8,128)(2,1)S(1)} %slice.67), channel_id=1, source_target_pairs={{2,0},{3,1},{4,2},{5,3},{6,4},{7,5},{0,6},{1,7},{10,8},{11,9},{12,... | collective-permute-start | bytes 786440 | tf_op jit(solution)/shard_map/ppermute | solution.py:49
  80.0 4.9 %collective-permute-done.7.refs_8_ = bf16[128,1024]{1,0:T(8,128)(2,1)S(1)} collective-permute-done((bf16[128,1024]{1,0:T(8,128)(2,1)S(1)}, bf16[128,1024]{1,0:T(8,128)(2,1)S(1)}, u32[]{:S(2)}, u32[]{:S(2)}) %collective-permute-start.7) | collective-permute-done | bytes 262176 | tf_op jit(solution)/shard_map/ppermute | solution.py:49
  84.9 3.7 %forward_half.4 = (bf16[128,2048]{1,0:T(8,128)(2,1)S(1)}, bf16[128,2048]{1,0:T(8,128)(2,1)S(1)}, bf16[128,1024]{1,0:T(8,128)(2,1)S(1)}) custom-call(f32[128,1024]{1,0:T(8,128)S(1)} %bitcast.39, f32[1,512]{1,0:T(1,128)S(1)} %copy-done.2, bf16[256,1024]{1,0:T(8,128)(2,1)S(1)} %bitcast.21, bf16[256,1024]{1,0:T(8,128)(2,1)S(1)} %bitcast.31, ...), custom_call_target="tpu_custom_call" | custom-call | flops 536870912 | bytes 5242880 | tf_op jit(solution)/shard_map/forward_half/pallas_call | solution.py:171
  90.5 3.4 %backward_half.4 = bf16[128,1024]{1,0:T(8,128)(2,1)S(1)} custom-call(f32[128,1024]{1,0:T(8,128)S(1)} %bitcast.40, f32[128,1024]{1,0:T(8,128)S(1)} %bitcast.41, f32[1,512]{1,0:T(1,128)S(1)} %copy-done.2, bf16[128,2048]{1,0:T(8,128)(2,1)S(1)} %get-tuple-element.19.slopes_ref, bf16[256,1024]{1,0:T(8,128)(2,1)S(1)} %bitcast.22, bf16[256,1024]{1,0:T(8,128)(2,1)S(1)} %bitcast.32, ...), custom_call_target="tpu_custom_call" | custom-call | flops 536870912 | bytes 5242880 | tf_op jit(solution)/shard_map/backward_half/pallas_call | solution.py:190
  96.5 3.7 %forward_half.5 = (bf16[128,2048]{1,0:T(8,128)(2,1)S(1)}, bf16[128,2048]{1,0:T(8,128)(2,1)S(1)}, bf16[128,1024]{1,0:T(8,128)(2,1)S(1)}) custom-call(bf16[128,1024]{1,0:T(8,128)(2,1)S(1)} %collective-permute-done.9.acts_ref, f32[1,512]{1,0:T(1,128)S(1)} %copy-done.2, bf16[256,1024]{1,0:T(8,128)(2,1)S(1)} %bitcast.23, bf16[256,1024]{1,0:T(8,128)(2,1)S(1)} %bitcast.33, ...), custom_call_target="tpu_custom_call" | custom-call | flops 536870912 | bytes 5242880 | tf_op jit(solution)/shard_map/forward_half/pallas_call | solution.py:171
  102.1 3.4 %backward_half.5 = bf16[128,1024]{1,0:T(8,128)(2,1)S(1)} custom-call(bf16[128,1024]{1,0:T(8,128)(2,1)S(1)} %collective-permute-done.9.acts_ref, bf16[128,1024]{1,0:T(8,128)(2,1)S(1)} %collective-permute-done.13.grads_ref, f32[1,512]{1,0:T(1,128)S(1)} %copy-done.2, bf16[128,2048]{1,0:T(8,128)(2,1)S(1)} %get-tuple-element.20.slopes_ref, ...), custom_call_target="tpu_custom_call" | custom-call | flops 536870912 | bytes 5242880 | tf_op jit(solution)/shard_map/backward_half/pallas_call | solution.py:190
  107.6 3.7 %forward_half.6 = (bf16[128,2048]{1,0:T(8,128)(2,1)S(1)}, bf16[128,2048]{1,0:T(8,128)(2,1)S(1)}, bf16[128,1024]{1,0:T(8,128)(2,1)S(1)}) custom-call(bf16[128,1024]{1,0:T(8,128)(2,1)S(1)} %collective-permute-done.10.acts_ref, f32[1,512]{1,0:T(1,128)S(1)} %copy-done.2, bf16[256,1024]{1,0:T(8,128)(2,1)S(1)} %bitcast.25, bf16[256,1024]{1,0:T(8,128)(2,1)S(1)} %bitcast.35, ...), custom_call_target="tpu_custom_call" | custom-call | flops 536870912 | bytes 5242880 | tf_op jit(solution)/shard_map/forward_half/pallas_call | solution.py:171
  113.6 3.4 %backward_half.6 = bf16[128,1024]{1,0:T(8,128)(2,1)S(1)} custom-call(bf16[128,1024]{1,0:T(8,128)(2,1)S(1)} %collective-permute-done.10.acts_ref, bf16[128,1024]{1,0:T(8,128)(2,1)S(1)} %collective-permute-done.14.grads_ref, f32[1,512]{1,0:T(1,128)S(1)} %copy-done.2, bf16[128,2048]{1,0:T(8,128)(2,1)S(1)} %get-tuple-element.21.slopes_ref, ...), custom_call_target="tpu_custom_call" | custom-call | flops 536870912 | bytes 5242880 | tf_op jit(solution)/shard_map/backward_half/pallas_call | solution.py:190
  119.0 3.7 %forward_half.7 = (bf16[128,2048]{1,0:T(8,128)(2,1)S(1)}, bf16[128,2048]{1,0:T(8,128)(2,1)S(1)}, bf16[128,1024]{1,0:T(8,128)(2,1)S(1)}) custom-call(bf16[128,1024]{1,0:T(8,128)(2,1)S(1)} %collective-permute-done.11.acts_ref, f32[1,512]{1,0:T(1,128)S(1)} %copy-done.2, bf16[256,1024]{1,0:T(8,128)(2,1)S(1)} %bitcast.27, bf16[256,1024]{1,0:T(8,128)(2,1)S(1)} %bitcast.37, ...), custom_call_target="tpu_custom_call" | custom-call | flops 536870912 | bytes 5242880 | tf_op jit(solution)/shard_map/forward_half/pallas_call | solution.py:171
  122.9 3.4 %backward_half.7 = bf16[128,1024]{1,0:T(8,128)(2,1)S(1)} custom-call(bf16[128,1024]{1,0:T(8,128)(2,1)S(1)} %collective-permute-done.11.acts_ref, bf16[128,1024]{1,0:T(8,128)(2,1)S(1)} %collective-permute-done.15.grads_ref, f32[1,512]{1,0:T(1,128)S(1)} %copy-done.2, bf16[128,2048]{1,0:T(8,128)(2,1)S(1)} %get-tuple-element.22.slopes_ref, ...), custom_call_target="tpu_custom_call" | custom-call | flops 536870912 | bytes 5242880 | tf_op jit(solution)/shard_map/backward_half/pallas_call | solution.py:190
  131.3 3.9 %collective-permute-start.18 = (bf16[512,512]{1,0:T(8,128)(2,1)}, bf16[512,512]{1,0:T(8,128)(2,1)S(1)}, u32[]{:S(2)}, u32[]{:S(2)}) collective-permute-start(bf16[512,512]{1,0:T(8,128)(2,1)} %convolution_convert_fusion.1), channel_id=1, source_target_pairs={{6,0},{7,1},{0,2},{1,3},{2,4},{3,5},{4,6},{5,7},{14,8},{15,9},{8,1... | collective-permute-start | bytes 1572872 | tf_op jit(solution)/shard_map/ppermute | solution.py:49
  137.2 7.9 %collective-permute-done.17 = bf16[512,512]{1,0:T(8,128)(2,1)S(1)} collective-permute-done((bf16[512,512]{1,0:T(8,128)(2,1)}, bf16[512,512]{1,0:T(8,128)(2,1)S(1)}, u32[]{:S(2)}, u32[]{:S(2)}) %collective-permute-start.17) | collective-permute-done | bytes 524320 | tf_op jit(solution)/shard_map/ppermute | solution.py:49
  145.1 14.4 %collective-permute-done.18 = bf16[512,512]{1,0:T(8,128)(2,1)S(1)} collective-permute-done((bf16[512,512]{1,0:T(8,128)(2,1)}, bf16[512,512]{1,0:T(8,128)(2,1)S(1)}, u32[]{:S(2)}, u32[]{:S(2)}) %collective-permute-start.18) | collective-permute-done | bytes 524320 | tf_op jit(solution)/shard_map/ppermute | solution.py:49
  162.0 7.2 %all-to-all-start.2 = ((bf16[16,32,512]{2,1,0:T(8,128)(2,1)}), bf16[16,32,512]{2,1,0:T(8,128)(2,1)S(1)}, u32[]{:S(2)}, u32[]{:S(2)}) async-start(bf16[16,32,512]{2,1,0:T(8,128)(2,1)} %bitcast.12), calls=%async_computation.2 | async-start | bytes 1048576 | tf_op jit(solution)/shard_map/all_to_all | solution.py:53
  173.0 10.0 %collective-permute-done.16 = bf16[128,1024]{1,0:T(8,128)(2,1)S(1)} collective-permute-done((bf16[128,1024]{1,0:T(8,128)(2,1)S(1)}, bf16[128,1024]{1,0:T(8,128)(2,1)S(1)}, u32[]{:S(2)}, u32[]{:S(2)}) %collective-permute-start.16) | collective-permute-done | bytes 262176 | tf_op jit(solution)/shard_map/ppermute | solution.py:58
  186.7 4.3 %all-to-all-done.2 = bf16[16,32,512]{2,1,0:T(8,128)(2,1)S(1)} async-done(((bf16[16,32,512]{2,1,0:T(8,128)(2,1)}), bf16[16,32,512]{2,1,0:T(8,128)(2,1)S(1)}, u32[]{:S(2)}, u32[]{:S(2)}) %all-to-all-start.2) | async-done | bytes 524320 | tf_op jit(solution)/shard_map/all_to_all | solution.py:53
  (65 shorter events, 50.4 us)
Async XLA Ops:
  2.3 27.8 %all-to-all-start = ((bf16[8,32,1024]{2,1,0:T(8,128)(2,1)}), bf16[8,32,1024]{2,1,0:T(8,128)(2,1)S(1)}, u32[]{:S(2)}, u32[]{:S(2)}) async-start(bf16[8,32,1024]{2,1,0:T(8,128)(2,1)} %tile.4), calls=%async_computation | async-start | bytes 1048576 | tf_op jit(solution)/shard_map/all_to_all | solution.py:53
  12.6 72.3 %copy-start = (f32[1,128,1024]{2,1,0:T(8,128)S(1)}, f32[1,128,1024]{2,1,0:T(8,128)}, u32[]{:S(2)}) copy-start(f32[1,128,1024]{2,1,0:T(8,128)} %param.5) | copy-start | bytes 1572868
  12.6 10.3 %collective-permute-start = (bf16[32,1024]{1,0:T(8,128)(2,1)S(1)}, bf16[32,1024]{1,0:T(8,128)(2,1)S(1)}, u32[]{:S(2)}, u32[]{:S(2)}) collective-permute-start(bf16[32,1024]{1,0:T(8,128)(2,1)S(1)} %pad_maximum_fusion.2), channel_id=1, source_target_pairs={{1,0},{0,1},{3,2},{2,3},{5,4},{4,5},{7,6},{6,7},{9,8},{8,9},{11,10... | collective-permute-start | bytes 196616 | tf_op jit(solution)/shard_map/ppermute | solution.py:49
  30.9 21.4 %all-to-all-start.1 = ((bf16[8,32,1024]{2,1,0:T(8,128)(2,1)}), bf16[8,32,1024]{2,1,0:T(8,128)(2,1)S(1)}, u32[]{:S(2)}, u32[]{:S(2)}) async-start(bf16[8,32,1024]{2,1,0:T(8,128)(2,1)} %tile.5), calls=%async_computation.1 | async-start | bytes 1048576 | tf_op jit(solution)/shard_map/all_to_all | solution.py:53
  34.4 24.5 %collective-permute-start.3 = (bf16[256,1024]{1,0:T(8,128)(2,1)S(1)}, bf16[256,1024]{1,0:T(8,128)(2,1)S(1)}, u32[]{:S(2)}, u32[]{:S(2)}) collective-permute-start(bf16[256,1024]{1,0:T(8,128)(2,1)S(1)} %bitcast.19), channel_id=1, source_target_pairs={{2,0},{3,1},{4,2},{5,3},{6,4},{7,5},{0,6},{1,7},{10,8},{11,9},{12,... | collective-permute-start | bytes 1572872 | tf_op jit(solution)/shard_map/ppermute | solution.py:49
  39.1 25.0 %collective-permute-start.1 = (bf16[256,1024]{1,0:T(8,128)(2,1)S(1)}, bf16[256,1024]{1,0:T(8,128)(2,1)S(1)}, u32[]{:S(2)}, u32[]{:S(2)}) collective-permute-start(bf16[256,1024]{1,0:T(8,128)(2,1)S(1)} %bitcast.20), channel_id=1, source_target_pairs={{6,0},{7,1},{0,2},{1,3},{2,4},{3,5},{4,6},{5,7},{14,8},{15,9},{8,1... | collective-permute-start | bytes 1572872 | tf_op jit(solution)/shard_map/ppermute | solution.py:49
  52.3 17.0 %collective-permute-start.4 = (bf16[256,1024]{1,0:T(8,128)(2,1)S(1)}, bf16[256,1024]{1,0:T(8,128)(2,1)S(1)}, u32[]{:S(2)}, u32[]{:S(2)}) collective-permute-start(bf16[256,1024]{1,0:T(8,128)(2,1)S(1)} %bitcast.29), channel_id=1, source_target_pairs={{2,0},{3,1},{4,2},{5,3},{6,4},{7,5},{0,6},{1,7},{10,8},{11,9},{12,... | collective-permute-start | bytes 1572872 | tf_op jit(solution)/shard_map/ppermute | solution.py:49
  57.0 17.9 %collective-permute-start.2 = (bf16[256,1024]{1,0:T(8,128)(2,1)S(1)}, bf16[256,1024]{1,0:T(8,128)(2,1)S(1)}, u32[]{:S(2)}, u32[]{:S(2)}) collective-permute-start(bf16[256,1024]{1,0:T(8,128)(2,1)S(1)} %bitcast.30), channel_id=1, source_target_pairs={{6,0},{7,1},{0,2},{1,3},{2,4},{3,5},{4,6},{5,7},{14,8},{15,9},{8,1... | collective-permute-start | bytes 1572872 | tf_op jit(solution)/shard_map/ppermute | solution.py:49
  58.9 17.9 %collective-permute-start.6 = (bf16[128,1024]{1,0:T(8,128)(2,1)S(1)}, bf16[128,1024]{1,0:T(8,128)(2,1)S(1)}, u32[]{:S(2)}, u32[]{:S(2)}) collective-permute-start(bf16[128,1024]{1,0:T(8,128)(2,1)S(1)} %slice.65), channel_id=1, source_target_pairs={{2,0},{3,1},{4,2},{5,3},{6,4},{7,5},{0,6},{1,7},{10,8},{11,9},{12,... | collective-permute-start | bytes 786440 | tf_op jit(solution)/shard_map/ppermute | solution.py:49
  64.1 15.8 %collective-permute-start.5 = (bf16[128,1024]{1,0:T(8,128)(2,1)S(1)}, bf16[128,1024]{1,0:T(8,128)(2,1)S(1)}, u32[]{:S(2)}, u32[]{:S(2)}) collective-permute-start(bf16[128,1024]{1,0:T(8,128)(2,1)S(1)} %slice.64), channel_id=1, source_target_pairs={{6,0},{7,1},{0,2},{1,3},{2,4},{3,5},{4,6},{5,7},{14,8},{15,9},{8,1... | collective-permute-start | bytes 786440 | tf_op jit(solution)/shard_map/ppermute | solution.py:49
  69.3 10.7 %collective-permute-start.8 = (bf16[128,1024]{1,0:T(8,128)(2,1)S(1)}, bf16[128,1024]{1,0:T(8,128)(2,1)S(1)}, u32[]{:S(2)}, u32[]{:S(2)}) collective-permute-start(bf16[128,1024]{1,0:T(8,128)(2,1)S(1)} %slice.67), channel_id=1, source_target_pairs={{2,0},{3,1},{4,2},{5,3},{6,4},{7,5},{0,6},{1,7},{10,8},{11,9},{12,... | collective-permute-start | bytes 786440 | tf_op jit(solution)/shard_map/ppermute | solution.py:49
  74.9 10.0 %collective-permute-start.7 = (bf16[128,1024]{1,0:T(8,128)(2,1)S(1)}, bf16[128,1024]{1,0:T(8,128)(2,1)S(1)}, u32[]{:S(2)}, u32[]{:S(2)}) collective-permute-start(bf16[128,1024]{1,0:T(8,128)(2,1)S(1)} %slice.66), channel_id=1, source_target_pairs={{6,0},{7,1},{0,2},{1,3},{2,4},{3,5},{4,6},{5,7},{14,8},{15,9},{8,1... | collective-permute-start | bytes 786440 | tf_op jit(solution)/shard_map/ppermute | solution.py:49
  88.6 7.9 %collective-permute-start.9 = (bf16[128,1024]{1,0:T(8,128)(2,1)S(1)}, bf16[128,1024]{1,0:T(8,128)(2,1)S(1)}, u32[]{:S(2)}, u32[]{:S(2)}) collective-permute-start(bf16[128,1024]{1,0:T(8,128)(2,1)S(1)} %get-tuple-element.15), channel_id=1, source_target_pairs={{64,0},{128,64},{192,128},{256,192},{320,256},{384,320},{448,384},... | collective-permute-start | bytes 786440 | tf_op jit(solution)/shard_map/ppermute | solution.py:58
  94.0 8.1 %collective-permute-start.13 = (bf16[128,1024]{1,0:T(8,128)(2,1)S(1)}, bf16[128,1024]{1,0:T(8,128)(2,1)S(1)}, u32[]{:S(2)}, u32[]{:S(2)}) collective-permute-start(bf16[128,1024]{1,0:T(8,128)(2,1)S(1)} %backward_half.4), channel_id=1, source_target_pairs={{64,0},{128,64},{192,128},{256,192},{320,256},{384,320},{448,384},... | collective-permute-start | bytes 786440 | tf_op jit(solution)/shard_map/ppermute | solution.py:58
  100.2 7.4 %collective-permute-start.10 = (bf16[128,1024]{1,0:T(8,128)(2,1)S(1)}, bf16[128,1024]{1,0:T(8,128)(2,1)S(1)}, u32[]{:S(2)}, u32[]{:S(2)}) collective-permute-start(bf16[128,1024]{1,0:T(8,128)(2,1)S(1)} %get-tuple-element.16), channel_id=1, source_target_pairs={{64,0},{128,64},{192,128},{256,192},{320,256},{384,320},{448,384},... | collective-permute-start | bytes 786440 | tf_op jit(solution)/shard_map/ppermute | solution.py:58
  105.5 8.1 %collective-permute-start.14 = (bf16[128,1024]{1,0:T(8,128)(2,1)S(1)}, bf16[128,1024]{1,0:T(8,128)(2,1)S(1)}, u32[]{:S(2)}, u32[]{:S(2)}) collective-permute-start(bf16[128,1024]{1,0:T(8,128)(2,1)S(1)} %backward_half.5), channel_id=1, source_target_pairs={{64,0},{128,64},{192,128},{256,192},{320,256},{384,320},{448,384},... | collective-permute-start | bytes 786440 | tf_op jit(solution)/shard_map/ppermute | solution.py:58
  111.3 7.8 %collective-permute-start.11 = (bf16[128,1024]{1,0:T(8,128)(2,1)S(1)}, bf16[128,1024]{1,0:T(8,128)(2,1)S(1)}, u32[]{:S(2)}, u32[]{:S(2)}) collective-permute-start(bf16[128,1024]{1,0:T(8,128)(2,1)S(1)} %get-tuple-element.17), channel_id=1, source_target_pairs={{64,0},{128,64},{192,128},{256,192},{320,256},{384,320},{448,384},... | collective-permute-start | bytes 786440 | tf_op jit(solution)/shard_map/ppermute | solution.py:58
  117.1 5.8 %collective-permute-start.15 = (bf16[128,1024]{1,0:T(8,128)(2,1)S(1)}, bf16[128,1024]{1,0:T(8,128)(2,1)S(1)}, u32[]{:S(2)}, u32[]{:S(2)}) collective-permute-start(bf16[128,1024]{1,0:T(8,128)(2,1)S(1)} %backward_half.6), channel_id=1, source_target_pairs={{64,0},{128,64},{192,128},{256,192},{320,256},{384,320},{448,384},... | collective-permute-start | bytes 786440 | tf_op jit(solution)/shard_map/ppermute | solution.py:58
  129.4 15.7 %collective-permute-start.17 = (bf16[512,512]{1,0:T(8,128)(2,1)}, bf16[512,512]{1,0:T(8,128)(2,1)S(1)}, u32[]{:S(2)}, u32[]{:S(2)}) collective-permute-start(bf16[512,512]{1,0:T(8,128)(2,1)} %convolution_convert_fusion.2), channel_id=1, source_target_pairs={{2,0},{3,1},{4,2},{5,3},{6,4},{7,5},{0,6},{1,7},{10,8},{11,9},{12,... | collective-permute-start | bytes 1572872 | tf_op jit(solution)/shard_map/ppermute | solution.py:49
  131.3 28.2 %collective-permute-start.18 = (bf16[512,512]{1,0:T(8,128)(2,1)}, bf16[512,512]{1,0:T(8,128)(2,1)S(1)}, u32[]{:S(2)}, u32[]{:S(2)}) collective-permute-start(bf16[512,512]{1,0:T(8,128)(2,1)} %convolution_convert_fusion.1), channel_id=1, source_target_pairs={{6,0},{7,1},{0,2},{1,3},{2,4},{3,5},{4,6},{5,7},{14,8},{15,9},{8,1... | collective-permute-start | bytes 1572872 | tf_op jit(solution)/shard_map/ppermute | solution.py:49
  135.2 24.2 %collective-permute-start.19 = (bf16[512,512]{1,0:T(8,128)(2,1)S(1)}, bf16[512,512]{1,0:T(8,128)(2,1)S(1)}, u32[]{:S(2)}, u32[]{:S(2)}) collective-permute-start(bf16[512,512]{1,0:T(8,128)(2,1)S(1)} %convolution_convert_fusion), channel_id=1, source_target_pairs={{4,0},{5,1},{6,2},{7,3},{0,4},{1,5},{2,6},{3,7},{12,8},{13,9},{14,... | collective-permute-start | bytes 1572872 | tf_op jit(solution)/shard_map/ppermute | solution.py:49
  162.0 29.0 %all-to-all-start.2 = ((bf16[16,32,512]{2,1,0:T(8,128)(2,1)}), bf16[16,32,512]{2,1,0:T(8,128)(2,1)S(1)}, u32[]{:S(2)}, u32[]{:S(2)}) async-start(bf16[16,32,512]{2,1,0:T(8,128)(2,1)} %bitcast.12), calls=%async_computation.2 | async-start | bytes 1048576 | tf_op jit(solution)/shard_map/all_to_all | solution.py:53
  169.2 13.9 %collective-permute-start.16 = (bf16[128,1024]{1,0:T(8,128)(2,1)S(1)}, bf16[128,1024]{1,0:T(8,128)(2,1)S(1)}, u32[]{:S(2)}, u32[]{:S(2)}) collective-permute-start(bf16[128,1024]{1,0:T(8,128)(2,1)S(1)} %backward_half.7), channel_id=1, source_target_pairs={{64,0},{128,64},{192,128},{256,192},{320,256},{384,320},{448,384},... | collective-permute-start | bytes 786440 | tf_op jit(solution)/shard_map/ppermute | solution.py:58
  171.1 14.8 %collective-permute-start.12 = (bf16[128,1024]{1,0:T(8,128)(2,1)S(1)}, bf16[128,1024]{1,0:T(8,128)(2,1)S(1)}, u32[]{:S(2)}, u32[]{:S(2)}) collective-permute-start(bf16[128,1024]{1,0:T(8,128)(2,1)S(1)} %get-tuple-element.18), channel_id=1, source_target_pairs={{64,0},{128,64},{192,128},{256,192},{320,256},{384,320},{448,384},... | collective-permute-start | bytes 786440 | tf_op jit(solution)/shard_map/ppermute | solution.py:58
  (3 other events, 79.7 us)

commit v3 on v2

v3 whole, which is shorter than its diff:
```python
import functools

import jax
import jax.numpy as jnp
from jax import lax
from jax.experimental import pallas as pl
from jax.experimental.pallas import tpu as pltpu
from jax.sharding import PartitionSpec as P

coupling_scale = 32.0**0.25
rms_epsilon = 1e-06
root_half = 0.7071067811865476
inv_root_two_pi = 0.3989422804014327

x_size = 4
pair_size = 2


def dp_index(z, x, y):
    return (z * x_size + x) * pair_size + y


def z_size():
    return lax.axis_size("dp") // (x_size * pair_size)


def along_z():
    return [
        [dp_index(z, x, y) for z in range(z_size())]
        for x in range(x_size)
        for y in range(pair_size)
    ]


def across_x():
    return [
        [dp_index(z, x, y) for z in range(z_size()) for y in range(pair_size)]
        for x in range(x_size)
    ]


def shifted(block, x_step, y_step=0):
    route = [
        (dp_index(z, (x + x_step) % x_size, (y + y_step) % pair_size), dp_index(z, x, y))
        for z in range(z_size())
        for x in range(x_size)
        for y in range(pair_size)
    ]
    return lax.ppermute(block, "dp", route)


def exchanged(blocks, groups):
    return lax.all_to_all(blocks, "dp", 0, 0, axis_index_groups=groups, tiled=True)


def passed_back(block):
    devices = range(lax.axis_size("section"))
    return lax.ppermute(block, "section", [(i, i - 1) for i in devices if i])


def gathered_along_z(shard):
    return exchanged(jnp.tile(shard, (z_size(), 1)), along_z())


def gathered_along_x(block):
    rows = block.shape[0] // 2
    left, right = shifted(block, -1), shifted(block, 1)
    far_head = shifted(left[:rows], -1)
    far_tail = shifted(right[rows:], 1)
    return block, left, right, far_head, far_tail


def forward_kernel(acts_ref, gain_ref, *refs):
    weight_refs, (hidden_ref, slopes_ref, acts_out_ref) = refs[:-3], refs[-3:]
    half = acts_ref.shape[1] // 2
    first = acts_ref[:, :half].astype(jnp.float32)
    inv_rms = lax.rsqrt(jnp.mean(first * first, axis=-1, keepdims=True) + rms_epsilon)
    normed = (first * inv_rms * gain_ref[...]).astype(jnp.bfloat16)
    for span, weight_ref in spans(weight_refs):
        preact = lax.dot_general(
            normed,
            weight_ref[:, :half],
            (((1,), (1,)), ((), ())),
            preferred_element_type=jnp.float32,
        )
        normal_cdf = 0.5 * (1.0 + lax.erf(preact * root_half))
        density = jnp.exp(-0.5 * preact * preact) * inv_root_two_pi
        hidden_ref[:, span] = (preact * normal_cdf).astype(jnp.bfloat16)
        slopes_ref[:, span] = (normal_cdf + preact * density).astype(slopes_ref.dtype)
    branch = sum(
        jnp.dot(hidden_ref[:, span], weight_ref[:, half:], preferred_element_type=jnp.float32)
        for span, weight_ref in spans(weight_refs)
    )
    second = acts_ref[:, half:].astype(jnp.float32)
    acts_out_ref[:, :half] = ((second - branch) / coupling_scale).astype(jnp.bfloat16)
    acts_out_ref[:, half:] = first.astype(jnp.bfloat16)


def backward_kernel(scale, acts_ref, grads_ref, gain_ref, slopes_ref, *refs):
    weight_refs, (grads_out_ref, pre_grad) = refs[:-2], refs[-2:]
    half = acts_ref.shape[1] // 2
    cotangent = grads_ref[:, half:].astype(jnp.bfloat16)
    for span, weight_ref in spans(weight_refs):
        hidden_grad = lax.dot_general(
            cotangent,
            weight_ref[:, half:],
            (((1,), (1,)), ((), ())),
            preferred_element_type=jnp.float32,
        )
        slopes = slopes_ref[:, span].astype(jnp.float32)
        pre_grad[:, span] = (hidden_grad * slopes).astype(jnp.bfloat16)
    norm_grad = sum(
        jnp.dot(pre_grad[:, span], weight_ref[:, :half], preferred_element_type=jnp.float32)
        for span, weight_ref in spans(weight_refs)
    )
    first = acts_ref[:, :half].astype(jnp.float32)
    inv_rms = lax.rsqrt(jnp.mean(first * first, axis=-1, keepdims=True) + rms_epsilon)
    scaled = norm_grad * gain_ref[...]
    inner = jnp.mean(first * scaled, axis=-1, keepdims=True)
    input_grad = inv_rms * scaled - first * (inv_rms * inv_rms * inv_rms) * inner
    first_grad = grads_ref[:, :half].astype(jnp.float32)
    if scale != 1.0:
        first_grad = first_grad * scale
    grads_out_ref[:, :half] = cotangent
    grads_out_ref[:, half:] = (first_grad + input_grad).astype(jnp.bfloat16)


def outer_kernel(start, columns, *refs):
    ticks = len(columns)
    hidden_refs, cotangent_refs, out_ref = refs[:ticks], refs[ticks:-1], refs[-1]
    count, half = out_ref.shape
    rows = jnp.concatenate([ref[:, start : start + count] for ref in hidden_refs], axis=0)
    cotangents = jnp.concatenate(
        [ref[:, at : at + half] for ref, at in zip(cotangent_refs, columns)], axis=0
    )
    total = lax.dot_general(
        rows, cotangents, (((0,), (0,)), ((), ())), preferred_element_type=jnp.float32
    )
    out_ref[...] = total.astype(out_ref.dtype)


def spans(weight_refs):
    offset = 0
    for ref in weight_refs:
        yield pl.ds(offset, ref.shape[0]), ref
        offset += ref.shape[0]


def in_vmem(count):
    return [pl.BlockSpec(memory_space=pltpu.VMEM)] * count


def cost(tokens, units, half):
    return pl.CostEstimate(
        flops=4 * tokens * units * half,
        bytes_accessed=4 * units * half + 4 * tokens * units,
        transcendentals=2 * tokens * units,
    )


def kernel_params():
    return pltpu.CompilerParams(vmem_limit_bytes=16 * 2**20)


def forward(acts, gain, weights):
    tokens, width = acts.shape
    units = sum(w.shape[0] for w in weights)
    return pl.pallas_call(
        forward_kernel,
        out_shape=(
            jax.ShapeDtypeStruct((tokens, units), jnp.bfloat16),
            jax.ShapeDtypeStruct((tokens, units), jnp.bfloat16),
            jax.ShapeDtypeStruct((tokens, width), jnp.bfloat16),
        ),
        in_specs=in_vmem(2 + len(weights)),
        out_specs=tuple(in_vmem(3)),
        cost_estimate=cost(tokens, units, width // 2),
        compiler_params=kernel_params(),
        name="forward_half",
    )(acts, gain, *weights)


def backward(scale, acts, grads, gain, slopes, weights):
    tokens, width = acts.shape
    units = slopes.shape[1]
    return pl.pallas_call(
        functools.partial(backward_kernel, scale),
        out_shape=jax.ShapeDtypeStruct((tokens, width), jnp.bfloat16),
        in_specs=in_vmem(4 + len(weights)),
        out_specs=in_vmem(1)[0],
        scratch_shapes=[pltpu.VMEM((tokens, units), jnp.bfloat16)],
        cost_estimate=cost(tokens, units, width // 2),
        compiler_params=kernel_params(),
        name="backward_half",
    )(acts, grads, gain, slopes, *weights)


def outer_rows(hiddens, cotangents, columns, start, count):
    half = cotangents[0].shape[1] // 2
    tokens = hiddens[0].shape[0] * len(hiddens)
    return pl.pallas_call(
        functools.partial(outer_kernel, start, columns),
        out_shape=jax.ShapeDtypeStruct((count, half), jnp.bfloat16),
        in_specs=in_vmem(2 * len(hiddens)),
        out_specs=in_vmem(1)[0],
        cost_estimate=pl.CostEstimate(
            flops=2 * tokens * count * half,
            bytes_accessed=2 * (tokens * count + tokens * half + count * half),
            transcendentals=0,
        ),
        compiler_params=kernel_params(),
        name="outer_rows",
    )(*hiddens, *cotangents)


def local(acts, grads, in_proj, out_proj, gain):
    half = acts.shape[2] // 2
    tick_count = min(4, lax.axis_size("section") // 2)
    is_low = (lax.axis_index("dp") & (pair_size - 1)) == 0
    shard = jnp.concatenate([in_proj[0], out_proj[0]], axis=1)
    shard, is_low = lax.optimization_barrier((shard, is_low))
    partner_shard = shifted(shard, 0, 1)
    near = gathered_along_x(gathered_along_z(shard))
    far = gathered_along_x(gathered_along_z(partner_shard))
    own_n, left_n, right_n, head_n, tail_n = near
    own_f, left_f, right_f, head_f, tail_f = far
    weights = (own_n, own_f, left_n, left_f, right_n, right_f, head_n, tail_n, head_f, tail_f)
    quarter = own_n.shape[0] * 2

    acts_pair, grads_pair, scale = acts[0], grads[0], 1.0
    hiddens, cotangents, columns = [], [], []
    for tick_index in range(tick_count):
        hidden, slopes, new_acts = forward(acts_pair, gain, weights)
        next_acts = passed_back(new_acts)
        hiddens.append(hidden)
        if tick_index == tick_count - 1:
            cotangents.append(grads_pair)
            columns.append(half)
            parts = [
                outer_rows(hiddens, cotangents, columns, i * quarter, quarter) for i in (3, 1, 2)
            ]
            far_x = shifted(parts[0], 2)
            from_right = shifted(parts[1], 1)
            from_left = shifted(parts[2], -1)
            acts_pair, grads_pair, _ = lax.optimization_barrier(
                (acts_pair, grads_pair, parts)
            )
        new_grads = backward(scale, acts_pair, grads_pair, gain, slopes, weights)
        if tick_index < tick_count - 1:
            cotangents.append(new_grads)
            columns.append(0)
        acts_pair, grads_pair, scale = next_acts, passed_back(new_grads), coupling_scale

    own = outer_rows(hiddens, cotangents, columns, 0, quarter)
    total = (
        own.astype(jnp.float32)
        + from_right.astype(jnp.float32)
        + from_left.astype(jnp.float32)
        + far_x.astype(jnp.float32)
    ).astype(jnp.bfloat16)
    mine, other = total[: quarter // 2], total[quarter // 2 :]
    low, high = jnp.where(is_low, mine, other), jnp.where(is_low, other, mine)
    units = in_proj.shape[1]
    blocks = jnp.stack([low.reshape(-1, units, half), high.reshape(-1, units, half)], axis=1)
    blocks, acts_pair, grads_pair = lax.optimization_barrier(
        (blocks.reshape(-1, half), acts_pair, grads_pair)
    )
    parts = exchanged(blocks, across_x()).reshape(-1, units, half)
    share = jnp.sum(parts.astype(jnp.float32), axis=0)

    grads_pair = grads_pair.astype(jnp.float32)
    grads_out = jnp.concatenate(
        [coupling_scale * grads_pair[:, :half], grads_pair[:, half:]], axis=1
    )
    return (acts_pair.astype(jnp.float32)[None], grads_out[None], share[None])


def solution(mesh):
    pair = P("section", "dp", None)
    return jax.shard_map(
        local,
        mesh=mesh,
        in_specs=(pair, pair, pair, pair, P("section", None)),
        out_specs=(pair, pair, pair),
        check_vma=False,
    )
```

time: 193 us -> 174 us (0.902)
  the two profiles are of different devices: /device:TPU:8 before, /device:TPU:40 now
where the time goes in v3:
time: 174 us; the launch traced here: 173 us
  starting transfers between devices  85.4 us (49%)
  waiting for transfers between devices  67.3 us (39%)
  Pallas kernels  12.6 us (7%)
  other arithmetic  4.4 us (3%)
  local copies, waits for them, and re-layouts  1.82 us (1%)
    ppermute x12, starting transfers between devices, shifted(): return lax.ppermute(block, 'dp', route)  41.7 us
    all_to_all x3, waiting for transfers between devices, exchanged(): lax.all_to_all(blocks, 'dp', 0, 0, axis_index_groups=groups, tiled=True)  32.5 us
    ppermute x12, waiting for transfers between devices, shifted(): return lax.ppermute(block, 'dp', route)  32.4 us
    ppermute x8, starting transfers between devices, passed_back(): return lax.ppermute(block, 'section', [(i, i - 1) for i in devices if i])  22.6 us
    all_to_all x3, starting transfers between devices, exchanged(): lax.all_to_all(blocks, 'dp', 0, 0, axis_index_groups=groups, tiled=True)  21 us
    pallas_call x4, Pallas kernels, forward(): pl.pallas_call(forward_kernel, out_shape=(jax.ShapeDtypeStruct((tokens, u...  5.7 us
    pallas_call x4, Pallas kernels, backward(): pl.pallas_call(functools.partial(backward_kernel, scale), out_shape=jax.S...  4.96 us
  transfers between devices with their start and end apart: 23, of which 11 were waited for; matrix products, arithmetic and copies ran while one was open for 2% of the time, Pallas kernels for 6%

profile of v3, /device:TPU:40, one launch (start us, length us, event | category | flops | bytes accessed | tf_op | source)
XLA Modules:
  0.0 172.5 jit_solution(10117590202918169322)
XLA Ops:
  2.3 10.3 %all-to-all-start = ((bf16[8,32,1024]{2,1,0:T(8,128)(2,1)}), bf16[8,32,1024]{2,1,0:T(8,128)(2,1)S(1)}, u32[]{:S(2)}, u32[]{:S(2)}) async-start(bf16[8,32,1024]{2,1,0:T(8,128)(2,1)} %tile.4), calls=%async_computation | async-start | bytes 1048576 | tf_op jit(solution)/shard_map/all_to_all | solution.py:53
  15.5 7.7 %collective-permute-done = bf16[32,1024]{1,0:T(8,128)(2,1)S(1)} collective-permute-done((bf16[32,1024]{1,0:T(8,128)(2,1)S(1)}, bf16[32,1024]{1,0:T(8,128)(2,1)S(1)}, u32[]{:S(2)}, u32[]{:S(2)}) %collective-permute-start) | collective-permute-done | bytes 65568 | tf_op jit(solution)/shard_map/ppermute | solution.py:49
  23.2 6.9 %all-to-all-done = bf16[8,32,1024]{2,1,0:T(8,128)(2,1)S(1)} async-done(((bf16[8,32,1024]{2,1,0:T(8,128)(2,1)}), bf16[8,32,1024]{2,1,0:T(8,128)(2,1)S(1)}, u32[]{:S(2)}, u32[]{:S(2)}) %all-to-all-start) | async-done | bytes 524320 | tf_op jit(solution)/shard_map/all_to_all | solution.py:53
  30.9 3.5 %all-to-all-start.1 = ((bf16[8,32,1024]{2,1,0:T(8,128)(2,1)}), bf16[8,32,1024]{2,1,0:T(8,128)(2,1)S(1)}, u32[]{:S(2)}, u32[]{:S(2)}) async-start(bf16[8,32,1024]{2,1,0:T(8,128)(2,1)} %tile.5), calls=%async_computation.1 | async-start | bytes 1048576 | tf_op jit(solution)/shard_map/all_to_all | solution.py:53
  34.4 3.4 %collective-permute-start.1 = (bf16[256,1024]{1,0:T(8,128)(2,1)S(1)}, bf16[256,1024]{1,0:T(8,128)(2,1)S(1)}, u32[]{:S(2)}, u32[]{:S(2)}) collective-permute-start(bf16[256,1024]{1,0:T(8,128)(2,1)S(1)} %bitcast.20), channel_id=1, source_target_pairs={{6,0},{7,1},{0,2},{1,3},{2,4},{3,5},{4,6},{5,7},{14,8},{15,9},{8,1... | collective-permute-start | bytes 1572872 | tf_op jit(solution)/shard_map/ppermute | solution.py:49
  37.8 3.7 %collective-permute-start.3 = (bf16[256,1024]{1,0:T(8,128)(2,1)S(1)}, bf16[256,1024]{1,0:T(8,128)(2,1)S(1)}, u32[]{:S(2)}, u32[]{:S(2)}) collective-permute-start(bf16[256,1024]{1,0:T(8,128)(2,1)S(1)} %bitcast.21), channel_id=1, source_target_pairs={{2,0},{3,1},{4,2},{5,3},{6,4},{7,5},{0,6},{1,7},{10,8},{11,9},{12,... | collective-permute-start | bytes 1572872 | tf_op jit(solution)/shard_map/ppermute | solution.py:49
  41.5 10.8 %all-to-all-done.1 = bf16[8,32,1024]{2,1,0:T(8,128)(2,1)S(1)} async-done(((bf16[8,32,1024]{2,1,0:T(8,128)(2,1)}), bf16[8,32,1024]{2,1,0:T(8,128)(2,1)S(1)}, u32[]{:S(2)}, u32[]{:S(2)}) %all-to-all-start.1) | async-done | bytes 524320 | tf_op jit(solution)/shard_map/all_to_all | solution.py:53
  52.3 3.4 %collective-permute-start.2 = (bf16[256,1024]{1,0:T(8,128)(2,1)S(1)}, bf16[256,1024]{1,0:T(8,128)(2,1)S(1)}, u32[]{:S(2)}, u32[]{:S(2)}) collective-permute-start(bf16[256,1024]{1,0:T(8,128)(2,1)S(1)} %bitcast.30), channel_id=1, source_target_pairs={{6,0},{7,1},{0,2},{1,3},{2,4},{3,5},{4,6},{5,7},{14,8},{15,9},{8,1... | collective-permute-start | bytes 1572872 | tf_op jit(solution)/shard_map/ppermute | solution.py:49
  55.7 3.7 %collective-permute-start.4 = (bf16[256,1024]{1,0:T(8,128)(2,1)S(1)}, bf16[256,1024]{1,0:T(8,128)(2,1)S(1)}, u32[]{:S(2)}, u32[]{:S(2)}) collective-permute-start(bf16[256,1024]{1,0:T(8,128)(2,1)S(1)} %bitcast.31), channel_id=1, source_target_pairs={{2,0},{3,1},{4,2},{5,3},{6,4},{7,5},{0,6},{1,7},{10,8},{11,9},{12,... | collective-permute-start | bytes 1572872 | tf_op jit(solution)/shard_map/ppermute | solution.py:49
  61.6 5.0 %collective-permute-start.6 = (bf16[128,1024]{1,0:T(8,128)(2,1)S(1)}, bf16[128,1024]{1,0:T(8,128)(2,1)S(1)}, u32[]{:S(2)}, u32[]{:S(2)}) collective-permute-start(bf16[128,1024]{1,0:T(8,128)(2,1)S(1)} %slice.33), channel_id=1, source_target_pairs={{2,0},{3,1},{4,2},{5,3},{6,4},{7,5},{0,6},{1,7},{10,8},{11,9},{12,... | collective-permute-start | bytes 786440 | tf_op jit(solution)/shard_map/ppermute | solution.py:49
  66.6 3.5 %collective-permute-done.2.refs_3_ = bf16[256,1024]{1,0:T(8,128)(2,1)S(1)} collective-permute-done((bf16[256,1024]{1,0:T(8,128)(2,1)S(1)}, bf16[256,1024]{1,0:T(8,128)(2,1)S(1)}, u32[]{:S(2)}, u32[]{:S(2)}) %collective-permute-start.2) | collective-permute-done | bytes 524320 | tf_op jit(solution)/shard_map/ppermute | solution.py:49
  72.5 4.9 %collective-permute-start.8 = (bf16[128,1024]{1,0:T(8,128)(2,1)S(1)}, bf16[128,1024]{1,0:T(8,128)(2,1)S(1)}, u32[]{:S(2)}, u32[]{:S(2)}) collective-permute-start(bf16[128,1024]{1,0:T(8,128)(2,1)S(1)} %slice.35), channel_id=1, source_target_pairs={{2,0},{3,1},{4,2},{5,3},{6,4},{7,5},{0,6},{1,7},{10,8},{11,9},{12,... | collective-permute-start | bytes 786440 | tf_op jit(solution)/shard_map/ppermute | solution.py:49
  87.0 3.4 %collective-permute-start.12 = (bf16[128,1024]{1,0:T(8,128)(2,1)S(1)}, bf16[128,1024]{1,0:T(8,128)(2,1)S(1)}, u32[]{:S(2)}, u32[]{:S(2)}) collective-permute-start(bf16[128,1024]{1,0:T(8,128)(2,1)S(1)} %backward_half.4.refs_4_), channel_id=1, source_target_pairs={{64,0},{128,64},{192,128},{256,192},{320,256},{384,320},{448,384},... | collective-permute-start | bytes 786440 | tf_op jit(solution)/shard_map/ppermute | solution.py:58
  91.8 3.1 %collective-permute-start.10 = (bf16[128,1024]{1,0:T(8,128)(2,1)S(1)}, bf16[128,1024]{1,0:T(8,128)(2,1)S(1)}, u32[]{:S(2)}, u32[]{:S(2)}) collective-permute-start(bf16[128,1024]{1,0:T(8,128)(2,1)S(1)} %get-tuple-element.27), channel_id=1, source_target_pairs={{64,0},{128,64},{192,128},{256,192},{320,256},{384,320},{448,384},... | collective-permute-start | bytes 786440 | tf_op jit(solution)/shard_map/ppermute | solution.py:58
  96.1 3.2 %collective-permute-start.13 = (bf16[128,1024]{1,0:T(8,128)(2,1)S(1)}, bf16[128,1024]{1,0:T(8,128)(2,1)S(1)}, u32[]{:S(2)}, u32[]{:S(2)}) collective-permute-start(bf16[128,1024]{1,0:T(8,128)(2,1)S(1)} %backward_half.5.refs_5_), channel_id=1, source_target_pairs={{64,0},{128,64},{192,128},{256,192},{320,256},{384,320},{448,384},... | collective-permute-start | bytes 786440 | tf_op jit(solution)/shard_map/ppermute | solution.py:58
  100.8 3.2 %collective-permute-start.11 = (bf16[128,1024]{1,0:T(8,128)(2,1)S(1)}, bf16[128,1024]{1,0:T(8,128)(2,1)S(1)}, u32[]{:S(2)}, u32[]{:S(2)}) collective-permute-start(bf16[128,1024]{1,0:T(8,128)(2,1)S(1)} %get-tuple-element.29), channel_id=1, source_target_pairs={{64,0},{128,64},{192,128},{256,192},{320,256},{384,320},{448,384},... | collective-permute-start | bytes 786440 | tf_op jit(solution)/shard_map/ppermute | solution.py:58
  105.3 3.0 %collective-permute-start.14 = (bf16[128,1024]{1,0:T(8,128)(2,1)S(1)}, bf16[128,1024]{1,0:T(8,128)(2,1)S(1)}, u32[]{:S(2)}, u32[]{:S(2)}) collective-permute-start(bf16[128,1024]{1,0:T(8,128)(2,1)S(1)} %backward_half.6.refs_6_), channel_id=1, source_target_pairs={{64,0},{128,64},{192,128},{256,192},{320,256},{384,320},{448,384},... | collective-permute-start | bytes 786440 | tf_op jit(solution)/shard_map/ppermute | solution.py:58
  112.6 4.9 %collective-permute-start.15 = (bf16[512,512]{1,0:T(8,128)(2,1)S(1)}, bf16[512,512]{1,0:T(8,128)(2,1)S(1)}, u32[]{:S(2)}, u32[]{:S(2)}) collective-permute-start(bf16[512,512]{1,0:T(8,128)(2,1)S(1)} %outer_rows.5), channel_id=1, source_target_pairs={{2,0},{3,1},{4,2},{5,3},{6,4},{7,5},{0,6},{1,7},{10,8},{11,9},{12,... | collective-permute-start | bytes 1572872 | tf_op jit(solution)/shard_map/ppermute | solution.py:49
  120.4 3.7 %collective-permute-start.17 = (bf16[512,512]{1,0:T(8,128)(2,1)S(1)}, bf16[512,512]{1,0:T(8,128)(2,1)S(1)}, u32[]{:S(2)}, u32[]{:S(2)}) collective-permute-start(bf16[512,512]{1,0:T(8,128)(2,1)S(1)} %outer_rows.7), channel_id=1, source_target_pairs={{4,0},{5,1},{6,2},{7,3},{0,4},{1,5},{2,6},{3,7},{12,8},{13,9},{14,... | collective-permute-start | bytes 1572872 | tf_op jit(solution)/shard_map/ppermute | solution.py:49
  125.3 3.0 %collective-permute-start.19 = (bf16[128,1024]{1,0:T(8,128)(2,1)S(1)}, bf16[128,1024]{1,0:T(8,128)(2,1)S(1)}, u32[]{:S(2)}, u32[]{:S(2)}) collective-permute-start(bf16[128,1024]{1,0:T(8,128)(2,1)S(1)} %backward_half.7), channel_id=1, source_target_pairs={{64,0},{128,64},{192,128},{256,192},{320,256},{384,320},{448,384},... | collective-permute-start | bytes 786440 | tf_op jit(solution)/shard_map/ppermute | solution.py:58
  130.8 10.3 %collective-permute-done.15 = bf16[512,512]{1,0:T(8,128)(2,1)S(1)} collective-permute-done((bf16[512,512]{1,0:T(8,128)(2,1)S(1)}, bf16[512,512]{1,0:T(8,128)(2,1)S(1)}, u32[]{:S(2)}, u32[]{:S(2)}) %collective-permute-start.15) | collective-permute-done | bytes 524320 | tf_op jit(solution)/shard_map/ppermute | solution.py:49
  141.0 5.8 %collective-permute-done.16 = bf16[512,512]{1,0:T(8,128)(2,1)S(1)} collective-permute-done((bf16[512,512]{1,0:T(8,128)(2,1)S(1)}, bf16[512,512]{1,0:T(8,128)(2,1)S(1)}, u32[]{:S(2)}, u32[]{:S(2)}) %collective-permute-start.16) | collective-permute-done | bytes 524320 | tf_op jit(solution)/shard_map/ppermute | solution.py:49
  148.0 7.2 %all-to-all-start.2 = ((bf16[16,32,512]{2,1,0:T(8,128)(2,1)}), bf16[16,32,512]{2,1,0:T(8,128)(2,1)S(1)}, u32[]{:S(2)}, u32[]{:S(2)}) async-start(bf16[16,32,512]{2,1,0:T(8,128)(2,1)} %bitcast.13), calls=%async_computation.2 | async-start | bytes 1048576 | tf_op jit(solution)/shard_map/all_to_all | solution.py:53
  157.0 14.8 %all-to-all-done.2 = bf16[16,32,512]{2,1,0:T(8,128)(2,1)S(1)} async-done(((bf16[16,32,512]{2,1,0:T(8,128)(2,1)}), bf16[16,32,512]{2,1,0:T(8,128)(2,1)S(1)}, u32[]{:S(2)}, u32[]{:S(2)}) %all-to-all-start.2) | async-done | bytes 524320 | tf_op jit(solution)/shard_map/all_to_all | solution.py:53
  (56 shorter events, 39.4 us)
Async XLA Ops:
  2.3 27.8 %all-to-all-start = ((bf16[8,32,1024]{2,1,0:T(8,128)(2,1)}), bf16[8,32,1024]{2,1,0:T(8,128)(2,1)S(1)}, u32[]{:S(2)}, u32[]{:S(2)}) async-start(bf16[8,32,1024]{2,1,0:T(8,128)(2,1)} %tile.4), calls=%async_computation | async-start | bytes 1048576 | tf_op jit(solution)/shard_map/all_to_all | solution.py:53
  12.6 10.6 %collective-permute-start = (bf16[32,1024]{1,0:T(8,128)(2,1)S(1)}, bf16[32,1024]{1,0:T(8,128)(2,1)S(1)}, u32[]{:S(2)}, u32[]{:S(2)}) collective-permute-start(bf16[32,1024]{1,0:T(8,128)(2,1)S(1)} %pad_maximum_fusion.1), channel_id=1, source_target_pairs={{1,0},{0,1},{3,2},{2,3},{5,4},{4,5},{7,6},{6,7},{9,8},{8,9},{11,10... | collective-permute-start | bytes 196616 | tf_op jit(solution)/shard_map/ppermute | solution.py:49
  30.9 21.4 %all-to-all-start.1 = ((bf16[8,32,1024]{2,1,0:T(8,128)(2,1)}), bf16[8,32,1024]{2,1,0:T(8,128)(2,1)S(1)}, u32[]{:S(2)}, u32[]{:S(2)}) async-start(bf16[8,32,1024]{2,1,0:T(8,128)(2,1)} %tile.5), calls=%async_computation.1 | async-start | bytes 1048576 | tf_op jit(solution)/shard_map/all_to_all | solution.py:53
  34.4 24.9 %collective-permute-start.1 = (bf16[256,1024]{1,0:T(8,128)(2,1)S(1)}, bf16[256,1024]{1,0:T(8,128)(2,1)S(1)}, u32[]{:S(2)}, u32[]{:S(2)}) collective-permute-start(bf16[256,1024]{1,0:T(8,128)(2,1)S(1)} %bitcast.20), channel_id=1, source_target_pairs={{6,0},{7,1},{0,2},{1,3},{2,4},{3,5},{4,6},{5,7},{14,8},{15,9},{8,1... | collective-permute-start | bytes 1572872 | tf_op jit(solution)/shard_map/ppermute | solution.py:49
  37.8 23.8 %collective-permute-start.3 = (bf16[256,1024]{1,0:T(8,128)(2,1)S(1)}, bf16[256,1024]{1,0:T(8,128)(2,1)S(1)}, u32[]{:S(2)}, u32[]{:S(2)}) collective-permute-start(bf16[256,1024]{1,0:T(8,128)(2,1)S(1)} %bitcast.21), channel_id=1, source_target_pairs={{2,0},{3,1},{4,2},{5,3},{6,4},{7,5},{0,6},{1,7},{10,8},{11,9},{12,... | collective-permute-start | bytes 1572872 | tf_op jit(solution)/shard_map/ppermute | solution.py:49
  52.3 17.9 %collective-permute-start.2 = (bf16[256,1024]{1,0:T(8,128)(2,1)S(1)}, bf16[256,1024]{1,0:T(8,128)(2,1)S(1)}, u32[]{:S(2)}, u32[]{:S(2)}) collective-permute-start(bf16[256,1024]{1,0:T(8,128)(2,1)S(1)} %bitcast.30), channel_id=1, source_target_pairs={{6,0},{7,1},{0,2},{1,3},{2,4},{3,5},{4,6},{5,7},{14,8},{15,9},{8,1... | collective-permute-start | bytes 1572872 | tf_op jit(solution)/shard_map/ppermute | solution.py:49
  55.7 16.7 %collective-permute-start.4 = (bf16[256,1024]{1,0:T(8,128)(2,1)S(1)}, bf16[256,1024]{1,0:T(8,128)(2,1)S(1)}, u32[]{:S(2)}, u32[]{:S(2)}) collective-permute-start(bf16[256,1024]{1,0:T(8,128)(2,1)S(1)} %bitcast.31), channel_id=1, source_target_pairs={{2,0},{3,1},{4,2},{5,3},{6,4},{7,5},{0,6},{1,7},{10,8},{11,9},{12,... | collective-permute-start | bytes 1572872 | tf_op jit(solution)/shard_map/ppermute | solution.py:49
  59.4 17.9 %collective-permute-start.5 = (bf16[128,1024]{1,0:T(8,128)(2,1)S(1)}, bf16[128,1024]{1,0:T(8,128)(2,1)S(1)}, u32[]{:S(2)}, u32[]{:S(2)}) collective-permute-start(bf16[128,1024]{1,0:T(8,128)(2,1)S(1)} %slice.32), channel_id=1, source_target_pairs={{6,0},{7,1},{0,2},{1,3},{2,4},{3,5},{4,6},{5,7},{14,8},{15,9},{8,1... | collective-permute-start | bytes 786440 | tf_op jit(solution)/shard_map/ppermute | solution.py:49
  61.6 20.8 %copy-start = (f32[1,128,1024]{2,1,0:T(8,128)S(1)}, f32[1,128,1024]{2,1,0:T(8,128)}, u32[]{:S(2)}) copy-start(f32[1,128,1024]{2,1,0:T(8,128)} %param.5) | copy-start | bytes 1572868
  61.6 16.4 %collective-permute-start.6 = (bf16[128,1024]{1,0:T(8,128)(2,1)S(1)}, bf16[128,1024]{1,0:T(8,128)(2,1)S(1)}, u32[]{:S(2)}, u32[]{:S(2)}) collective-permute-start(bf16[128,1024]{1,0:T(8,128)(2,1)S(1)} %slice.33), channel_id=1, source_target_pairs={{2,0},{3,1},{4,2},{5,3},{6,4},{7,5},{0,6},{1,7},{10,8},{11,9},{12,... | collective-permute-start | bytes 786440 | tf_op jit(solution)/shard_map/ppermute | solution.py:49
  70.2 10.3 %collective-permute-start.7 = (bf16[128,1024]{1,0:T(8,128)(2,1)S(1)}, bf16[128,1024]{1,0:T(8,128)(2,1)S(1)}, u32[]{:S(2)}, u32[]{:S(2)}) collective-permute-start(bf16[128,1024]{1,0:T(8,128)(2,1)S(1)} %slice.34), channel_id=1, source_target_pairs={{6,0},{7,1},{0,2},{1,3},{2,4},{3,5},{4,6},{5,7},{14,8},{15,9},{8,1... | collective-permute-start | bytes 786440 | tf_op jit(solution)/shard_map/ppermute | solution.py:49
  72.5 9.9 %collective-permute-start.8 = (bf16[128,1024]{1,0:T(8,128)(2,1)S(1)}, bf16[128,1024]{1,0:T(8,128)(2,1)S(1)}, u32[]{:S(2)}, u32[]{:S(2)}) collective-permute-start(bf16[128,1024]{1,0:T(8,128)(2,1)S(1)} %slice.35), channel_id=1, source_target_pairs={{2,0},{3,1},{4,2},{5,3},{6,4},{7,5},{0,6},{1,7},{10,8},{11,9},{12,... | collective-permute-start | bytes 786440 | tf_op jit(solution)/shard_map/ppermute | solution.py:49
  83.8 6.6 %collective-permute-start.9 = (bf16[128,1024]{1,0:T(8,128)(2,1)S(1)}, bf16[128,1024]{1,0:T(8,128)(2,1)S(1)}, u32[]{:S(2)}, u32[]{:S(2)}) collective-permute-start(bf16[128,1024]{1,0:T(8,128)(2,1)S(1)} %get-tuple-element.25), channel_id=1, source_target_pairs={{64,0},{128,64},{192,128},{256,192},{320,256},{384,320},{448,384},... | collective-permute-start | bytes 786440 | tf_op jit(solution)/shard_map/ppermute | solution.py:58
  87.0 7.9 %collective-permute-start.12 = (bf16[128,1024]{1,0:T(8,128)(2,1)S(1)}, bf16[128,1024]{1,0:T(8,128)(2,1)S(1)}, u32[]{:S(2)}, u32[]{:S(2)}) collective-permute-start(bf16[128,1024]{1,0:T(8,128)(2,1)S(1)} %backward_half.4.refs_4_), channel_id=1, source_target_pairs={{64,0},{128,64},{192,128},{256,192},{320,256},{384,320},{448,384},... | collective-permute-start | bytes 786440 | tf_op jit(solution)/shard_map/ppermute | solution.py:58
  91.8 7.5 %collective-permute-start.10 = (bf16[128,1024]{1,0:T(8,128)(2,1)S(1)}, bf16[128,1024]{1,0:T(8,128)(2,1)S(1)}, u32[]{:S(2)}, u32[]{:S(2)}) collective-permute-start(bf16[128,1024]{1,0:T(8,128)(2,1)S(1)} %get-tuple-element.27), channel_id=1, source_target_pairs={{64,0},{128,64},{192,128},{256,192},{320,256},{384,320},{448,384},... | collective-permute-start | bytes 786440 | tf_op jit(solution)/shard_map/ppermute | solution.py:58
  96.1 7.9 %collective-permute-start.13 = (bf16[128,1024]{1,0:T(8,128)(2,1)S(1)}, bf16[128,1024]{1,0:T(8,128)(2,1)S(1)}, u32[]{:S(2)}, u32[]{:S(2)}) collective-permute-start(bf16[128,1024]{1,0:T(8,128)(2,1)S(1)} %backward_half.5.refs_5_), channel_id=1, source_target_pairs={{64,0},{128,64},{192,128},{256,192},{320,256},{384,320},{448,384},... | collective-permute-start | bytes 786440 | tf_op jit(solution)/shard_map/ppermute | solution.py:58
  100.8 7.5 %collective-permute-start.11 = (bf16[128,1024]{1,0:T(8,128)(2,1)S(1)}, bf16[128,1024]{1,0:T(8,128)(2,1)S(1)}, u32[]{:S(2)}, u32[]{:S(2)}) collective-permute-start(bf16[128,1024]{1,0:T(8,128)(2,1)S(1)} %get-tuple-element.29), channel_id=1, source_target_pairs={{64,0},{128,64},{192,128},{256,192},{320,256},{384,320},{448,384},... | collective-permute-start | bytes 786440 | tf_op jit(solution)/shard_map/ppermute | solution.py:58
  105.3 6.9 %collective-permute-start.14 = (bf16[128,1024]{1,0:T(8,128)(2,1)S(1)}, bf16[128,1024]{1,0:T(8,128)(2,1)S(1)}, u32[]{:S(2)}, u32[]{:S(2)}) collective-permute-start(bf16[128,1024]{1,0:T(8,128)(2,1)S(1)} %backward_half.6.refs_6_), channel_id=1, source_target_pairs={{64,0},{128,64},{192,128},{256,192},{320,256},{384,320},{448,384},... | collective-permute-start | bytes 786440 | tf_op jit(solution)/shard_map/ppermute | solution.py:58
  112.6 28.4 %collective-permute-start.15 = (bf16[512,512]{1,0:T(8,128)(2,1)S(1)}, bf16[512,512]{1,0:T(8,128)(2,1)S(1)}, u32[]{:S(2)}, u32[]{:S(2)}) collective-permute-start(bf16[512,512]{1,0:T(8,128)(2,1)S(1)} %outer_rows.5), channel_id=1, source_target_pairs={{2,0},{3,1},{4,2},{5,3},{6,4},{7,5},{0,6},{1,7},{10,8},{11,9},{12,... | collective-permute-start | bytes 1572872 | tf_op jit(solution)/shard_map/ppermute | solution.py:49
  118.0 28.9 %collective-permute-start.16 = (bf16[512,512]{1,0:T(8,128)(2,1)S(1)}, bf16[512,512]{1,0:T(8,128)(2,1)S(1)}, u32[]{:S(2)}, u32[]{:S(2)}) collective-permute-start(bf16[512,512]{1,0:T(8,128)(2,1)S(1)} %outer_rows.6), channel_id=1, source_target_pairs={{6,0},{7,1},{0,2},{1,3},{2,4},{3,5},{4,6},{5,7},{14,8},{15,9},{8,1... | collective-permute-start | bytes 1572872 | tf_op jit(solution)/shard_map/ppermute | solution.py:49
  120.4 26.4 %collective-permute-start.17 = (bf16[512,512]{1,0:T(8,128)(2,1)S(1)}, bf16[512,512]{1,0:T(8,128)(2,1)S(1)}, u32[]{:S(2)}, u32[]{:S(2)}) collective-permute-start(bf16[512,512]{1,0:T(8,128)(2,1)S(1)} %outer_rows.7), channel_id=1, source_target_pairs={{4,0},{5,1},{6,2},{7,3},{0,4},{1,5},{2,6},{3,7},{12,8},{13,9},{14,... | collective-permute-start | bytes 1572872 | tf_op jit(solution)/shard_map/ppermute | solution.py:49
  125.3 22.7 %collective-permute-start.19 = (bf16[128,1024]{1,0:T(8,128)(2,1)S(1)}, bf16[128,1024]{1,0:T(8,128)(2,1)S(1)}, u32[]{:S(2)}, u32[]{:S(2)}) collective-permute-start(bf16[128,1024]{1,0:T(8,128)(2,1)S(1)} %backward_half.7), channel_id=1, source_target_pairs={{64,0},{128,64},{192,128},{256,192},{320,256},{384,320},{448,384},... | collective-permute-start | bytes 786440 | tf_op jit(solution)/shard_map/ppermute | solution.py:58
  128.3 19.7 %collective-permute-start.18 = (bf16[128,1024]{1,0:T(8,128)(2,1)S(1)}, bf16[128,1024]{1,0:T(8,128)(2,1)S(1)}, u32[]{:S(2)}, u32[]{:S(2)}) collective-permute-start(bf16[128,1024]{1,0:T(8,128)(2,1)S(1)} %get-tuple-element.34), channel_id=1, source_target_pairs={{64,0},{128,64},{192,128},{256,192},{320,256},{384,320},{448,384},... | collective-permute-start | bytes 786440 | tf_op jit(solution)/shard_map/ppermute | solution.py:58
  148.0 23.8 %all-to-all-start.2 = ((bf16[16,32,512]{2,1,0:T(8,128)(2,1)}), bf16[16,32,512]{2,1,0:T(8,128)(2,1)S(1)}, u32[]{:S(2)}, u32[]{:S(2)}) async-start(bf16[16,32,512]{2,1,0:T(8,128)(2,1)} %bitcast.13), calls=%async_computation.2 | async-start | bytes 1048576 | tf_op jit(solution)/shard_map/all_to_all | solution.py:53
  (2 other events, 13.3 us)

commit v4 on v3

--- a/solution.py
+++ b/solution.py
@@ -39,9 +39,9 @@
     ]
 
 
-def shifted(block, x_step, y_step=0):
+def swapped(block, peer_x=lambda x: x, peer_y=lambda y: y):
     route = [
-        (dp_index(z, (x + x_step) % x_size, (y + y_step) % pair_size), dp_index(z, x, y))
+        (dp_index(z, peer_x(x), peer_y(y)), dp_index(z, x, y))
         for z in range(z_size())
         for x in range(x_size)
         for y in range(pair_size)
@@ -49,6 +49,22 @@
     return lax.ppermute(block, "dp", route)
 
 
+def near_x(x):
+    return x ^ 1
+
+
+def next_x(x):
+    return (x + 1 if x % 2 else x - 1) % x_size
+
+
+def far_x(x):
+    return (x + 2) % x_size
+
+
+def other_y(y):
+    return 1 - y
+
+
 def exchanged(blocks, groups):
     return lax.all_to_all(blocks, "dp", 0, 0, axis_index_groups=groups, tiled=True)
 
@@ -64,10 +80,10 @@
 
 def gathered_along_x(block):
     rows = block.shape[0] // 2
-    left, right = shifted(block, -1), shifted(block, 1)
-    far_head = shifted(left[:rows], -1)
-    far_tail = shifted(right[rows:], 1)
-    return block, left, right, far_head, far_tail
+    near, following = swapped(block, near_x), swapped(block, next_x)
+    far_head = swapped(following[:rows], near_x)
+    far_tail = swapped(near[rows:], next_x)
+    return block, near, following, far_head, far_tail
 
 
 def forward_kernel(acts_ref, gain_ref, *refs):
@@ -139,6 +155,25 @@
     out_ref[...] = total.astype(out_ref.dtype)
 
 
+def combine_kernel(y_ref, own_ref, near_ref, next_ref, far_ref, out_ref):
+    units = out_ref.shape[2]
+    half_rows = own_ref.shape[0] // 2
+    for part in range(pair_size):
+        rows = pl.ds(part * half_rows, half_rows)
+        total = (
+            own_ref[rows, :].astype(jnp.float32)
+            + near_ref[rows, :].astype(jnp.float32)
+            + next_ref[rows, :].astype(jnp.float32)
+            + far_ref[rows, :].astype(jnp.float32)
+        ).astype(out_ref.dtype)
+        blocks = total.reshape(-1, units, total.shape[1])
+        for y in range(pair_size):
+
+            @pl.when(y_ref[0] == y)
+            def _():
+                out_ref[:, y if part == 0 else 1 - y] = blocks
+
+
 def spans(weight_refs):
     offset = 0
     for ref in weight_refs:
@@ -213,18 +248,35 @@
     )(*hiddens, *cotangents)
 
 
+def combined(y_hi, units, parts):
+    rows, half = parts[0].shape
+    return pl.pallas_call(
+        combine_kernel,
+        out_shape=jax.ShapeDtypeStruct(
+            (rows // (pair_size * units), pair_size, units, half), jnp.bfloat16
+        ),
+        in_specs=[pl.BlockSpec(memory_space=pltpu.SMEM)] + in_vmem(len(parts)),
+        out_specs=in_vmem(1)[0],
+        cost_estimate=pl.CostEstimate(
+            flops=4 * rows * half, bytes_accessed=10 * rows * half, transcendentals=0
+        ),
+        compiler_params=kernel_params(),
+        name="combine_parts",
+    )(y_hi, *parts)
+
+
 def local(acts, grads, in_proj, out_proj, gain):
     half = acts.shape[2] // 2
     tick_count = min(4, lax.axis_size("section") // 2)
-    is_low = (lax.axis_index("dp") & (pair_size - 1)) == 0
+    y_hi = (lax.axis_index("dp") & (pair_size - 1)).reshape(1)
     shard = jnp.concatenate([in_proj[0], out_proj[0]], axis=1)
-    shard, is_low = lax.optimization_barrier((shard, is_low))
-    partner_shard = shifted(shard, 0, 1)
+    shard, y_hi = lax.optimization_barrier((shard, y_hi))
+    partner_shard = swapped(shard, peer_y=other_y)
     near = gathered_along_x(gathered_along_z(shard))
     far = gathered_along_x(gathered_along_z(partner_shard))
-    own_n, left_n, right_n, head_n, tail_n = near
-    own_f, left_f, right_f, head_f, tail_f = far
-    weights = (own_n, own_f, left_n, left_f, right_n, right_f, head_n, tail_n, head_f, tail_f)
+    own_n, near_n, next_n, head_n, tail_n = near
+    own_f, near_f, next_f, head_f, tail_f = far
+    weights = (own_n, own_f, near_n, near_f, next_n, next_f, head_n, tail_n, head_f, tail_f)
     quarter = own_n.shape[0] * 2
 
     acts_pair, grads_pair, scale = acts[0], grads[0], 1.0
@@ -239,9 +291,9 @@
             parts = [
                 outer_rows(hiddens, cotangents, columns, i * quarter, quarter) for i in (3, 1, 2)
             ]
-            far_x = shifted(parts[0], 2)
-            from_right = shifted(parts[1], 1)
-            from_left = shifted(parts[2], -1)
+            from_far = swapped(parts[0], far_x)
+            from_near = swapped(parts[1], near_x)
+            from_next = swapped(parts[2], next_x)
             acts_pair, grads_pair, _ = lax.optimization_barrier(
                 (acts_pair, grads_pair, parts)
             )
@@ -252,16 +304,8 @@
         acts_pair, grads_pair, scale = next_acts, passed_back(new_grads), coupling_scale
 
     own = outer_rows(hiddens, cotangents, columns, 0, quarter)
-    total = (
-        own.astype(jnp.float32)
-        + from_right.astype(jnp.float32)
-        + from_left.astype(jnp.float32)
-        + far_x.astype(jnp.float32)
-    ).astype(jnp.bfloat16)
-    mine, other = total[: quarter // 2], total[quarter // 2 :]
-    low, high = jnp.where(is_low, mine, other), jnp.where(is_low, other, mine)
     units = in_proj.shape[1]
-    blocks = jnp.stack([low.reshape(-1, units, half), high.reshape(-1, units, half)], axis=1)
+    blocks = combined(y_hi, units, (own, from_near, from_next, from_far))
     blocks, acts_pair, grads_pair = lax.optimization_barrier(
         (blocks.reshape(-1, half), acts_pair, grads_pair)
     )

time: 174 us -> 172 us (0.989)
  the two profiles are of different devices: /device:TPU:40 before, /device:TPU:16 now
where the time goes in v4:
time: 172 us; the launch traced here: 171 us
  starting transfers between devices  81.7 us (48%)
  waiting for transfers between devices  69.6 us (40%)
  Pallas kernels  13.9 us (8%)
  other arithmetic  3.22 us (2%)
  local copies, waits for them, and re-layouts  1.82 us (1%)
    ppermute x12, starting transfers between devices, swapped(): return lax.ppermute(block, 'dp', route)  40.3 us
    all_to_all x3, waiting for transfers between devices, exchanged(): lax.all_to_all(blocks, 'dp', 0, 0, axis_index_groups=groups, tiled=True)  36.5 us
    ppermute x12, waiting for transfers between devices, swapped(): return lax.ppermute(block, 'dp', route)  30.2 us
    ppermute x8, starting transfers between devices, passed_back(): return lax.ppermute(block, 'section', [(i, i - 1) for i in devices if i])  21.2 us
    all_to_all x3, starting transfers between devices, exchanged(): lax.all_to_all(blocks, 'dp', 0, 0, axis_index_groups=groups, tiled=True)  20.2 us
    pallas_call x4, Pallas kernels, forward(): pl.pallas_call(forward_kernel, out_shape=(jax.ShapeDtypeStruct((tokens, u...  5.7 us
    pallas_call x4, Pallas kernels, backward(): pl.pallas_call(functools.partial(backward_kernel, scale), out_shape=jax.S...  4.97 us
  transfers between devices with their start and end apart: 23, of which 14 were waited for; matrix products, arithmetic and copies ran while one was open for 1% of the time, Pallas kernels for 7%

profile of v4, /device:TPU:16, one launch (start us, length us, event | category | flops | bytes accessed | tf_op | source)
XLA Modules:
  0.0 171.2 jit_solution(479501272791727747)
XLA Ops:
  2.3 10.3 %all-to-all-start = ((bf16[8,32,1024]{2,1,0:T(8,128)(2,1)}), bf16[8,32,1024]{2,1,0:T(8,128)(2,1)S(1)}, u32[]{:S(2)}, u32[]{:S(2)}) async-start(bf16[8,32,1024]{2,1,0:T(8,128)(2,1)} %tile.4), calls=%async_computation | async-start | bytes 1048576 | tf_op jit(solution)/shard_map/all_to_all | solution.py:69
  12.6 5.9 %collective-permute-start = (bf16[32,1024]{1,0:T(8,128)(2,1)S(1)}, bf16[32,1024]{1,0:T(8,128)(2,1)S(1)}, u32[]{:S(2)}, u32[]{:S(2)}) collective-permute-start(bf16[32,1024]{1,0:T(8,128)(2,1)S(1)} %pad_maximum_fusion), channel_id=1, source_target_pairs={{1,0},{0,1},{3,2},{2,3},{5,4},{4,5},{7,6},{6,7},{9,8},{8,9},{11,10... | collective-permute-start | bytes 196616 | tf_op jit(solution)/shard_map/ppermute | solution.py:49
  18.5 4.9 %collective-permute-done = bf16[32,1024]{1,0:T(8,128)(2,1)S(1)} collective-permute-done((bf16[32,1024]{1,0:T(8,128)(2,1)S(1)}, bf16[32,1024]{1,0:T(8,128)(2,1)S(1)}, u32[]{:S(2)}, u32[]{:S(2)}) %collective-permute-start) | collective-permute-done | bytes 65568 | tf_op jit(solution)/shard_map/ppermute | solution.py:49
  23.4 6.7 %all-to-all-done = bf16[8,32,1024]{2,1,0:T(8,128)(2,1)S(1)} async-done(((bf16[8,32,1024]{2,1,0:T(8,128)(2,1)}), bf16[8,32,1024]{2,1,0:T(8,128)(2,1)S(1)}, u32[]{:S(2)}, u32[]{:S(2)}) %all-to-all-start) | async-done | bytes 524320 | tf_op jit(solution)/shard_map/all_to_all | solution.py:69
  30.9 3.5 %all-to-all-start.1 = ((bf16[8,32,1024]{2,1,0:T(8,128)(2,1)}), bf16[8,32,1024]{2,1,0:T(8,128)(2,1)S(1)}, u32[]{:S(2)}, u32[]{:S(2)}) async-start(bf16[8,32,1024]{2,1,0:T(8,128)(2,1)} %tile.5), calls=%async_computation.1 | async-start | bytes 1048576 | tf_op jit(solution)/shard_map/all_to_all | solution.py:69
  34.4 4.7 %collective-permute-start.3 = (bf16[256,1024]{1,0:T(8,128)(2,1)S(1)}, bf16[256,1024]{1,0:T(8,128)(2,1)S(1)}, u32[]{:S(2)}, u32[]{:S(2)}) collective-permute-start(bf16[256,1024]{1,0:T(8,128)(2,1)S(1)} %bitcast.15), channel_id=1, source_target_pairs={{6,0},{7,1},{4,2},{5,3},{2,4},{3,5},{0,6},{1,7},{14,8},{15,9},{12,... | collective-permute-start | bytes 1572872 | tf_op jit(solution)/shard_map/ppermute | solution.py:49
  41.3 11.1 %all-to-all-done.1 = bf16[8,32,1024]{2,1,0:T(8,128)(2,1)S(1)} async-done(((bf16[8,32,1024]{2,1,0:T(8,128)(2,1)}), bf16[8,32,1024]{2,1,0:T(8,128)(2,1)S(1)}, u32[]{:S(2)}, u32[]{:S(2)}) %all-to-all-start.1) | async-done | bytes 524320 | tf_op jit(solution)/shard_map/all_to_all | solution.py:69
  52.3 4.7 %collective-permute-start.4 = (bf16[256,1024]{1,0:T(8,128)(2,1)S(1)}, bf16[256,1024]{1,0:T(8,128)(2,1)S(1)}, u32[]{:S(2)}, u32[]{:S(2)}) collective-permute-start(bf16[256,1024]{1,0:T(8,128)(2,1)S(1)} %bitcast.25), channel_id=1, source_target_pairs={{6,0},{7,1},{4,2},{5,3},{2,4},{3,5},{0,6},{1,7},{14,8},{15,9},{12,... | collective-permute-start | bytes 1572872 | tf_op jit(solution)/shard_map/ppermute | solution.py:49
  59.1 3.7 %collective-permute-start.5 = (bf16[128,1024]{1,0:T(8,128)(2,1)S(1)}, bf16[128,1024]{1,0:T(8,128)(2,1)S(1)}, u32[]{:S(2)}, u32[]{:S(2)}) collective-permute-start(bf16[128,1024]{1,0:T(8,128)(2,1)S(1)} %slice.24), channel_id=1, source_target_pairs={{2,0},{3,1},{0,2},{1,3},{6,4},{7,5},{4,6},{5,7},{10,8},{11,9},{8,1... | collective-permute-start | bytes 786440 | tf_op jit(solution)/shard_map/ppermute | solution.py:49
  62.9 2.5 %collective-permute-start.6 = (bf16[128,1024]{1,0:T(8,128)(2,1)S(1)}, bf16[128,1024]{1,0:T(8,128)(2,1)S(1)}, u32[]{:S(2)}, u32[]{:S(2)}) collective-permute-start(bf16[128,1024]{1,0:T(8,128)(2,1)S(1)} %slice.25), channel_id=1, source_target_pairs={{6,0},{7,1},{4,2},{5,3},{2,4},{3,5},{0,6},{1,7},{14,8},{15,9},{12,... | collective-permute-start | bytes 786440 | tf_op jit(solution)/shard_map/ppermute | solution.py:49
  65.4 4.8 %collective-permute-done.4.refs_5_ = bf16[256,1024]{1,0:T(8,128)(2,1)S(1)} collective-permute-done((bf16[256,1024]{1,0:T(8,128)(2,1)S(1)}, bf16[256,1024]{1,0:T(8,128)(2,1)S(1)}, u32[]{:S(2)}, u32[]{:S(2)}) %collective-permute-start.4) | collective-permute-done | bytes 524320 | tf_op jit(solution)/shard_map/ppermute | solution.py:49
  73.7 3.2 %collective-permute-start.8 = (bf16[128,1024]{1,0:T(8,128)(2,1)S(1)}, bf16[128,1024]{1,0:T(8,128)(2,1)S(1)}, u32[]{:S(2)}, u32[]{:S(2)}) collective-permute-start(bf16[128,1024]{1,0:T(8,128)(2,1)S(1)} %slice.27), channel_id=1, source_target_pairs={{6,0},{7,1},{4,2},{5,3},{2,4},{3,5},{0,6},{1,7},{14,8},{15,9},{12,... | collective-permute-start | bytes 786440 | tf_op jit(solution)/shard_map/ppermute | solution.py:49
  76.9 2.4 %collective-permute-done.5.refs_6_ = bf16[128,1024]{1,0:T(8,128)(2,1)S(1)} collective-permute-done((bf16[128,1024]{1,0:T(8,128)(2,1)S(1)}, bf16[128,1024]{1,0:T(8,128)(2,1)S(1)}, u32[]{:S(2)}, u32[]{:S(2)}) %collective-permute-start.5) | collective-permute-done | bytes 262176 | tf_op jit(solution)/shard_map/ppermute | solution.py:49
  79.3 4.4 %collective-permute-done.7.refs_8_ = bf16[128,1024]{1,0:T(8,128)(2,1)S(1)} collective-permute-done((bf16[128,1024]{1,0:T(8,128)(2,1)S(1)}, bf16[128,1024]{1,0:T(8,128)(2,1)S(1)}, u32[]{:S(2)}, u32[]{:S(2)}) %collective-permute-start.7) | collective-permute-done | bytes 262176 | tf_op jit(solution)/shard_map/ppermute | solution.py:49
  88.3 2.4 %collective-permute-start.12 = (bf16[128,1024]{1,0:T(8,128)(2,1)S(1)}, bf16[128,1024]{1,0:T(8,128)(2,1)S(1)}, u32[]{:S(2)}, u32[]{:S(2)}) collective-permute-start(bf16[128,1024]{1,0:T(8,128)(2,1)S(1)} %backward_half.4.refs_4_), channel_id=1, source_target_pairs={{64,0},{128,64},{192,128},{256,192},{320,256},{384,320},{448,384},... | collective-permute-start | bytes 786440 | tf_op jit(solution)/shard_map/ppermute | solution.py:74
  92.4 3.8 %collective-permute-start.10 = (bf16[128,1024]{1,0:T(8,128)(2,1)S(1)}, bf16[128,1024]{1,0:T(8,128)(2,1)S(1)}, u32[]{:S(2)}, u32[]{:S(2)}) collective-permute-start(bf16[128,1024]{1,0:T(8,128)(2,1)S(1)} %get-tuple-element.27), channel_id=1, source_target_pairs={{64,0},{128,64},{192,128},{256,192},{320,256},{384,320},{448,384},... | collective-permute-start | bytes 786440 | tf_op jit(solution)/shard_map/ppermute | solution.py:74
  101.5 3.8 %collective-permute-start.11 = (bf16[128,1024]{1,0:T(8,128)(2,1)S(1)}, bf16[128,1024]{1,0:T(8,128)(2,1)S(1)}, u32[]{:S(2)}, u32[]{:S(2)}) collective-permute-start(bf16[128,1024]{1,0:T(8,128)(2,1)S(1)} %get-tuple-element.29), channel_id=1, source_target_pairs={{64,0},{128,64},{192,128},{256,192},{320,256},{384,320},{448,384},... | collective-permute-start | bytes 786440 | tf_op jit(solution)/shard_map/ppermute | solution.py:74
  113.0 2.9 %collective-permute-start.17 = (bf16[512,512]{1,0:T(8,128)(2,1)S(1)}, bf16[512,512]{1,0:T(8,128)(2,1)S(1)}, u32[]{:S(2)}, u32[]{:S(2)}) collective-permute-start(bf16[512,512]{1,0:T(8,128)(2,1)S(1)} %outer_rows.7), channel_id=1, source_target_pairs={{4,0},{5,1},{6,2},{7,3},{0,4},{1,5},{2,6},{3,7},{12,8},{13,9},{14,... | collective-permute-start | bytes 1572872 | tf_op jit(solution)/shard_map/ppermute | solution.py:49
  116.4 3.9 %collective-permute-start.16 = (bf16[512,512]{1,0:T(8,128)(2,1)S(1)}, bf16[512,512]{1,0:T(8,128)(2,1)S(1)}, u32[]{:S(2)}, u32[]{:S(2)}) collective-permute-start(bf16[512,512]{1,0:T(8,128)(2,1)S(1)} %outer_rows.6), channel_id=1, source_target_pairs={{6,0},{7,1},{4,2},{5,3},{2,4},{3,5},{0,6},{1,7},{14,8},{15,9},{12,... | collective-permute-start | bytes 1572872 | tf_op jit(solution)/shard_map/ppermute | solution.py:49
  120.8 2.4 %collective-permute-start.15 = (bf16[512,512]{1,0:T(8,128)(2,1)S(1)}, bf16[512,512]{1,0:T(8,128)(2,1)S(1)}, u32[]{:S(2)}, u32[]{:S(2)}) collective-permute-start(bf16[512,512]{1,0:T(8,128)(2,1)S(1)} %outer_rows.5), channel_id=1, source_target_pairs={{2,0},{3,1},{0,2},{1,3},{6,4},{7,5},{4,6},{5,7},{10,8},{11,9},{8,1... | collective-permute-start | bytes 1572872 | tf_op jit(solution)/shard_map/ppermute | solution.py:49
  124.5 3.0 %collective-permute-start.19 = (bf16[128,1024]{1,0:T(8,128)(2,1)S(1)}, bf16[128,1024]{1,0:T(8,128)(2,1)S(1)}, u32[]{:S(2)}, u32[]{:S(2)}) collective-permute-start(bf16[128,1024]{1,0:T(8,128)(2,1)S(1)} %backward_half.7), channel_id=1, source_target_pairs={{64,0},{128,64},{192,128},{256,192},{320,256},{384,320},{448,384},... | collective-permute-start | bytes 786440 | tf_op jit(solution)/shard_map/ppermute | solution.py:74
  130.4 12.0 %collective-permute-done.16.next_ref = bf16[512,512]{1,0:T(8,128)(2,1)S(1)} collective-permute-done((bf16[512,512]{1,0:T(8,128)(2,1)S(1)}, bf16[512,512]{1,0:T(8,128)(2,1)S(1)}, u32[]{:S(2)}, u32[]{:S(2)}) %collective-permute-start.16) | collective-permute-done | bytes 524320 | tf_op jit(solution)/shard_map/ppermute | solution.py:49
  143.7 6.3 %all-to-all-start.2 = ((bf16[16,32,512]{2,1,0:T(8,128)(2,1)}), bf16[16,32,512]{2,1,0:T(8,128)(2,1)S(1)}, u32[]{:S(2)}, u32[]{:S(2)}) async-start(bf16[16,32,512]{2,1,0:T(8,128)(2,1)} %bitcast.10), calls=%async_computation.2 | async-start | bytes 1048576 | tf_op jit(solution)/shard_map/all_to_all | solution.py:69
  151.8 18.7 %all-to-all-done.2 = bf16[16,32,512]{2,1,0:T(8,128)(2,1)S(1)} async-done(((bf16[16,32,512]{2,1,0:T(8,128)(2,1)}), bf16[16,32,512]{2,1,0:T(8,128)(2,1)S(1)}, u32[]{:S(2)}, u32[]{:S(2)}) %all-to-all-start.2) | async-done | bytes 524320 | tf_op jit(solution)/shard_map/all_to_all | solution.py:69
  (54 shorter events, 38.3 us)
Async XLA Ops:
  2.3 27.8 %all-to-all-start = ((bf16[8,32,1024]{2,1,0:T(8,128)(2,1)}), bf16[8,32,1024]{2,1,0:T(8,128)(2,1)S(1)}, u32[]{:S(2)}, u32[]{:S(2)}) async-start(bf16[8,32,1024]{2,1,0:T(8,128)(2,1)} %tile.4), calls=%async_computation | async-start | bytes 1048576 | tf_op jit(solution)/shard_map/all_to_all | solution.py:69
  12.6 10.8 %collective-permute-start = (bf16[32,1024]{1,0:T(8,128)(2,1)S(1)}, bf16[32,1024]{1,0:T(8,128)(2,1)S(1)}, u32[]{:S(2)}, u32[]{:S(2)}) collective-permute-start(bf16[32,1024]{1,0:T(8,128)(2,1)S(1)} %pad_maximum_fusion), channel_id=1, source_target_pairs={{1,0},{0,1},{3,2},{2,3},{5,4},{4,5},{7,6},{6,7},{9,8},{8,9},{11,10... | collective-permute-start | bytes 196616 | tf_op jit(solution)/shard_map/ppermute | solution.py:49
  30.9 21.4 %all-to-all-start.1 = ((bf16[8,32,1024]{2,1,0:T(8,128)(2,1)}), bf16[8,32,1024]{2,1,0:T(8,128)(2,1)S(1)}, u32[]{:S(2)}, u32[]{:S(2)}) async-start(bf16[8,32,1024]{2,1,0:T(8,128)(2,1)} %tile.5), calls=%async_computation.1 | async-start | bytes 1048576 | tf_op jit(solution)/shard_map/all_to_all | solution.py:69
  34.4 24.7 %collective-permute-start.3 = (bf16[256,1024]{1,0:T(8,128)(2,1)S(1)}, bf16[256,1024]{1,0:T(8,128)(2,1)S(1)}, u32[]{:S(2)}, u32[]{:S(2)}) collective-permute-start(bf16[256,1024]{1,0:T(8,128)(2,1)S(1)} %bitcast.15), channel_id=1, source_target_pairs={{6,0},{7,1},{4,2},{5,3},{2,4},{3,5},{0,6},{1,7},{14,8},{15,9},{12,... | collective-permute-start | bytes 1572872 | tf_op jit(solution)/shard_map/ppermute | solution.py:49
  39.1 23.8 %collective-permute-start.1 = (bf16[256,1024]{1,0:T(8,128)(2,1)S(1)}, bf16[256,1024]{1,0:T(8,128)(2,1)S(1)}, u32[]{:S(2)}, u32[]{:S(2)}) collective-permute-start(bf16[256,1024]{1,0:T(8,128)(2,1)S(1)} %bitcast.16), channel_id=1, source_target_pairs={{2,0},{3,1},{0,2},{1,3},{6,4},{7,5},{4,6},{5,7},{10,8},{11,9},{8,1... | collective-permute-start | bytes 1572872 | tf_op jit(solution)/shard_map/ppermute | solution.py:49
  52.3 17.9 %collective-permute-start.4 = (bf16[256,1024]{1,0:T(8,128)(2,1)S(1)}, bf16[256,1024]{1,0:T(8,128)(2,1)S(1)}, u32[]{:S(2)}, u32[]{:S(2)}) collective-permute-start(bf16[256,1024]{1,0:T(8,128)(2,1)S(1)} %bitcast.25), channel_id=1, source_target_pairs={{6,0},{7,1},{4,2},{5,3},{2,4},{3,5},{0,6},{1,7},{14,8},{15,9},{12,... | collective-permute-start | bytes 1572872 | tf_op jit(solution)/shard_map/ppermute | solution.py:49
  57.0 16.7 %collective-permute-start.2 = (bf16[256,1024]{1,0:T(8,128)(2,1)S(1)}, bf16[256,1024]{1,0:T(8,128)(2,1)S(1)}, u32[]{:S(2)}, u32[]{:S(2)}) collective-permute-start(bf16[256,1024]{1,0:T(8,128)(2,1)S(1)} %bitcast.26), channel_id=1, source_target_pairs={{2,0},{3,1},{0,2},{1,3},{6,4},{7,5},{4,6},{5,7},{10,8},{11,9},{8,1... | collective-permute-start | bytes 1572872 | tf_op jit(solution)/shard_map/ppermute | solution.py:49
  59.1 20.1 %collective-permute-start.5 = (bf16[128,1024]{1,0:T(8,128)(2,1)S(1)}, bf16[128,1024]{1,0:T(8,128)(2,1)S(1)}, u32[]{:S(2)}, u32[]{:S(2)}) collective-permute-start(bf16[128,1024]{1,0:T(8,128)(2,1)S(1)} %slice.24), channel_id=1, source_target_pairs={{2,0},{3,1},{0,2},{1,3},{6,4},{7,5},{4,6},{5,7},{10,8},{11,9},{8,1... | collective-permute-start | bytes 786440 | tf_op jit(solution)/shard_map/ppermute | solution.py:49
  62.9 20.8 %copy-start = (f32[1,128,1024]{2,1,0:T(8,128)S(1)}, f32[1,128,1024]{2,1,0:T(8,128)}, u32[]{:S(2)}) copy-start(f32[1,128,1024]{2,1,0:T(8,128)} %param.5) | copy-start | bytes 1572868
  62.9 16.4 %collective-permute-start.6 = (bf16[128,1024]{1,0:T(8,128)(2,1)S(1)}, bf16[128,1024]{1,0:T(8,128)(2,1)S(1)}, u32[]{:S(2)}, u32[]{:S(2)}) collective-permute-start(bf16[128,1024]{1,0:T(8,128)(2,1)S(1)} %slice.25), channel_id=1, source_target_pairs={{6,0},{7,1},{4,2},{5,3},{2,4},{3,5},{0,6},{1,7},{14,8},{15,9},{12,... | collective-permute-start | bytes 786440 | tf_op jit(solution)/shard_map/ppermute | solution.py:49
  70.2 13.5 %collective-permute-start.7 = (bf16[128,1024]{1,0:T(8,128)(2,1)S(1)}, bf16[128,1024]{1,0:T(8,128)(2,1)S(1)}, u32[]{:S(2)}, u32[]{:S(2)}) collective-permute-start(bf16[128,1024]{1,0:T(8,128)(2,1)S(1)} %slice.26), channel_id=1, source_target_pairs={{2,0},{3,1},{0,2},{1,3},{6,4},{7,5},{4,6},{5,7},{10,8},{11,9},{8,1... | collective-permute-start | bytes 786440 | tf_op jit(solution)/shard_map/ppermute | solution.py:49
  73.7 10.0 %collective-permute-start.8 = (bf16[128,1024]{1,0:T(8,128)(2,1)S(1)}, bf16[128,1024]{1,0:T(8,128)(2,1)S(1)}, u32[]{:S(2)}, u32[]{:S(2)}) collective-permute-start(bf16[128,1024]{1,0:T(8,128)(2,1)S(1)} %slice.27), channel_id=1, source_target_pairs={{6,0},{7,1},{4,2},{5,3},{2,4},{3,5},{0,6},{1,7},{14,8},{15,9},{12,... | collective-permute-start | bytes 786440 | tf_op jit(solution)/shard_map/ppermute | solution.py:49
  85.1 5.8 %collective-permute-start.9 = (bf16[128,1024]{1,0:T(8,128)(2,1)S(1)}, bf16[128,1024]{1,0:T(8,128)(2,1)S(1)}, u32[]{:S(2)}, u32[]{:S(2)}) collective-permute-start(bf16[128,1024]{1,0:T(8,128)(2,1)S(1)} %get-tuple-element.25), channel_id=1, source_target_pairs={{64,0},{128,64},{192,128},{256,192},{320,256},{384,320},{448,384},... | collective-permute-start | bytes 786440 | tf_op jit(solution)/shard_map/ppermute | solution.py:74
  88.3 7.9 %collective-permute-start.12 = (bf16[128,1024]{1,0:T(8,128)(2,1)S(1)}, bf16[128,1024]{1,0:T(8,128)(2,1)S(1)}, u32[]{:S(2)}, u32[]{:S(2)}) collective-permute-start(bf16[128,1024]{1,0:T(8,128)(2,1)S(1)} %backward_half.4.refs_4_), channel_id=1, source_target_pairs={{64,0},{128,64},{192,128},{256,192},{320,256},{384,320},{448,384},... | collective-permute-start | bytes 786440 | tf_op jit(solution)/shard_map/ppermute | solution.py:74
  92.4 7.7 %collective-permute-start.10 = (bf16[128,1024]{1,0:T(8,128)(2,1)S(1)}, bf16[128,1024]{1,0:T(8,128)(2,1)S(1)}, u32[]{:S(2)}, u32[]{:S(2)}) collective-permute-start(bf16[128,1024]{1,0:T(8,128)(2,1)S(1)} %get-tuple-element.27), channel_id=1, source_target_pairs={{64,0},{128,64},{192,128},{256,192},{320,256},{384,320},{448,384},... | collective-permute-start | bytes 786440 | tf_op jit(solution)/shard_map/ppermute | solution.py:74
  97.4 7.9 %collective-permute-start.13 = (bf16[128,1024]{1,0:T(8,128)(2,1)S(1)}, bf16[128,1024]{1,0:T(8,128)(2,1)S(1)}, u32[]{:S(2)}, u32[]{:S(2)}) collective-permute-start(bf16[128,1024]{1,0:T(8,128)(2,1)S(1)} %backward_half.5.refs_5_), channel_id=1, source_target_pairs={{64,0},{128,64},{192,128},{256,192},{320,256},{384,320},{448,384},... | collective-permute-start | bytes 786440 | tf_op jit(solution)/shard_map/ppermute | solution.py:74
  101.5 7.7 %collective-permute-start.11 = (bf16[128,1024]{1,0:T(8,128)(2,1)S(1)}, bf16[128,1024]{1,0:T(8,128)(2,1)S(1)}, u32[]{:S(2)}, u32[]{:S(2)}) collective-permute-start(bf16[128,1024]{1,0:T(8,128)(2,1)S(1)} %get-tuple-element.29), channel_id=1, source_target_pairs={{64,0},{128,64},{192,128},{256,192},{320,256},{384,320},{448,384},... | collective-permute-start | bytes 786440 | tf_op jit(solution)/shard_map/ppermute | solution.py:74
  106.6 6.0 %collective-permute-start.14 = (bf16[128,1024]{1,0:T(8,128)(2,1)S(1)}, bf16[128,1024]{1,0:T(8,128)(2,1)S(1)}, u32[]{:S(2)}, u32[]{:S(2)}) collective-permute-start(bf16[128,1024]{1,0:T(8,128)(2,1)S(1)} %backward_half.6.refs_6_), channel_id=1, source_target_pairs={{64,0},{128,64},{192,128},{256,192},{320,256},{384,320},{448,384},... | collective-permute-start | bytes 786440 | tf_op jit(solution)/shard_map/ppermute | solution.py:74
  113.0 17.4 %collective-permute-start.17 = (bf16[512,512]{1,0:T(8,128)(2,1)S(1)}, bf16[512,512]{1,0:T(8,128)(2,1)S(1)}, u32[]{:S(2)}, u32[]{:S(2)}) collective-permute-start(bf16[512,512]{1,0:T(8,128)(2,1)S(1)} %outer_rows.7), channel_id=1, source_target_pairs={{4,0},{5,1},{6,2},{7,3},{0,4},{1,5},{2,6},{3,7},{12,8},{13,9},{14,... | collective-permute-start | bytes 1572872 | tf_op jit(solution)/shard_map/ppermute | solution.py:49
  116.4 26.0 %collective-permute-start.16 = (bf16[512,512]{1,0:T(8,128)(2,1)S(1)}, bf16[512,512]{1,0:T(8,128)(2,1)S(1)}, u32[]{:S(2)}, u32[]{:S(2)}) collective-permute-start(bf16[512,512]{1,0:T(8,128)(2,1)S(1)} %outer_rows.6), channel_id=1, source_target_pairs={{6,0},{7,1},{4,2},{5,3},{2,4},{3,5},{0,6},{1,7},{14,8},{15,9},{12,... | collective-permute-start | bytes 1572872 | tf_op jit(solution)/shard_map/ppermute | solution.py:49
  120.8 21.6 %collective-permute-start.15 = (bf16[512,512]{1,0:T(8,128)(2,1)S(1)}, bf16[512,512]{1,0:T(8,128)(2,1)S(1)}, u32[]{:S(2)}, u32[]{:S(2)}) collective-permute-start(bf16[512,512]{1,0:T(8,128)(2,1)S(1)} %outer_rows.5), channel_id=1, source_target_pairs={{2,0},{3,1},{0,2},{1,3},{6,4},{7,5},{4,6},{5,7},{10,8},{11,9},{8,1... | collective-permute-start | bytes 1572872 | tf_op jit(solution)/shard_map/ppermute | solution.py:49
  124.5 19.2 %collective-permute-start.19 = (bf16[128,1024]{1,0:T(8,128)(2,1)S(1)}, bf16[128,1024]{1,0:T(8,128)(2,1)S(1)}, u32[]{:S(2)}, u32[]{:S(2)}) collective-permute-start(bf16[128,1024]{1,0:T(8,128)(2,1)S(1)} %backward_half.7), channel_id=1, source_target_pairs={{64,0},{128,64},{192,128},{256,192},{320,256},{384,320},{448,384},... | collective-permute-start | bytes 786440 | tf_op jit(solution)/shard_map/ppermute | solution.py:74
  127.4 16.2 %collective-permute-start.18 = (bf16[128,1024]{1,0:T(8,128)(2,1)S(1)}, bf16[128,1024]{1,0:T(8,128)(2,1)S(1)}, u32[]{:S(2)}, u32[]{:S(2)}) collective-permute-start(bf16[128,1024]{1,0:T(8,128)(2,1)S(1)} %get-tuple-element.34), channel_id=1, source_target_pairs={{64,0},{128,64},{192,128},{256,192},{320,256},{384,320},{448,384},... | collective-permute-start | bytes 786440 | tf_op jit(solution)/shard_map/ppermute | solution.py:74
  143.7 26.9 %all-to-all-start.2 = ((bf16[16,32,512]{2,1,0:T(8,128)(2,1)}), bf16[16,32,512]{2,1,0:T(8,128)(2,1)S(1)}, u32[]{:S(2)}, u32[]{:S(2)}) async-start(bf16[16,32,512]{2,1,0:T(8,128)(2,1)} %bitcast.10), calls=%async_computation.2 | async-start | bytes 1048576 | tf_op jit(solution)/shard_map/all_to_all | solution.py:69
  (2 other events, 13.4 us)

commit v5 on v3

v5 whole, which is shorter than its diff:
```python
import functools

import jax
import jax.numpy as jnp
from jax import lax
from jax.experimental import pallas as pl
from jax.experimental.pallas import tpu as pltpu
from jax.sharding import PartitionSpec as P

coupling_scale = 32.0**0.25
rms_epsilon = 1e-06
root_half = 0.7071067811865476
inv_root_two_pi = 0.3989422804014327

x_size = 4
pair_size = 2


def dp_index(z, x, y):
    return (z * x_size + x) * pair_size + y


def z_size():
    return lax.axis_size("dp") // (x_size * pair_size)


def alike_groups():
    return [
        [
            dp_index(z, x, y)
            for z in range(parity, z_size(), 2)
            for y in range(pair_size)
        ]
        for parity in range(2)
        for x in range(x_size)
    ]


def swapped_along_x(block, peer):
    route = [
        (dp_index(z, peer(x), y), dp_index(z, x, y))
        for z in range(z_size())
        for x in range(x_size)
        for y in range(pair_size)
    ]
    return lax.ppermute(block, "dp", route)


def partner(index):
    return index ^ (x_size * pair_size)


def swapped_with_partner(block):
    return lax.ppermute(block, "dp", [(partner(i), i) for i in range(lax.axis_size("dp"))])


def near_x(x):
    return x ^ 1


def next_x(x):
    return (x + 1 if x % 2 else x - 1) % x_size


def far_x(x):
    return (x + 2) % x_size


def exchanged(blocks):
    return lax.all_to_all(
        blocks, "dp", 0, 0, axis_index_groups=alike_groups(), tiled=True
    )


def passed_back(block):
    devices = range(lax.axis_size("section"))
    return lax.ppermute(block, "section", [(i, i - 1) for i in devices if i])


def passed_back_to_partner(block):
    size = lax.axis_size("dp")
    route = [
        (section * size + i, (section - 1) * size + partner(i))
        for section in range(1, lax.axis_size("section"))
        for i in range(size)
    ]
    return lax.ppermute(block, ("section", "dp"), route)


def gathered_along_x(block):
    rows = block.shape[0] // 2
    near, following = swapped_along_x(block, near_x), swapped_along_x(block, next_x)
    far_head = swapped_along_x(following[:rows], near_x)
    far_tail = swapped_along_x(near[rows:], next_x)
    return block, near, following, far_head, far_tail


def inverse_rms(first):
    return lax.rsqrt(jnp.mean(first * first, axis=-1, keepdims=True) + rms_epsilon)


def forward_kernel(acts_ref, partner_ref, gain_ref, *refs):
    weight_refs, (hidden_ref, slopes_ref, kept_ref, sent_ref) = refs[:-4], refs[-4:]
    tokens, half = partner_ref.shape
    first = jnp.concatenate(
        [acts_ref[:, :half].astype(jnp.float32), partner_ref[...].astype(jnp.float32)], axis=0
    )
    normed = (first * inverse_rms(first) * gain_ref[...]).astype(jnp.bfloat16)
    for span, weight_ref in spans(weight_refs):
        preact = lax.dot_general(
            normed,
            weight_ref[:, :half],
            (((1,), (1,)), ((), ())),
            preferred_element_type=jnp.float32,
        )
        normal_cdf = 0.5 * (1.0 + lax.erf(preact * root_half))
        density = jnp.exp(-0.5 * preact * preact) * inv_root_two_pi
        hidden_ref[:, span] = (preact * normal_cdf).astype(jnp.bfloat16)
        slopes_ref[:, span] = (normal_cdf + preact * density).astype(slopes_ref.dtype)
    branch = sum(
        jnp.dot(hidden_ref[:, span], weight_ref[:, half:], preferred_element_type=jnp.float32)
        for span, weight_ref in spans(weight_refs)
    )
    kept_ref[...] = branch[:tokens]
    sent_ref[...] = branch[tokens:].astype(sent_ref.dtype)


def acts_kernel(acts_ref, kept_ref, received_ref, acts_out_ref, first_out_ref):
    half = kept_ref.shape[1]
    branch = kept_ref[...] + received_ref[...].astype(jnp.float32)
    second = acts_ref[:, half:].astype(jnp.float32)
    new_first = ((second - branch) / coupling_scale).astype(jnp.bfloat16)
    acts_out_ref[:, :half] = new_first
    acts_out_ref[:, half:] = acts_ref[:, :half].astype(jnp.bfloat16)
    first_out_ref[...] = new_first


def backward_kernel(grads_ref, partner_ref, slopes_ref, *refs):
    weight_refs, (kept_ref, sent_ref, pre_grad) = refs[:-3], refs[-3:]
    tokens, half = partner_ref.shape
    cotangent = jnp.concatenate(
        [grads_ref[:, half:].astype(jnp.bfloat16), partner_ref[...].astype(jnp.bfloat16)], axis=0
    )
    for span, weight_ref in spans(weight_refs):
        hidden_grad = lax.dot_general(
            cotangent,
            weight_ref[:, half:],
            (((1,), (1,)), ((), ())),
            preferred_element_type=jnp.float32,
        )
        slopes = slopes_ref[:, span].astype(jnp.float32)
        pre_grad[:, span] = (hidden_grad * slopes).astype(jnp.bfloat16)
    norm_grad = sum(
        jnp.dot(pre_grad[:, span], weight_ref[:, :half], preferred_element_type=jnp.float32)
        for span, weight_ref in spans(weight_refs)
    )
    kept_ref[...] = norm_grad[:tokens]
    sent_ref[...] = norm_grad[tokens:].astype(sent_ref.dtype)


def grads_kernel(
    scale, acts_ref, grads_ref, gain_ref, kept_ref, received_ref, grads_out_ref, second_out_ref
):
    half = kept_ref.shape[1]
    first = acts_ref[:, :half].astype(jnp.float32)
    inv_rms = inverse_rms(first)
    scaled = (kept_ref[...] + received_ref[...].astype(jnp.float32)) * gain_ref[...]
    inner = jnp.mean(first * scaled, axis=-1, keepdims=True)
    input_grad = inv_rms * scaled - first * (inv_rms * inv_rms * inv_rms) * inner
    first_grad = grads_ref[:, :half].astype(jnp.float32)
    if scale != 1.0:
        first_grad = first_grad * scale
    new_second = (first_grad + input_grad).astype(jnp.bfloat16)
    grads_out_ref[:, :half] = grads_ref[:, half:].astype(jnp.bfloat16)
    grads_out_ref[:, half:] = new_second
    second_out_ref[...] = new_second


def outer_kernel(start, columns, *refs):
    ticks = len(refs) // 3
    hidden_refs, cotangent_refs, out_ref = refs[:ticks], refs[ticks:-1], refs[-1]
    count, half = out_ref.shape
    rows = jnp.concatenate([ref[:, start : start + count] for ref in hidden_refs], axis=0)
    cotangents = jnp.concatenate(
        [ref[:, at : at + half] for ref, at in zip(cotangent_refs, columns)], axis=0
    )
    total = lax.dot_general(
        rows, cotangents, (((0,), (0,)), ((), ())), preferred_element_type=jnp.float32
    )
    out_ref[...] = total.astype(out_ref.dtype)


def spans(weight_refs):
    offset = 0
    for ref in weight_refs:
        yield pl.ds(offset, ref.shape[0]), ref
        offset += ref.shape[0]


def in_vmem(count):
    return [pl.BlockSpec(memory_space=pltpu.VMEM)] * count


def cost(tokens, units, half):
    return pl.CostEstimate(
        flops=4 * tokens * units * half,
        bytes_accessed=4 * units * half + 4 * tokens * units,
        transcendentals=2 * tokens * units,
    )


def kernel_params():
    return pltpu.CompilerParams(vmem_limit_bytes=16 * 2**20)


def call(kernel, name, cost_estimate, outs, operands, scratch=()):
    return pl.pallas_call(
        kernel,
        out_shape=tuple(jax.ShapeDtypeStruct(shape, dtype) for shape, dtype in outs),
        in_specs=in_vmem(len(operands)),
        out_specs=tuple(in_vmem(len(outs))),
        scratch_shapes=list(scratch),
        cost_estimate=cost_estimate,
        compiler_params=kernel_params(),
        name=name,
    )(*operands)


def forward(acts, partner_first, gain, weights):
    tokens, half = partner_first.shape
    units = sum(w.shape[0] for w in weights)
    return call(
        forward_kernel,
        "forward_half",
        cost(2 * tokens, units, half),
        (
            ((2 * tokens, units), jnp.bfloat16),
            ((2 * tokens, units), jnp.bfloat16),
            ((tokens, half), jnp.float32),
            ((tokens, half), jnp.bfloat16),
        ),
        (acts, partner_first, gain, *weights),
    )


def backward(grads, partner_cotangent, slopes, weights):
    tokens, half = partner_cotangent.shape
    units = slopes.shape[1]
    return call(
        backward_kernel,
        "backward_half",
        cost(2 * tokens, units, half),
        (((tokens, half), jnp.float32), ((tokens, half), jnp.bfloat16)),
        (grads, partner_cotangent, slopes, *weights),
        (pltpu.VMEM((2 * tokens, units), jnp.bfloat16),),
    )


def small_cost(tokens, half):
    return pl.CostEstimate(
        flops=16 * tokens * half, bytes_accessed=16 * tokens * half, transcendentals=0
    )


def new_acts_of(acts, kept, received):
    tokens, half = kept.shape
    return call(
        acts_kernel,
        "new_acts",
        small_cost(tokens, half),
        (((tokens, 2 * half), jnp.bfloat16), ((tokens, half), jnp.bfloat16)),
        (acts, kept, received),
    )


def new_grads_of(scale, acts, grads, gain, kept, received):
    tokens, half = kept.shape
    return call(
        functools.partial(grads_kernel, scale),
        "new_grads",
        small_cost(tokens, half),
        (((tokens, 2 * half), jnp.bfloat16), ((tokens, half), jnp.bfloat16)),
        (acts, grads, gain, kept, received),
    )


def outer_rows(hiddens, cotangents, columns, start, count, half):
    tokens = hiddens[0].shape[0] * len(hiddens)
    return call(
        functools.partial(outer_kernel, start, columns),
        "outer_rows",
        pl.CostEstimate(
            flops=2 * tokens * count * half,
            bytes_accessed=2 * (tokens * count + tokens * half + count * half),
            transcendentals=0,
        ),
        (((count, half), jnp.bfloat16),),
        (*hiddens, *cotangents),
    )[0]


def local(acts, grads, in_proj, out_proj, gain):
    half = acts.shape[2] // 2
    units = in_proj.shape[1]
    tick_count = min(4, lax.axis_size("section") // 2)
    shard = jnp.concatenate([in_proj[0], out_proj[0]], axis=1)
    group_size = len(alike_groups()[0])
    weights = gathered_along_x(exchanged(jnp.tile(shard, (group_size, 1))))
    quarter = group_size * units

    acts_pair, grads_pair, scale = acts[0], grads[0], 1.0
    partner_first = swapped_with_partner(acts_pair[:, :half])
    partner_cotangent = swapped_with_partner(grads_pair[:, half:].astype(jnp.bfloat16))
    hiddens, cotangents, columns = [], [], []
    for tick_index in range(tick_count):
        last = tick_index == tick_count - 1
        hidden, slopes, kept, sent = forward(acts_pair, partner_first, gain, weights)
        received = swapped_with_partner(sent)
        hiddens.append(hidden)
        if last:
            cotangents += [grads_pair, partner_cotangent]
            columns += [half, 0]
            parts = [
                outer_rows(hiddens, cotangents, columns, i * quarter, quarter, half)
                for i in (3, 1, 2)
            ]
            from_far = swapped_along_x(parts[0], far_x)
            from_near = swapped_along_x(parts[1], near_x)
            from_next = swapped_along_x(parts[2], next_x)
            acts_pair, grads_pair, _ = lax.optimization_barrier((acts_pair, grads_pair, parts))
        kept_grad, sent_grad = backward(grads_pair, partner_cotangent, slopes, weights)
        received_grad = swapped_with_partner(sent_grad)
        new_acts, new_first = new_acts_of(acts_pair, kept, received)
        next_acts = passed_back(new_acts)
        new_grads, new_second = new_grads_of(
            scale, acts_pair, grads_pair, gain, kept_grad, received_grad
        )
        next_grads = passed_back(new_grads)
        if not last:
            cotangents += [new_grads, partner_cotangent]
            columns += [0, 0]
            partner_first = passed_back_to_partner(new_first)
            partner_cotangent = passed_back_to_partner(new_second)
        acts_pair, grads_pair, scale = next_acts, next_grads, coupling_scale

    own = outer_rows(hiddens, cotangents, columns, 0, quarter, half)
    blocks = sum(x.astype(jnp.float32) for x in (own, from_near, from_next, from_far))
    blocks, acts_pair, grads_pair = lax.optimization_barrier(
        (blocks.astype(jnp.bfloat16), acts_pair, grads_pair)
    )
    parts = exchanged(blocks).reshape(-1, units, half)
    share = jnp.sum(parts.astype(jnp.float32), axis=0)

    grads_pair = grads_pair.astype(jnp.float32)
    grads_out = jnp.concatenate(
        [coupling_scale * grads_pair[:, :half], grads_pair[:, half:]], axis=1
    )
    return (acts_pair.astype(jnp.float32)[None], grads_out[None], share[None])


def solution(mesh):
    pair = P("section", "dp", None)
    return jax.shard_map(
        local,
        mesh=mesh,
        in_specs=(pair, pair, pair, pair, P("section", None)),
        out_specs=(pair, pair, pair),
        check_vma=False,
    )
```

time: 174 us -> 188 us (1.080)
  the two profiles are of different devices: /device:TPU:40 before, /device:TPU:16 now
where the time goes in v5:
time: 188 us; the launch traced here: 187 us
  starting transfers between devices  89.1 us (47%)
  waiting for transfers between devices  42.4 us (23%)
  blocking collectives  35.8 us (19%)
  Pallas kernels  14 us (7%)
  other arithmetic  4.02 us (2%)
    all_to_all x1, blocking collectives, exchanged(): lax.all_to_all(blocks, 'dp', 0, 0, axis_index_groups=alike_groups(), tile...  35.8 us
    ppermute x10, starting transfers between devices, swapped_with_partner(): lax.ppermute(block, 'dp', [(partner(i), i) for i in range(lax.axis_size('...  31.4 us
    ppermute x7, starting transfers between devices, swapped_along_x(): return lax.ppermute(block, 'dp', route)  20.7 us
    ppermute x6, starting transfers between devices, passed_back_to_partner(): return lax.ppermute(block, ('section', 'dp'), route)  17.3 us
    ppermute x8, starting transfers between devices, passed_back(): return lax.ppermute(block, 'section', [(i, i - 1) for i in devices if i])  16.3 us
    all_to_all x1, waiting for transfers between devices, exchanged(): lax.all_to_all(blocks, 'dp', 0, 0, axis_index_groups=alike_groups(), tile...  14.1 us
    pallas_call x20, Pallas kernels, call(): pl.pallas_call(kernel, out_shape=tuple((jax.ShapeDtypeStruct(shape, dtype...  14 us
    ppermute x7, waiting for transfers between devices, swapped_along_x(): return lax.ppermute(block, 'dp', route)  11.7 us
  transfers between devices with their start and end apart: 32, of which 14 were waited for; matrix products, arithmetic and copies ran while one was open for 1% of the time, Pallas kernels for 7%

profile of v5, /device:TPU:16, one launch (start us, length us, event | category | flops | bytes accessed | tf_op | source)
XLA Modules:
  0.0 186.7 jit_solution(1283045132769001806)
XLA Ops:
  1.5 35.8 %all_to_all.17 = bf16[8,32,1024]{2,1,0:T(8,128)(2,1)S(1)} all-to-all(bf16[8,32,1024]{2,1,0:T(8,128)(2,1)S(1)} %tile.2), channel_id=1, replica_groups={{0,1,16,17,32,33,48,49},{2,3,18,19,34,35,50,51},{4,5,20,21,36,37,52,53}..., dimensions={0} | all-to-all | bytes 1048576 | tf_op jit(solution)/shard_map/all_to_all | solution.py:70
  37.3 4.7 %collective-permute-start.2 = (bf16[256,1024]{1,0:T(8,128)(2,1)S(1)}, bf16[256,1024]{1,0:T(8,128)(2,1)S(1)}, u32[]{:S(2)}, u32[]{:S(2)}) collective-permute-start(bf16[256,1024]{1,0:T(8,128)(2,1)S(1)} %bitcast.12), channel_id=1, source_target_pairs={{6,0},{7,1},{4,2},{5,3},{2,4},{3,5},{0,6},{1,7},{14,8},{15,9},{12,... | collective-permute-start | bytes 1572872 | tf_op jit(solution)/shard_map/ppermute | solution.py:46
  44.1 3.3 %collective-permute-start = (f32[128,512]{1,0:T(8,128)S(1)}, f32[128,512]{1,0:T(8,128)S(1)}, u32[]{:S(2)}, u32[]{:S(2)}) collective-permute-start(f32[128,512]{1,0:T(8,128)S(1)} %slice.25), channel_id=1, source_target_pairs={{8,0},{9,1},{10,2},{11,3},{12,4},{13,5},{14,6},{15,7},{0,8},{1,9},... | collective-permute-start | bytes 786440 | tf_op jit(solution)/shard_map/ppermute | solution.py:54
  47.4 4.3 %collective-permute-done.2.refs_2_ = bf16[256,1024]{1,0:T(8,128)(2,1)S(1)} collective-permute-done((bf16[256,1024]{1,0:T(8,128)(2,1)S(1)}, bf16[256,1024]{1,0:T(8,128)(2,1)S(1)}, u32[]{:S(2)}, u32[]{:S(2)}) %collective-permute-start.2) | collective-permute-done | bytes 524320 | tf_op jit(solution)/shard_map/ppermute | solution.py:46
  53.9 3.0 %collective-permute-done.1.refs_1_ = bf16[256,1024]{1,0:T(8,128)(2,1)S(1)} collective-permute-done((bf16[256,1024]{1,0:T(8,128)(2,1)S(1)}, bf16[256,1024]{1,0:T(8,128)(2,1)S(1)}, u32[]{:S(2)}, u32[]{:S(2)}) %collective-permute-start.1) | collective-permute-done | bytes 524320 | tf_op jit(solution)/shard_map/ppermute | solution.py:46
  58.9 3.1 %collective-permute-start.14 = (bf16[128,512]{1,0:T(8,128)(2,1)S(1)}, bf16[128,512]{1,0:T(8,128)(2,1)S(1)}, u32[]{:S(2)}, u32[]{:S(2)}) collective-permute-start(bf16[128,512]{1,0:T(8,128)(2,1)S(1)} %slice.33), channel_id=1, source_target_pairs={{8,0},{9,1},{10,2},{11,3},{12,4},{13,5},{14,6},{15,7},{0,8},{1,9},... | collective-permute-start | bytes 393224 | tf_op jit(solution)/shard_map/ppermute | solution.py:54
  62.1 4.3 %collective-permute-done.4.refs_4_ = bf16[128,1024]{1,0:T(8,128)(2,1)S(1)} collective-permute-done((bf16[128,1024]{1,0:T(8,128)(2,1)S(1)}, bf16[128,1024]{1,0:T(8,128)(2,1)S(1)}, u32[]{:S(2)}, u32[]{:S(2)}) %collective-permute-start.4) | collective-permute-done | bytes 262176 | tf_op jit(solution)/shard_map/ppermute | solution.py:46
  67.7 3.1 %collective-permute-start.5 = (bf16[128,512]{1,0:T(8,128)(2,1)S(1)}, bf16[128,512]{1,0:T(8,128)(2,1)S(1)}, u32[]{:S(2)}, u32[]{:S(2)}) collective-permute-start(bf16[128,512]{1,0:T(8,128)(2,1)S(1)} %get-tuple-element.48), channel_id=1, source_target_pairs={{8,0},{9,1},{10,2},{11,3},{12,4},{13,5},{14,6},{15,7},{0,8},{1,9},... | collective-permute-start | bytes 393224 | tf_op jit(solution)/shard_map/ppermute | solution.py:54
  72.0 2.7 %collective-permute-start.15 = (bf16[128,512]{1,0:T(8,128)(2,1)S(1)}, bf16[128,512]{1,0:T(8,128)(2,1)S(1)}, u32[]{:S(2)}, u32[]{:S(2)}) collective-permute-start(bf16[128,512]{1,0:T(8,128)(2,1)S(1)} %get-tuple-element.64), channel_id=1, source_target_pairs={{8,0},{9,1},{10,2},{11,3},{12,4},{13,5},{14,6},{15,7},{0,8},{1,9},... | collective-permute-start | bytes 393224 | tf_op jit(solution)/shard_map/ppermute | solution.py:54
  81.0 3.3 %collective-permute-start.7 = (bf16[128,512]{1,0:T(8,128)(2,1)S(1)}, bf16[128,512]{1,0:T(8,128)(2,1)S(1)}, u32[]{:S(2)}, u32[]{:S(2)}) collective-permute-start(bf16[128,512]{1,0:T(8,128)(2,1)S(1)} %get-tuple-element.50), channel_id=1, source_target_pairs={{64,8},{65,9},{66,10},{67,11},{68,12},{69,13},{70,14},{71,15},{72,... | collective-permute-start | bytes 393224 | tf_op jit(solution)/shard_map/ppermute | solution.py:87
  84.3 3.2 %collective-permute-start.17 = (bf16[128,512]{1,0:T(8,128)(2,1)S(1)}, bf16[128,512]{1,0:T(8,128)(2,1)S(1)}, u32[]{:S(2)}, u32[]{:S(2)}) collective-permute-start(bf16[128,512]{1,0:T(8,128)(2,1)S(1)} %get-tuple-element.66), channel_id=1, source_target_pairs={{64,8},{65,9},{66,10},{67,11},{68,12},{69,13},{70,14},{71,15},{72,... | collective-permute-start | bytes 393224 | tf_op jit(solution)/shard_map/ppermute | solution.py:87
  88.9 4.6 %collective-permute-start.8 = (bf16[128,512]{1,0:T(8,128)(2,1)S(1)}, bf16[128,512]{1,0:T(8,128)(2,1)S(1)}, u32[]{:S(2)}, u32[]{:S(2)}) collective-permute-start(bf16[128,512]{1,0:T(8,128)(2,1)S(1)} %get-tuple-element.53), channel_id=1, source_target_pairs={{8,0},{9,1},{10,2},{11,3},{12,4},{13,5},{14,6},{15,7},{0,8},{1,9},... | collective-permute-start | bytes 393224 | tf_op jit(solution)/shard_map/ppermute | solution.py:54
  97.4 2.4 %collective-permute-start.9 = (bf16[128,1024]{1,0:T(8,128)(2,1)S(1)}, bf16[128,1024]{1,0:T(8,128)(2,1)S(1)}, u32[]{:S(2)}, u32[]{:S(2)}) collective-permute-start(bf16[128,1024]{1,0:T(8,128)(2,1)S(1)} %get-tuple-element.54), channel_id=1, source_target_pairs={{64,0},{128,64},{192,128},{256,192},{320,256},{384,320},{448,384},... | collective-permute-start | bytes 786440 | tf_op jit(solution)/shard_map/ppermute | solution.py:77
  103.6 3.1 %collective-permute-start.10 = (bf16[128,512]{1,0:T(8,128)(2,1)S(1)}, bf16[128,512]{1,0:T(8,128)(2,1)S(1)}, u32[]{:S(2)}, u32[]{:S(2)}) collective-permute-start(bf16[128,512]{1,0:T(8,128)(2,1)S(1)} %get-tuple-element.55), channel_id=1, source_target_pairs={{64,8},{65,9},{66,10},{67,11},{68,12},{69,13},{70,14},{71,15},{72,... | collective-permute-start | bytes 393224 | tf_op jit(solution)/shard_map/ppermute | solution.py:87
  111.3 4.7 %collective-permute-start.11 = (bf16[128,512]{1,0:T(8,128)(2,1)S(1)}, bf16[128,512]{1,0:T(8,128)(2,1)S(1)}, u32[]{:S(2)}, u32[]{:S(2)}) collective-permute-start(bf16[128,512]{1,0:T(8,128)(2,1)S(1)} %get-tuple-element.58), channel_id=1, source_target_pairs={{8,0},{9,1},{10,2},{11,3},{12,4},{13,5},{14,6},{15,7},{0,8},{1,9},... | collective-permute-start | bytes 393224 | tf_op jit(solution)/shard_map/ppermute | solution.py:54
  126.2 2.6 %collective-permute-start.13 = (bf16[128,512]{1,0:T(8,128)(2,1)S(1)}, bf16[128,512]{1,0:T(8,128)(2,1)S(1)}, u32[]{:S(2)}, u32[]{:S(2)}) collective-permute-start(bf16[128,512]{1,0:T(8,128)(2,1)S(1)} %get-tuple-element.60), channel_id=1, source_target_pairs={{64,8},{65,9},{66,10},{67,11},{68,12},{69,13},{70,14},{71,15},{72,... | collective-permute-start | bytes 393224 | tf_op jit(solution)/shard_map/ppermute | solution.py:87
  128.8 2.7 %collective-permute-start.23 = (bf16[128,512]{1,0:T(8,128)(2,1)S(1)}, bf16[128,512]{1,0:T(8,128)(2,1)S(1)}, u32[]{:S(2)}, u32[]{:S(2)}) collective-permute-start(bf16[128,512]{1,0:T(8,128)(2,1)S(1)} %get-tuple-element.76), channel_id=1, source_target_pairs={{64,8},{65,9},{66,10},{67,11},{68,12},{69,13},{70,14},{71,15},{72,... | collective-permute-start | bytes 393224 | tf_op jit(solution)/shard_map/ppermute | solution.py:87
  133.8 3.0 %collective-permute-done.23.refs_11_.partner_ref = bf16[128,512]{1,0:T(8,128)(2,1)S(1)} collective-permute-done((bf16[128,512]{1,0:T(8,128)(2,1)S(1)}, bf16[128,512]{1,0:T(8,128)(2,1)S(1)}, u32[]{:S(2)}, u32[]{:S(2)}) %collective-permute-start.23) | collective-permute-done | bytes 131104 | tf_op jit(solution)/shard_map/ppermute | solution.py:87
  139.7 3.9 %collective-permute-start.25 = (bf16[256,512]{1,0:T(8,128)(2,1)S(1)}, bf16[256,512]{1,0:T(8,128)(2,1)S(1)}, u32[]{:S(2)}, u32[]{:S(2)}) collective-permute-start(bf16[256,512]{1,0:T(8,128)(2,1)S(1)} %outer_rows.6), channel_id=1, source_target_pairs={{6,0},{7,1},{4,2},{5,3},{2,4},{3,5},{0,6},{1,7},{14,8},{15,9},{12,... | collective-permute-start | bytes 786440 | tf_op jit(solution)/shard_map/ppermute | solution.py:46
  144.0 4.1 %collective-permute-start.26 = (bf16[256,512]{1,0:T(8,128)(2,1)S(1)}, bf16[256,512]{1,0:T(8,128)(2,1)S(1)}, u32[]{:S(2)}, u32[]{:S(2)}) collective-permute-start(bf16[256,512]{1,0:T(8,128)(2,1)S(1)} %outer_rows.7), channel_id=1, source_target_pairs={{4,0},{5,1},{6,2},{7,3},{0,4},{1,5},{2,6},{3,7},{12,8},{13,9},{14,... | collective-permute-start | bytes 786440 | tf_op jit(solution)/shard_map/ppermute | solution.py:46
  151.2 3.9 %collective-permute-start.27 = (bf16[128,512]{1,0:T(8,128)(2,1)S(1)}, bf16[128,512]{1,0:T(8,128)(2,1)S(1)}, u32[]{:S(2)}, u32[]{:S(2)}) collective-permute-start(bf16[128,512]{1,0:T(8,128)(2,1)S(1)} %get-tuple-element.79), channel_id=1, source_target_pairs={{8,0},{9,1},{10,2},{11,3},{12,4},{13,5},{14,6},{15,7},{0,8},{1,9},... | collective-permute-start | bytes 393224 | tf_op jit(solution)/shard_map/ppermute | solution.py:54
  164.2 2.5 %collective-permute-done.28 = bf16[128,1024]{1,0:T(8,128)(2,1)S(1)} collective-permute-done((bf16[128,1024]{1,0:T(8,128)(2,1)S(1)}, bf16[128,1024]{1,0:T(8,128)(2,1)S(1)}, u32[]{:S(2)}, u32[]{:S(2)}) %collective-permute-start.28) | collective-permute-done | bytes 262176 | tf_op jit(solution)/shard_map/ppermute | solution.py:77
  166.7 3.4 %all-to-all-start.1 = ((bf16[8,32,512]{2,1,0:T(8,128)(2,1)}), bf16[8,32,512]{2,1,0:T(8,128)(2,1)S(1)}, u32[]{:S(2)}, u32[]{:S(2)}) async-start(bf16[8,32,512]{2,1,0:T(8,128)(2,1)} %bitcast.7), calls=%async_computation.1 | async-start | bytes 524288 | tf_op jit(solution)/shard_map/all_to_all | solution.py:70
  171.9 14.1 %all-to-all-done.1 = bf16[8,32,512]{2,1,0:T(8,128)(2,1)S(1)} async-done(((bf16[8,32,512]{2,1,0:T(8,128)(2,1)}), bf16[8,32,512]{2,1,0:T(8,128)(2,1)S(1)}, u32[]{:S(2)}, u32[]{:S(2)}) %all-to-all-start.1) | async-done | bytes 262176 | tf_op jit(solution)/shard_map/all_to_all | solution.py:70
  (80 shorter events, 59.6 us)
Async XLA Ops:
  37.3 14.4 %collective-permute-start.2 = (bf16[256,1024]{1,0:T(8,128)(2,1)S(1)}, bf16[256,1024]{1,0:T(8,128)(2,1)S(1)}, u32[]{:S(2)}, u32[]{:S(2)}) collective-permute-start(bf16[256,1024]{1,0:T(8,128)(2,1)S(1)} %bitcast.12), channel_id=1, source_target_pairs={{6,0},{7,1},{4,2},{5,3},{2,4},{3,5},{0,6},{1,7},{14,8},{15,9},{12,... | collective-permute-start | bytes 1572872 | tf_op jit(solution)/shard_map/ppermute | solution.py:46
  41.9 15.0 %collective-permute-start.1 = (bf16[256,1024]{1,0:T(8,128)(2,1)S(1)}, bf16[256,1024]{1,0:T(8,128)(2,1)S(1)}, u32[]{:S(2)}, u32[]{:S(2)}) collective-permute-start(bf16[256,1024]{1,0:T(8,128)(2,1)S(1)} %bitcast.13), channel_id=1, source_target_pairs={{2,0},{3,1},{0,2},{1,3},{6,4},{7,5},{4,6},{5,7},{10,8},{11,9},{8,1... | collective-permute-start | bytes 1572872 | tf_op jit(solution)/shard_map/ppermute | solution.py:46
  44.1 17.9 %collective-permute-start = (f32[128,512]{1,0:T(8,128)S(1)}, f32[128,512]{1,0:T(8,128)S(1)}, u32[]{:S(2)}, u32[]{:S(2)}) collective-permute-start(f32[128,512]{1,0:T(8,128)S(1)} %slice.25), channel_id=1, source_target_pairs={{8,0},{9,1},{10,2},{11,3},{12,4},{13,5},{14,6},{15,7},{0,8},{1,9},... | collective-permute-start | bytes 786440 | tf_op jit(solution)/shard_map/ppermute | solution.py:54
  51.7 10.4 %collective-permute-start.3 = (bf16[128,1024]{1,0:T(8,128)(2,1)S(1)}, bf16[128,1024]{1,0:T(8,128)(2,1)S(1)}, u32[]{:S(2)}, u32[]{:S(2)}) collective-permute-start(bf16[128,1024]{1,0:T(8,128)(2,1)S(1)} %slice.26), channel_id=1, source_target_pairs={{2,0},{3,1},{0,2},{1,3},{6,4},{7,5},{4,6},{5,7},{10,8},{11,9},{8,1... | collective-permute-start | bytes 786440 | tf_op jit(solution)/shard_map/ppermute | solution.py:46
  56.9 9.5 %collective-permute-start.4 = (bf16[128,1024]{1,0:T(8,128)(2,1)S(1)}, bf16[128,1024]{1,0:T(8,128)(2,1)S(1)}, u32[]{:S(2)}, u32[]{:S(2)}) collective-permute-start(bf16[128,1024]{1,0:T(8,128)(2,1)S(1)} %slice.27), channel_id=1, source_target_pairs={{6,0},{7,1},{4,2},{5,3},{2,4},{3,5},{0,6},{1,7},{14,8},{15,9},{12,... | collective-permute-start | bytes 786440 | tf_op jit(solution)/shard_map/ppermute | solution.py:46
  58.9 12.0 %collective-permute-start.14 = (bf16[128,512]{1,0:T(8,128)(2,1)S(1)}, bf16[128,512]{1,0:T(8,128)(2,1)S(1)}, u32[]{:S(2)}, u32[]{:S(2)}) collective-permute-start(bf16[128,512]{1,0:T(8,128)(2,1)S(1)} %slice.33), channel_id=1, source_target_pairs={{8,0},{9,1},{10,2},{11,3},{12,4},{13,5},{14,6},{15,7},{0,8},{1,9},... | collective-permute-start | bytes 393224 | tf_op jit(solution)/shard_map/ppermute | solution.py:54
  67.7 7.0 %collective-permute-start.5 = (bf16[128,512]{1,0:T(8,128)(2,1)S(1)}, bf16[128,512]{1,0:T(8,128)(2,1)S(1)}, u32[]{:S(2)}, u32[]{:S(2)}) collective-permute-start(bf16[128,512]{1,0:T(8,128)(2,1)S(1)} %get-tuple-element.48), channel_id=1, source_target_pairs={{8,0},{9,1},{10,2},{11,3},{12,4},{13,5},{14,6},{15,7},{0,8},{1,9},... | collective-permute-start | bytes 393224 | tf_op jit(solution)/shard_map/ppermute | solution.py:54
  74.8 12.7 %collective-permute-start.6 = (bf16[128,1024]{1,0:T(8,128)(2,1)S(1)}, bf16[128,1024]{1,0:T(8,128)(2,1)S(1)}, u32[]{:S(2)}, u32[]{:S(2)}) collective-permute-start(bf16[128,1024]{1,0:T(8,128)(2,1)S(1)} %get-tuple-element.49), channel_id=1, source_target_pairs={{64,0},{128,64},{192,128},{256,192},{320,256},{384,320},{448,384},... | collective-permute-start | bytes 786440 | tf_op jit(solution)/shard_map/ppermute | solution.py:77
  79.1 14.5 %collective-permute-start.16 = (bf16[128,1024]{1,0:T(8,128)(2,1)S(1)}, bf16[128,1024]{1,0:T(8,128)(2,1)S(1)}, u32[]{:S(2)}, u32[]{:S(2)}) collective-permute-start(bf16[128,1024]{1,0:T(8,128)(2,1)S(1)} %get-tuple-element.65.refs_4_), channel_id=1, source_target_pairs={{64,0},{128,64},{192,128},{256,192},{320,256},{384,320},{448,384},... | collective-permute-start | bytes 786440 | tf_op jit(solution)/shard_map/ppermute | solution.py:77
  84.3 9.2 %collective-permute-start.17 = (bf16[128,512]{1,0:T(8,128)(2,1)S(1)}, bf16[128,512]{1,0:T(8,128)(2,1)S(1)}, u32[]{:S(2)}, u32[]{:S(2)}) collective-permute-start(bf16[128,512]{1,0:T(8,128)(2,1)S(1)} %get-tuple-element.66), channel_id=1, source_target_pairs={{64,8},{65,9},{66,10},{67,11},{68,12},{69,13},{70,14},{71,15},{72,... | collective-permute-start | bytes 393224 | tf_op jit(solution)/shard_map/ppermute | solution.py:87
  88.9 8.5 %collective-permute-start.8 = (bf16[128,512]{1,0:T(8,128)(2,1)S(1)}, bf16[128,512]{1,0:T(8,128)(2,1)S(1)}, u32[]{:S(2)}, u32[]{:S(2)}) collective-permute-start(bf16[128,512]{1,0:T(8,128)(2,1)S(1)} %get-tuple-element.53), channel_id=1, source_target_pairs={{8,0},{9,1},{10,2},{11,3},{12,4},{13,5},{14,6},{15,7},{0,8},{1,9},... | collective-permute-start | bytes 393224 | tf_op jit(solution)/shard_map/ppermute | solution.py:54
  97.4 12.6 %collective-permute-start.9 = (bf16[128,1024]{1,0:T(8,128)(2,1)S(1)}, bf16[128,1024]{1,0:T(8,128)(2,1)S(1)}, u32[]{:S(2)}, u32[]{:S(2)}) collective-permute-start(bf16[128,1024]{1,0:T(8,128)(2,1)S(1)} %get-tuple-element.54), channel_id=1, source_target_pairs={{64,0},{128,64},{192,128},{256,192},{320,256},{384,320},{448,384},... | collective-permute-start | bytes 786440 | tf_op jit(solution)/shard_map/ppermute | solution.py:77
  101.7 14.3 %collective-permute-start.19 = (bf16[128,1024]{1,0:T(8,128)(2,1)S(1)}, bf16[128,1024]{1,0:T(8,128)(2,1)S(1)}, u32[]{:S(2)}, u32[]{:S(2)}) collective-permute-start(bf16[128,1024]{1,0:T(8,128)(2,1)S(1)} %get-tuple-element.70.refs_6_), channel_id=1, source_target_pairs={{64,0},{128,64},{192,128},{256,192},{320,256},{384,320},{448,384},... | collective-permute-start | bytes 786440 | tf_op jit(solution)/shard_map/ppermute | solution.py:77
  106.8 9.2 %collective-permute-start.20 = (bf16[128,512]{1,0:T(8,128)(2,1)S(1)}, bf16[128,512]{1,0:T(8,128)(2,1)S(1)}, u32[]{:S(2)}, u32[]{:S(2)}) collective-permute-start(bf16[128,512]{1,0:T(8,128)(2,1)S(1)} %get-tuple-element.71), channel_id=1, source_target_pairs={{64,8},{65,9},{66,10},{67,11},{68,12},{69,13},{70,14},{71,15},{72,... | collective-permute-start | bytes 393224 | tf_op jit(solution)/shard_map/ppermute | solution.py:87
  111.3 8.7 %collective-permute-start.11 = (bf16[128,512]{1,0:T(8,128)(2,1)S(1)}, bf16[128,512]{1,0:T(8,128)(2,1)S(1)}, u32[]{:S(2)}, u32[]{:S(2)}) collective-permute-start(bf16[128,512]{1,0:T(8,128)(2,1)S(1)} %get-tuple-element.58), channel_id=1, source_target_pairs={{8,0},{9,1},{10,2},{11,3},{12,4},{13,5},{14,6},{15,7},{0,8},{1,9},... | collective-permute-start | bytes 393224 | tf_op jit(solution)/shard_map/ppermute | solution.py:54
  120.0 12.4 %collective-permute-start.12 = (bf16[128,1024]{1,0:T(8,128)(2,1)S(1)}, bf16[128,1024]{1,0:T(8,128)(2,1)S(1)}, u32[]{:S(2)}, u32[]{:S(2)}) collective-permute-start(bf16[128,1024]{1,0:T(8,128)(2,1)S(1)} %get-tuple-element.59), channel_id=1, source_target_pairs={{64,0},{128,64},{192,128},{256,192},{320,256},{384,320},{448,384},... | collective-permute-start | bytes 786440 | tf_op jit(solution)/shard_map/ppermute | solution.py:77
  124.2 12.6 %collective-permute-start.22 = (bf16[128,1024]{1,0:T(8,128)(2,1)S(1)}, bf16[128,1024]{1,0:T(8,128)(2,1)S(1)}, u32[]{:S(2)}, u32[]{:S(2)}) collective-permute-start(bf16[128,1024]{1,0:T(8,128)(2,1)S(1)} %get-tuple-element.75.refs_8_), channel_id=1, source_target_pairs={{64,0},{128,64},{192,128},{256,192},{320,256},{384,320},{448,384},... | collective-permute-start | bytes 786440 | tf_op jit(solution)/shard_map/ppermute | solution.py:77
  128.8 8.0 %collective-permute-start.23 = (bf16[128,512]{1,0:T(8,128)(2,1)S(1)}, bf16[128,512]{1,0:T(8,128)(2,1)S(1)}, u32[]{:S(2)}, u32[]{:S(2)}) collective-permute-start(bf16[128,512]{1,0:T(8,128)(2,1)S(1)} %get-tuple-element.76), channel_id=1, source_target_pairs={{64,8},{65,9},{66,10},{67,11},{68,12},{69,13},{70,14},{71,15},{72,... | collective-permute-start | bytes 393224 | tf_op jit(solution)/shard_map/ppermute | solution.py:87
  137.3 26.0 %collective-permute-start.24 = (bf16[256,512]{1,0:T(8,128)(2,1)S(1)}, bf16[256,512]{1,0:T(8,128)(2,1)S(1)}, u32[]{:S(2)}, u32[]{:S(2)}) collective-permute-start(bf16[256,512]{1,0:T(8,128)(2,1)S(1)} %outer_rows.5), channel_id=1, source_target_pairs={{2,0},{3,1},{0,2},{1,3},{6,4},{7,5},{4,6},{5,7},{10,8},{11,9},{8,1... | collective-permute-start | bytes 786440 | tf_op jit(solution)/shard_map/ppermute | solution.py:46
  139.7 23.6 %collective-permute-start.25 = (bf16[256,512]{1,0:T(8,128)(2,1)S(1)}, bf16[256,512]{1,0:T(8,128)(2,1)S(1)}, u32[]{:S(2)}, u32[]{:S(2)}) collective-permute-start(bf16[256,512]{1,0:T(8,128)(2,1)S(1)} %outer_rows.6), channel_id=1, source_target_pairs={{6,0},{7,1},{4,2},{5,3},{2,4},{3,5},{0,6},{1,7},{14,8},{15,9},{12,... | collective-permute-start | bytes 786440 | tf_op jit(solution)/shard_map/ppermute | solution.py:46
  144.0 19.3 %collective-permute-start.26 = (bf16[256,512]{1,0:T(8,128)(2,1)S(1)}, bf16[256,512]{1,0:T(8,128)(2,1)S(1)}, u32[]{:S(2)}, u32[]{:S(2)}) collective-permute-start(bf16[256,512]{1,0:T(8,128)(2,1)S(1)} %outer_rows.7), channel_id=1, source_target_pairs={{4,0},{5,1},{6,2},{7,3},{0,4},{1,5},{2,6},{3,7},{12,8},{13,9},{14,... | collective-permute-start | bytes 786440 | tf_op jit(solution)/shard_map/ppermute | solution.py:46
  149.2 7.8 %collective-permute-start.29 = (bf16[128,512]{1,0:T(8,128)(2,1)S(1)}, bf16[128,512]{1,0:T(8,128)(2,1)S(1)}, u32[]{:S(2)}, u32[]{:S(2)}) collective-permute-start(bf16[128,512]{1,0:T(8,128)(2,1)S(1)} %get-tuple-element.84), channel_id=1, source_target_pairs={{8,0},{9,1},{10,2},{11,3},{12,4},{13,5},{14,6},{15,7},{0,8},{1,9},... | collective-permute-start | bytes 393224 | tf_op jit(solution)/shard_map/ppermute | solution.py:54
  151.2 8.6 %collective-permute-start.27 = (bf16[128,512]{1,0:T(8,128)(2,1)S(1)}, bf16[128,512]{1,0:T(8,128)(2,1)S(1)}, u32[]{:S(2)}, u32[]{:S(2)}) collective-permute-start(bf16[128,512]{1,0:T(8,128)(2,1)S(1)} %get-tuple-element.79), channel_id=1, source_target_pairs={{8,0},{9,1},{10,2},{11,3},{12,4},{13,5},{14,6},{15,7},{0,8},{1,9},... | collective-permute-start | bytes 393224 | tf_op jit(solution)/shard_map/ppermute | solution.py:54
  166.7 19.3 %all-to-all-start.1 = ((bf16[8,32,512]{2,1,0:T(8,128)(2,1)}), bf16[8,32,512]{2,1,0:T(8,128)(2,1)S(1)}, u32[]{:S(2)}, u32[]{:S(2)}) async-start(bf16[8,32,512]{2,1,0:T(8,128)(2,1)} %bitcast.7), calls=%async_computation.1 | async-start | bytes 524288 | tf_op jit(solution)/shard_map/all_to_all | solution.py:70
  (11 other events, 117.1 us)

commit v6 on v5

--- a/solution.py
+++ b/solution.py
@@ -6,6 +6,7 @@
 from jax.experimental import pallas as pl
 from jax.experimental.pallas import tpu as pltpu
 from jax.sharding import PartitionSpec as P
+
 
 coupling_scale = 32.0**0.25
 rms_epsilon = 1e-06
@@ -213,7 +214,7 @@
     return pltpu.CompilerParams(vmem_limit_bytes=16 * 2**20)
 
 
-def call(kernel, name, cost_estimate, outs, operands, scratch=()):
+def call(kernel, cost_estimate, outs, operands, scratch=()):
     return pl.pallas_call(
         kernel,
         out_shape=tuple(jax.ShapeDtypeStruct(shape, dtype) for shape, dtype in outs),
@@ -222,7 +223,6 @@
         scratch_shapes=list(scratch),
         cost_estimate=cost_estimate,
         compiler_params=kernel_params(),
-        name=name,
     )(*operands)
 
 
@@ -231,7 +231,6 @@
     units = sum(w.shape[0] for w in weights)
     return call(
         forward_kernel,
-        "forward_half",
         cost(2 * tokens, units, half),
         (
             ((2 * tokens, units), jnp.bfloat16),
@@ -248,7 +247,6 @@
     units = slopes.shape[1]
     return call(
         backward_kernel,
-        "backward_half",
         cost(2 * tokens, units, half),
         (((tokens, half), jnp.float32), ((tokens, half), jnp.bfloat16)),
         (grads, partner_cotangent, slopes, *weights),
@@ -266,7 +264,6 @@
     tokens, half = kept.shape
     return call(
         acts_kernel,
-        "new_acts",
         small_cost(tokens, half),
         (((tokens, 2 * half), jnp.bfloat16), ((tokens, half), jnp.bfloat16)),
         (acts, kept, received),
@@ -277,7 +274,6 @@
     tokens, half = kept.shape
     return call(
         functools.partial(grads_kernel, scale),
-        "new_grads",
         small_cost(tokens, half),
         (((tokens, 2 * half), jnp.bfloat16), ((tokens, half), jnp.bfloat16)),
         (acts, grads, gain, kept, received),
@@ -288,7 +284,6 @@
     tokens = hiddens[0].shape[0] * len(hiddens)
     return call(
         functools.partial(outer_kernel, start, columns),
-        "outer_rows",
         pl.CostEstimate(
             flops=2 * tokens * count * half,
             bytes_accessed=2 * (tokens * count + tokens * half + count * half),
@@ -312,43 +307,47 @@
     partner_first = swapped_with_partner(acts_pair[:, :half])
     partner_cotangent = swapped_with_partner(grads_pair[:, half:].astype(jnp.bfloat16))
     hiddens, cotangents, columns = [], [], []
-    for tick_index in range(tick_count):
-        last = tick_index == tick_count - 1
+    for _ in range(tick_count - 1):
         hidden, slopes, kept, sent = forward(acts_pair, partner_first, gain, weights)
         received = swapped_with_partner(sent)
         hiddens.append(hidden)
-        if last:
-            cotangents += [grads_pair, partner_cotangent]
-            columns += [half, 0]
-            parts = [
-                outer_rows(hiddens, cotangents, columns, i * quarter, quarter, half)
-                for i in (3, 1, 2)
-            ]
-            from_far = swapped_along_x(parts[0], far_x)
-            from_near = swapped_along_x(parts[1], near_x)
-            from_next = swapped_along_x(parts[2], next_x)
-            acts_pair, grads_pair, _ = lax.optimization_barrier((acts_pair, grads_pair, parts))
         kept_grad, sent_grad = backward(grads_pair, partner_cotangent, slopes, weights)
         received_grad = swapped_with_partner(sent_grad)
         new_acts, new_first = new_acts_of(acts_pair, kept, received)
         next_acts = passed_back(new_acts)
+        next_first = passed_back_to_partner(new_first)
         new_grads, new_second = new_grads_of(
             scale, acts_pair, grads_pair, gain, kept_grad, received_grad
         )
         next_grads = passed_back(new_grads)
-        if not last:
-            cotangents += [new_grads, partner_cotangent]
-            columns += [0, 0]
-            partner_first = passed_back_to_partner(new_first)
-            partner_cotangent = passed_back_to_partner(new_second)
+        next_cotangent = passed_back_to_partner(new_second)
+        cotangents += [new_grads, partner_cotangent]
+        columns += [0, 0]
         acts_pair, grads_pair, scale = next_acts, next_grads, coupling_scale
-
-    own = outer_rows(hiddens, cotangents, columns, 0, quarter, half)
+        partner_first, partner_cotangent = next_first, next_cotangent
+
+    hidden, slopes, kept, sent = forward(acts_pair, partner_first, gain, weights)
+    hiddens.append(hidden)
+    cotangents += [grads_pair, partner_cotangent]
+    columns += [half, 0]
+    outer = functools.partial(outer_rows, hiddens, cotangents, columns, count=quarter, half=half)
+    parts = [outer(start=i * quarter) for i in (3, 1, 2)]
+    from_far = swapped_along_x(parts[0], far_x)
+    from_near = swapped_along_x(parts[1], near_x)
+    from_next = swapped_along_x(parts[2], next_x)
+    grads_pair, sent, _ = lax.optimization_barrier((grads_pair, sent, parts))
+    kept_grad, sent_grad = backward(grads_pair, partner_cotangent, slopes, weights)
+    received = swapped_with_partner(sent)
+    received_grad = swapped_with_partner(sent_grad)
+    own = outer(start=0)
     blocks = sum(x.astype(jnp.float32) for x in (own, from_near, from_next, from_far))
-    blocks, acts_pair, grads_pair = lax.optimization_barrier(
-        (blocks.astype(jnp.bfloat16), acts_pair, grads_pair)
-    )
+    blocks, received, received_grad = lax.optimization_barrier(
+        (blocks.astype(jnp.bfloat16), received, received_grad)
+    )
+    new_acts, _ = new_acts_of(acts_pair, kept, received)
+    new_grads, _ = new_grads_of(scale, acts_pair, grads_pair, gain, kept_grad, received_grad)
     parts = exchanged(blocks).reshape(-1, units, half)
+    acts_pair, grads_pair = passed_back(new_acts), passed_back(new_grads)
     share = jnp.sum(parts.astype(jnp.float32), axis=0)
 
     grads_pair = grads_pair.astype(jnp.float32)

time: 188 us -> 184 us (0.979)
  the two profiles are of different devices: /device:TPU:16 before, /device:TPU:8 now
where the time goes in v6:
time: 184 us; the launch traced here: 183 us
  starting transfers between devices  82.7 us (45%)
  waiting for transfers between devices  44.7 us (24%)
  blocking collectives  36.2 us (20%)
  Pallas kernels  14 us (8%)
  other arithmetic  4.02 us (2%)
    all_to_all x1, blocking collectives, exchanged(): lax.all_to_all(blocks, 'dp', 0, 0, axis_index_groups=alike_groups(), tile...  36.2 us
    ppermute x10, starting transfers between devices, swapped_with_partner(): lax.ppermute(block, 'dp', [(partner(i), i) for i in range(lax.axis_size('...  29.7 us
    ppermute x7, starting transfers between devices, swapped_along_x(): return lax.ppermute(block, 'dp', route)  22.2 us
    ppermute x8, starting transfers between devices, passed_back(): return lax.ppermute(block, 'section', [(i, i - 1) for i in devices if i])  15.9 us
    pallas_call x20, Pallas kernels, call(): pl.pallas_call(kernel, out_shape=tuple((jax.ShapeDtypeStruct(shape, dtype...  14 us
    ppermute x6, starting transfers between devices, passed_back_to_partner(): return lax.ppermute(block, ('section', 'dp'), route)  11.5 us
    ppermute x6, waiting for transfers between devices, passed_back_to_partner(): return lax.ppermute(block, ('section', 'dp'), route)  11.2 us
    ppermute x7, waiting for transfers between devices, swapped_along_x(): return lax.ppermute(block, 'dp', route)  10.4 us
  transfers between devices with their start and end apart: 32, of which 19 were waited for; matrix products, arithmetic and copies ran while one was open for 1% of the time, Pallas kernels for 7%

profile of v6, /device:TPU:8, one launch (start us, length us, event | category | flops | bytes accessed | tf_op | source)
XLA Modules:
  0.0 182.9 jit_solution(349611965242159713)
XLA Ops:
  1.5 36.2 %all_to_all.17 = bf16[8,32,1024]{2,1,0:T(8,128)(2,1)S(1)} all-to-all(bf16[8,32,1024]{2,1,0:T(8,128)(2,1)S(1)} %tile.2), channel_id=1, replica_groups={{0,1,16,17,32,33,48,49},{2,3,18,19,34,35,50,51},{4,5,20,21,36,37,52,53}..., dimensions={0} | all-to-all | bytes 1048576 | tf_op jit(solution)/shard_map/all_to_all | solution.py:71
  37.7 4.7 %collective-permute-start.2 = (bf16[256,1024]{1,0:T(8,128)(2,1)S(1)}, bf16[256,1024]{1,0:T(8,128)(2,1)S(1)}, u32[]{:S(2)}, u32[]{:S(2)}) collective-permute-start(bf16[256,1024]{1,0:T(8,128)(2,1)S(1)} %bitcast.12), channel_id=1, source_target_pairs={{6,0},{7,1},{4,2},{5,3},{2,4},{3,5},{0,6},{1,7},{14,8},{15,9},{12,... | collective-permute-start | bytes 1572872 | tf_op jit(solution)/shard_map/ppermute | solution.py:47
  44.6 3.9 %collective-permute-start = (f32[128,512]{1,0:T(8,128)S(1)}, f32[128,512]{1,0:T(8,128)S(1)}, u32[]{:S(2)}, u32[]{:S(2)}) collective-permute-start(f32[128,512]{1,0:T(8,128)S(1)} %slice.25), channel_id=1, source_target_pairs={{8,0},{9,1},{10,2},{11,3},{12,4},{13,5},{14,6},{15,7},{0,8},{1,9},... | collective-permute-start | bytes 786440 | tf_op jit(solution)/shard_map/ppermute | solution.py:55
  48.4 5.7 %collective-permute-done.2.refs_2_ = bf16[256,1024]{1,0:T(8,128)(2,1)S(1)} collective-permute-done((bf16[256,1024]{1,0:T(8,128)(2,1)S(1)}, bf16[256,1024]{1,0:T(8,128)(2,1)S(1)}, u32[]{:S(2)}, u32[]{:S(2)}) %collective-permute-start.2) | collective-permute-done | bytes 524320 | tf_op jit(solution)/shard_map/ppermute | solution.py:47
  57.4 3.4 %collective-permute-start.4 = (bf16[128,1024]{1,0:T(8,128)(2,1)S(1)}, bf16[128,1024]{1,0:T(8,128)(2,1)S(1)}, u32[]{:S(2)}, u32[]{:S(2)}) collective-permute-start(bf16[128,1024]{1,0:T(8,128)(2,1)S(1)} %slice.27), channel_id=1, source_target_pairs={{6,0},{7,1},{4,2},{5,3},{2,4},{3,5},{0,6},{1,7},{14,8},{15,9},{12,... | collective-permute-start | bytes 786440 | tf_op jit(solution)/shard_map/ppermute | solution.py:47
  60.8 3.1 %collective-permute-start.14 = (bf16[128,512]{1,0:T(8,128)(2,1)S(1)}, bf16[128,512]{1,0:T(8,128)(2,1)S(1)}, u32[]{:S(2)}, u32[]{:S(2)}) collective-permute-start(bf16[128,512]{1,0:T(8,128)(2,1)S(1)} %slice.33), channel_id=1, source_target_pairs={{8,0},{9,1},{10,2},{11,3},{12,4},{13,5},{14,6},{15,7},{0,8},{1,9},... | collective-permute-start | bytes 393224 | tf_op jit(solution)/shard_map/ppermute | solution.py:55
  63.9 3.1 %collective-permute-done.4.refs_4_ = bf16[128,1024]{1,0:T(8,128)(2,1)S(1)} collective-permute-done((bf16[128,1024]{1,0:T(8,128)(2,1)S(1)}, bf16[128,1024]{1,0:T(8,128)(2,1)S(1)}, u32[]{:S(2)}, u32[]{:S(2)}) %collective-permute-start.4) | collective-permute-done | bytes 262176 | tf_op jit(solution)/shard_map/ppermute | solution.py:47
  68.3 3.6 %collective-permute-start.5 = (bf16[128,512]{1,0:T(8,128)(2,1)S(1)}, bf16[128,512]{1,0:T(8,128)(2,1)S(1)}, u32[]{:S(2)}, u32[]{:S(2)}) collective-permute-start(bf16[128,512]{1,0:T(8,128)(2,1)S(1)} %get-tuple-element.47), channel_id=1, source_target_pairs={{8,0},{9,1},{10,2},{11,3},{12,4},{13,5},{14,6},{15,7},{0,8},{1,9},... | collective-permute-start | bytes 393224 | tf_op jit(solution)/shard_map/ppermute | solution.py:55
  85.9 2.4 %collective-permute-done.7.partner_ref = bf16[128,512]{1,0:T(8,128)(2,1)S(1)} collective-permute-done((bf16[128,512]{1,0:T(8,128)(2,1)S(1)}, bf16[128,512]{1,0:T(8,128)(2,1)S(1)}, u32[]{:S(2)}, u32[]{:S(2)}) %collective-permute-start.7) | collective-permute-done | bytes 131104 | tf_op jit(solution)/shard_map/ppermute | solution.py:88
  93.9 2.8 %collective-permute-start.18 = (bf16[128,512]{1,0:T(8,128)(2,1)S(1)}, bf16[128,512]{1,0:T(8,128)(2,1)S(1)}, u32[]{:S(2)}, u32[]{:S(2)}) collective-permute-start(bf16[128,512]{1,0:T(8,128)(2,1)S(1)} %get-tuple-element.70), channel_id=1, source_target_pairs={{8,0},{9,1},{10,2},{11,3},{12,4},{13,5},{14,6},{15,7},{0,8},{1,9},... | collective-permute-start | bytes 393224 | tf_op jit(solution)/shard_map/ppermute | solution.py:55
  107.6 2.4 %collective-permute-done.10.partner_ref = bf16[128,512]{1,0:T(8,128)(2,1)S(1)} collective-permute-done((bf16[128,512]{1,0:T(8,128)(2,1)S(1)}, bf16[128,512]{1,0:T(8,128)(2,1)S(1)}, u32[]{:S(2)}, u32[]{:S(2)}) %collective-permute-start.10) | collective-permute-done | bytes 131104 | tf_op jit(solution)/shard_map/ppermute | solution.py:88
  111.3 3.1 %collective-permute-start.11 = (bf16[128,512]{1,0:T(8,128)(2,1)S(1)}, bf16[128,512]{1,0:T(8,128)(2,1)S(1)}, u32[]{:S(2)}, u32[]{:S(2)}) collective-permute-start(bf16[128,512]{1,0:T(8,128)(2,1)S(1)} %get-tuple-element.55), channel_id=1, source_target_pairs={{8,0},{9,1},{10,2},{11,3},{12,4},{13,5},{14,6},{15,7},{0,8},{1,9},... | collective-permute-start | bytes 393224 | tf_op jit(solution)/shard_map/ppermute | solution.py:55
  115.8 2.9 %collective-permute-start.21 = (bf16[128,512]{1,0:T(8,128)(2,1)S(1)}, bf16[128,512]{1,0:T(8,128)(2,1)S(1)}, u32[]{:S(2)}, u32[]{:S(2)}) collective-permute-start(bf16[128,512]{1,0:T(8,128)(2,1)S(1)} %get-tuple-element.75), channel_id=1, source_target_pairs={{8,0},{9,1},{10,2},{11,3},{12,4},{13,5},{14,6},{15,7},{0,8},{1,9},... | collective-permute-start | bytes 393224 | tf_op jit(solution)/shard_map/ppermute | solution.py:55
  118.9 2.4 %collective-permute-start.12 = (bf16[128,1024]{1,0:T(8,128)(2,1)S(1)}, bf16[128,1024]{1,0:T(8,128)(2,1)S(1)}, u32[]{:S(2)}, u32[]{:S(2)}) collective-permute-start(bf16[128,1024]{1,0:T(8,128)(2,1)S(1)} %get-tuple-element.56), channel_id=1, source_target_pairs={{64,0},{128,64},{192,128},{256,192},{320,256},{384,320},{448,384},... | collective-permute-start | bytes 786440 | tf_op jit(solution)/shard_map/ppermute | solution.py:78
  121.3 2.6 %collective-permute-done.21.received_ref = bf16[128,512]{1,0:T(8,128)(2,1)S(1)} collective-permute-done((bf16[128,512]{1,0:T(8,128)(2,1)S(1)}, bf16[128,512]{1,0:T(8,128)(2,1)S(1)}, u32[]{:S(2)}, u32[]{:S(2)}) %collective-permute-start.21) | collective-permute-done | bytes 131104 | tf_op jit(solution)/shard_map/ppermute | solution.py:55
  129.9 2.4 %collective-permute-done.13.partner_ref = bf16[128,512]{1,0:T(8,128)(2,1)S(1)} collective-permute-done((bf16[128,512]{1,0:T(8,128)(2,1)S(1)}, bf16[128,512]{1,0:T(8,128)(2,1)S(1)}, u32[]{:S(2)}, u32[]{:S(2)}) %collective-permute-start.13) | collective-permute-done | bytes 131104 | tf_op jit(solution)/shard_map/ppermute | solution.py:88
  133.6 3.0 %collective-permute-done.23.refs_11_.partner_ref = bf16[128,512]{1,0:T(8,128)(2,1)S(1)} collective-permute-done((bf16[128,512]{1,0:T(8,128)(2,1)S(1)}, bf16[128,512]{1,0:T(8,128)(2,1)S(1)}, u32[]{:S(2)}, u32[]{:S(2)}) %collective-permute-start.23) | collective-permute-done | bytes 131104 | tf_op jit(solution)/shard_map/ppermute | solution.py:88
  139.6 3.8 %collective-permute-start.25 = (bf16[256,512]{1,0:T(8,128)(2,1)S(1)}, bf16[256,512]{1,0:T(8,128)(2,1)S(1)}, u32[]{:S(2)}, u32[]{:S(2)}) collective-permute-start(bf16[256,512]{1,0:T(8,128)(2,1)S(1)} %shard_map.91), channel_id=1, source_target_pairs={{6,0},{7,1},{4,2},{5,3},{2,4},{3,5},{0,6},{1,7},{14,8},{15,9},{12,... | collective-permute-start | bytes 786440 | tf_op jit(solution)/shard_map/ppermute | solution.py:47
  143.9 4.0 %collective-permute-start.26 = (bf16[256,512]{1,0:T(8,128)(2,1)S(1)}, bf16[256,512]{1,0:T(8,128)(2,1)S(1)}, u32[]{:S(2)}, u32[]{:S(2)}) collective-permute-start(bf16[256,512]{1,0:T(8,128)(2,1)S(1)} %shard_map.92), channel_id=1, source_target_pairs={{4,0},{5,1},{6,2},{7,3},{0,4},{1,5},{2,6},{3,7},{12,8},{13,9},{14,... | collective-permute-start | bytes 786440 | tf_op jit(solution)/shard_map/ppermute | solution.py:47
  149.1 3.0 %collective-permute-start.28 = (bf16[128,512]{1,0:T(8,128)(2,1)S(1)}, bf16[128,512]{1,0:T(8,128)(2,1)S(1)}, u32[]{:S(2)}, u32[]{:S(2)}) collective-permute-start(bf16[128,512]{1,0:T(8,128)(2,1)S(1)} %get-tuple-element.82), channel_id=1, source_target_pairs={{8,0},{9,1},{10,2},{11,3},{12,4},{13,5},{14,6},{15,7},{0,8},{1,9},... | collective-permute-start | bytes 393224 | tf_op jit(solution)/shard_map/ppermute | solution.py:55
  152.1 2.9 %collective-permute-start.27 = (bf16[128,512]{1,0:T(8,128)(2,1)S(1)}, bf16[128,512]{1,0:T(8,128)(2,1)S(1)}, u32[]{:S(2)}, u32[]{:S(2)}) collective-permute-start(bf16[128,512]{1,0:T(8,128)(2,1)S(1)} %get-tuple-element.79), channel_id=1, source_target_pairs={{8,0},{9,1},{10,2},{11,3},{12,4},{13,5},{14,6},{15,7},{0,8},{1,9},... | collective-permute-start | bytes 393224 | tf_op jit(solution)/shard_map/ppermute | solution.py:55
  161.7 3.4 %all-to-all-start.1 = ((bf16[8,32,512]{2,1,0:T(8,128)(2,1)}), bf16[8,32,512]{2,1,0:T(8,128)(2,1)S(1)}, u32[]{:S(2)}, u32[]{:S(2)}) async-start(bf16[8,32,512]{2,1,0:T(8,128)(2,1)} %bitcast.7), calls=%async_computation.1 | async-start | bytes 524288 | tf_op jit(solution)/shard_map/all_to_all | solution.py:71
  168.7 5.9 %collective-permute-done.29 = bf16[128,1024]{1,0:T(8,128)(2,1)S(1)} collective-permute-done((bf16[128,1024]{1,0:T(8,128)(2,1)S(1)}, bf16[128,1024]{1,0:T(8,128)(2,1)S(1)}, u32[]{:S(2)}, u32[]{:S(2)}) %collective-permute-start.29) | collective-permute-done | bytes 262176 | tf_op jit(solution)/shard_map/ppermute | solution.py:78
  175.4 6.8 %all-to-all-done.1 = bf16[8,32,512]{2,1,0:T(8,128)(2,1)S(1)} async-done(((bf16[8,32,512]{2,1,0:T(8,128)(2,1)}), bf16[8,32,512]{2,1,0:T(8,128)(2,1)S(1)}, u32[]{:S(2)}, u32[]{:S(2)}) %all-to-all-start.1) | async-done | bytes 262176 | tf_op jit(solution)/shard_map/all_to_all | solution.py:71
  (80 shorter events, 64.3 us)
Async XLA Ops:
  37.7 16.4 %collective-permute-start.2 = (bf16[256,1024]{1,0:T(8,128)(2,1)S(1)}, bf16[256,1024]{1,0:T(8,128)(2,1)S(1)}, u32[]{:S(2)}, u32[]{:S(2)}) collective-permute-start(bf16[256,1024]{1,0:T(8,128)(2,1)S(1)} %bitcast.12), channel_id=1, source_target_pairs={{6,0},{7,1},{4,2},{5,3},{2,4},{3,5},{0,6},{1,7},{14,8},{15,9},{12,... | collective-permute-start | bytes 1572872 | tf_op jit(solution)/shard_map/ppermute | solution.py:47
  42.4 15.0 %collective-permute-start.1 = (bf16[256,1024]{1,0:T(8,128)(2,1)S(1)}, bf16[256,1024]{1,0:T(8,128)(2,1)S(1)}, u32[]{:S(2)}, u32[]{:S(2)}) collective-permute-start(bf16[256,1024]{1,0:T(8,128)(2,1)S(1)} %bitcast.13), channel_id=1, source_target_pairs={{2,0},{3,1},{0,2},{1,3},{6,4},{7,5},{4,6},{5,7},{10,8},{11,9},{8,1... | collective-permute-start | bytes 1572872 | tf_op jit(solution)/shard_map/ppermute | solution.py:47
  44.6 19.3 %collective-permute-start = (f32[128,512]{1,0:T(8,128)S(1)}, f32[128,512]{1,0:T(8,128)S(1)}, u32[]{:S(2)}, u32[]{:S(2)}) collective-permute-start(f32[128,512]{1,0:T(8,128)S(1)} %slice.25), channel_id=1, source_target_pairs={{8,0},{9,1},{10,2},{11,3},{12,4},{13,5},{14,6},{15,7},{0,8},{1,9},... | collective-permute-start | bytes 786440 | tf_op jit(solution)/shard_map/ppermute | solution.py:55
  54.1 9.8 %collective-permute-start.3 = (bf16[128,1024]{1,0:T(8,128)(2,1)S(1)}, bf16[128,1024]{1,0:T(8,128)(2,1)S(1)}, u32[]{:S(2)}, u32[]{:S(2)}) collective-permute-start(bf16[128,1024]{1,0:T(8,128)(2,1)S(1)} %slice.26), channel_id=1, source_target_pairs={{2,0},{3,1},{0,2},{1,3},{6,4},{7,5},{4,6},{5,7},{10,8},{11,9},{8,1... | collective-permute-start | bytes 786440 | tf_op jit(solution)/shard_map/ppermute | solution.py:47
  57.4 9.6 %collective-permute-start.4 = (bf16[128,1024]{1,0:T(8,128)(2,1)S(1)}, bf16[128,1024]{1,0:T(8,128)(2,1)S(1)}, u32[]{:S(2)}, u32[]{:S(2)}) collective-permute-start(bf16[128,1024]{1,0:T(8,128)(2,1)S(1)} %slice.27), channel_id=1, source_target_pairs={{6,0},{7,1},{4,2},{5,3},{2,4},{3,5},{0,6},{1,7},{14,8},{15,9},{12,... | collective-permute-start | bytes 786440 | tf_op jit(solution)/shard_map/ppermute | solution.py:47
  60.8 11.1 %collective-permute-start.14 = (bf16[128,512]{1,0:T(8,128)(2,1)S(1)}, bf16[128,512]{1,0:T(8,128)(2,1)S(1)}, u32[]{:S(2)}, u32[]{:S(2)}) collective-permute-start(bf16[128,512]{1,0:T(8,128)(2,1)S(1)} %slice.33), channel_id=1, source_target_pairs={{8,0},{9,1},{10,2},{11,3},{12,4},{13,5},{14,6},{15,7},{0,8},{1,9},... | collective-permute-start | bytes 393224 | tf_op jit(solution)/shard_map/ppermute | solution.py:55
  68.3 7.9 %collective-permute-start.5 = (bf16[128,512]{1,0:T(8,128)(2,1)S(1)}, bf16[128,512]{1,0:T(8,128)(2,1)S(1)}, u32[]{:S(2)}, u32[]{:S(2)}) collective-permute-start(bf16[128,512]{1,0:T(8,128)(2,1)S(1)} %get-tuple-element.47), channel_id=1, source_target_pairs={{8,0},{9,1},{10,2},{11,3},{12,4},{13,5},{14,6},{15,7},{0,8},{1,9},... | collective-permute-start | bytes 393224 | tf_op jit(solution)/shard_map/ppermute | solution.py:55
  76.3 12.1 %collective-permute-start.6 = (bf16[128,1024]{1,0:T(8,128)(2,1)S(1)}, bf16[128,1024]{1,0:T(8,128)(2,1)S(1)}, u32[]{:S(2)}, u32[]{:S(2)}) collective-permute-start(bf16[128,1024]{1,0:T(8,128)(2,1)S(1)} %get-tuple-element.48), channel_id=1, source_target_pairs={{64,0},{128,64},{192,128},{256,192},{320,256},{384,320},{448,384},... | collective-permute-start | bytes 786440 | tf_op jit(solution)/shard_map/ppermute | solution.py:78
  80.1 12.6 %collective-permute-start.16 = (bf16[128,1024]{1,0:T(8,128)(2,1)S(1)}, bf16[128,1024]{1,0:T(8,128)(2,1)S(1)}, u32[]{:S(2)}, u32[]{:S(2)}) collective-permute-start(bf16[128,1024]{1,0:T(8,128)(2,1)S(1)} %get-tuple-element.66.refs_4_), channel_id=1, source_target_pairs={{64,0},{128,64},{192,128},{256,192},{320,256},{384,320},{448,384},... | collective-permute-start | bytes 786440 | tf_op jit(solution)/shard_map/ppermute | solution.py:78
  84.0 8.7 %collective-permute-start.17 = (bf16[128,512]{1,0:T(8,128)(2,1)S(1)}, bf16[128,512]{1,0:T(8,128)(2,1)S(1)}, u32[]{:S(2)}, u32[]{:S(2)}) collective-permute-start(bf16[128,512]{1,0:T(8,128)(2,1)S(1)} %get-tuple-element.67), channel_id=1, source_target_pairs={{64,8},{65,9},{66,10},{67,11},{68,12},{69,13},{70,14},{71,15},{72,... | collective-permute-start | bytes 393224 | tf_op jit(solution)/shard_map/ppermute | solution.py:88
  93.9 7.8 %collective-permute-start.18 = (bf16[128,512]{1,0:T(8,128)(2,1)S(1)}, bf16[128,512]{1,0:T(8,128)(2,1)S(1)}, u32[]{:S(2)}, u32[]{:S(2)}) collective-permute-start(bf16[128,512]{1,0:T(8,128)(2,1)S(1)} %get-tuple-element.70), channel_id=1, source_target_pairs={{8,0},{9,1},{10,2},{11,3},{12,4},{13,5},{14,6},{15,7},{0,8},{1,9},... | collective-permute-start | bytes 393224 | tf_op jit(solution)/shard_map/ppermute | solution.py:55
  97.5 12.6 %collective-permute-start.9 = (bf16[128,1024]{1,0:T(8,128)(2,1)S(1)}, bf16[128,1024]{1,0:T(8,128)(2,1)S(1)}, u32[]{:S(2)}, u32[]{:S(2)}) collective-permute-start(bf16[128,1024]{1,0:T(8,128)(2,1)S(1)} %get-tuple-element.52), channel_id=1, source_target_pairs={{64,0},{128,64},{192,128},{256,192},{320,256},{384,320},{448,384},... | collective-permute-start | bytes 786440 | tf_op jit(solution)/shard_map/ppermute | solution.py:78
  101.8 12.8 %collective-permute-start.19 = (bf16[128,1024]{1,0:T(8,128)(2,1)S(1)}, bf16[128,1024]{1,0:T(8,128)(2,1)S(1)}, u32[]{:S(2)}, u32[]{:S(2)}) collective-permute-start(bf16[128,1024]{1,0:T(8,128)(2,1)S(1)} %get-tuple-element.71.refs_6_), channel_id=1, source_target_pairs={{64,0},{128,64},{192,128},{256,192},{320,256},{384,320},{448,384},... | collective-permute-start | bytes 786440 | tf_op jit(solution)/shard_map/ppermute | solution.py:78
  105.6 8.9 %collective-permute-start.20 = (bf16[128,512]{1,0:T(8,128)(2,1)S(1)}, bf16[128,512]{1,0:T(8,128)(2,1)S(1)}, u32[]{:S(2)}, u32[]{:S(2)}) collective-permute-start(bf16[128,512]{1,0:T(8,128)(2,1)S(1)} %get-tuple-element.72), channel_id=1, source_target_pairs={{64,8},{65,9},{66,10},{67,11},{68,12},{69,13},{70,14},{71,15},{72,... | collective-permute-start | bytes 393224 | tf_op jit(solution)/shard_map/ppermute | solution.py:88
  115.8 8.2 %collective-permute-start.21 = (bf16[128,512]{1,0:T(8,128)(2,1)S(1)}, bf16[128,512]{1,0:T(8,128)(2,1)S(1)}, u32[]{:S(2)}, u32[]{:S(2)}) collective-permute-start(bf16[128,512]{1,0:T(8,128)(2,1)S(1)} %get-tuple-element.75), channel_id=1, source_target_pairs={{8,0},{9,1},{10,2},{11,3},{12,4},{13,5},{14,6},{15,7},{0,8},{1,9},... | collective-permute-start | bytes 393224 | tf_op jit(solution)/shard_map/ppermute | solution.py:55
  118.9 13.4 %collective-permute-start.12 = (bf16[128,1024]{1,0:T(8,128)(2,1)S(1)}, bf16[128,1024]{1,0:T(8,128)(2,1)S(1)}, u32[]{:S(2)}, u32[]{:S(2)}) collective-permute-start(bf16[128,1024]{1,0:T(8,128)(2,1)S(1)} %get-tuple-element.56), channel_id=1, source_target_pairs={{64,0},{128,64},{192,128},{256,192},{320,256},{384,320},{448,384},... | collective-permute-start | bytes 786440 | tf_op jit(solution)/shard_map/ppermute | solution.py:78
  124.1 12.6 %collective-permute-start.22 = (bf16[128,1024]{1,0:T(8,128)(2,1)S(1)}, bf16[128,1024]{1,0:T(8,128)(2,1)S(1)}, u32[]{:S(2)}, u32[]{:S(2)}) collective-permute-start(bf16[128,1024]{1,0:T(8,128)(2,1)S(1)} %get-tuple-element.76.refs_8_), channel_id=1, source_target_pairs={{64,0},{128,64},{192,128},{256,192},{320,256},{384,320},{448,384},... | collective-permute-start | bytes 786440 | tf_op jit(solution)/shard_map/ppermute | solution.py:78
  127.9 8.7 %collective-permute-start.23 = (bf16[128,512]{1,0:T(8,128)(2,1)S(1)}, bf16[128,512]{1,0:T(8,128)(2,1)S(1)}, u32[]{:S(2)}, u32[]{:S(2)}) collective-permute-start(bf16[128,512]{1,0:T(8,128)(2,1)S(1)} %get-tuple-element.77), channel_id=1, source_target_pairs={{64,8},{65,9},{66,10},{67,11},{68,12},{69,13},{70,14},{71,15},{72,... | collective-permute-start | bytes 393224 | tf_op jit(solution)/shard_map/ppermute | solution.py:88
  137.2 18.3 %collective-permute-start.24 = (bf16[256,512]{1,0:T(8,128)(2,1)S(1)}, bf16[256,512]{1,0:T(8,128)(2,1)S(1)}, u32[]{:S(2)}, u32[]{:S(2)}) collective-permute-start(bf16[256,512]{1,0:T(8,128)(2,1)S(1)} %shard_map.90), channel_id=1, source_target_pairs={{2,0},{3,1},{0,2},{1,3},{6,4},{7,5},{4,6},{5,7},{10,8},{11,9},{8,1... | collective-permute-start | bytes 786440 | tf_op jit(solution)/shard_map/ppermute | solution.py:47
  139.6 16.4 %collective-permute-start.25 = (bf16[256,512]{1,0:T(8,128)(2,1)S(1)}, bf16[256,512]{1,0:T(8,128)(2,1)S(1)}, u32[]{:S(2)}, u32[]{:S(2)}) collective-permute-start(bf16[256,512]{1,0:T(8,128)(2,1)S(1)} %shard_map.91), channel_id=1, source_target_pairs={{6,0},{7,1},{4,2},{5,3},{2,4},{3,5},{0,6},{1,7},{14,8},{15,9},{12,... | collective-permute-start | bytes 786440 | tf_op jit(solution)/shard_map/ppermute | solution.py:47
  143.9 12.1 %collective-permute-start.26 = (bf16[256,512]{1,0:T(8,128)(2,1)S(1)}, bf16[256,512]{1,0:T(8,128)(2,1)S(1)}, u32[]{:S(2)}, u32[]{:S(2)}) collective-permute-start(bf16[256,512]{1,0:T(8,128)(2,1)S(1)} %shard_map.92), channel_id=1, source_target_pairs={{4,0},{5,1},{6,2},{7,3},{0,4},{1,5},{2,6},{3,7},{12,8},{13,9},{14,... | collective-permute-start | bytes 786440 | tf_op jit(solution)/shard_map/ppermute | solution.py:47
  159.8 8.0 %collective-permute-start.30 = (bf16[128,1024]{1,0:T(8,128)(2,1)S(1)}, bf16[128,1024]{1,0:T(8,128)(2,1)S(1)}, u32[]{:S(2)}, u32[]{:S(2)}) collective-permute-start(bf16[128,1024]{1,0:T(8,128)(2,1)S(1)} %get-tuple-element.87), channel_id=1, source_target_pairs={{64,0},{128,64},{192,128},{256,192},{320,256},{384,320},{448,384},... | collective-permute-start | bytes 786440 | tf_op jit(solution)/shard_map/ppermute | solution.py:78
  161.7 20.5 %all-to-all-start.1 = ((bf16[8,32,512]{2,1,0:T(8,128)(2,1)}), bf16[8,32,512]{2,1,0:T(8,128)(2,1)S(1)}, u32[]{:S(2)}, u32[]{:S(2)}) async-start(bf16[8,32,512]{2,1,0:T(8,128)(2,1)} %bitcast.7), calls=%async_computation.1 | async-start | bytes 524288 | tf_op jit(solution)/shard_map/all_to_all | solution.py:71
  165.8 8.8 %collective-permute-start.29 = (bf16[128,1024]{1,0:T(8,128)(2,1)S(1)}, bf16[128,1024]{1,0:T(8,128)(2,1)S(1)}, u32[]{:S(2)}, u32[]{:S(2)}) collective-permute-start(bf16[128,1024]{1,0:T(8,128)(2,1)S(1)} %get-tuple-element.84), channel_id=1, source_target_pairs={{64,0},{128,64},{192,128},{256,192},{320,256},{384,320},{448,384},... | collective-permute-start | bytes 786440 | tf_op jit(solution)/shard_map/ppermute | solution.py:78
  (11 other events, 121.1 us)
